TPU v7x, 128 devices: a whole 4x4x4 slice. The times are simulated.
128 devices in a mesh: vocab: 8 (over x_lo, y), dp: 8 (over z, core), teacher: 2 (over x_hi).
Axes of the slice: x: 4 (x_hi: 2, x_lo: 2; x = x_hi * 2 + x_lo), y: 4, z: 4, core: 2. Of those that a mesh axis runs over, the one named last changes fastest.
Arguments:
- hidden_states: bfloat16 [2048, 4096], P('teacher'), may hold values from -300 to 300
- head_weight: bfloat16 [4096, 65536], P(None, ('vocab', 'dp')), may hold values from -3 to 3
- teacher_logits: bfloat16 [2048, 65536], P(None, ('vocab', 'dp', 'teacher')), may hold values from -20 to 460
- token_weight: float32 [2048], P('teacher'), may hold values from 2 to 20
Outputs:
- hidden_grad: bfloat16 [2048, 4096], P('teacher', ('vocab', 'dp'))
- weight_grad: bfloat16 [4096, 65536], P('teacher', ('vocab', 'dp'))
All inputs are finite; a program needn't handle non-finite values.
Results may differ from a plain program's by a relative error of at most 0.005.
Values may be sent and summed in bfloat16 or wider, within the bound.
No kernel may reach another device: no remote copies, remote signals or barrier semaphores. Data moves between devices by JAX's collectives and lax.ppermute only.
A program may use at most 192 MiB of HBM per device.

v0:
```python
import jax
import jax.numpy as jnp
from jax import lax
from jax.experimental.layout import Layout, with_layout_constraint
from jax.sharding import PartitionSpec as P


AXES = ("vocab", "dp", "teacher")
BF16, F32 = jnp.bfloat16, jnp.float32


def pairs(move):
    out = []
    for x in range(2):
        for y in range(4):
            for z in range(4):
                for c in range(2):
                    for h in range(2):
                        a, b, d, e, g = move(x, y, z, c, h)
                        source = ((x * 4 + y) * 8 + z * 2 + c) * 2 + h
                        target = ((a * 4 + b % 4) * 8 + d % 4 * 2 + e) * 2 + g
                        out.append((source, target))
    return out


CORE = pairs(lambda x, y, z, c, h: (x, y, z, 1 - c, h))
LOW = pairs(lambda x, y, z, c, h: (1 - x, y, z, c, h))
HIGH = pairs(lambda x, y, z, c, h: (x, y, z, c, 1 - h))
Z = {k: pairs(lambda x, y, z, c, h, k=k: (x, y, z + k, c, h)) for k in (1, 2, 3)}
Y = {k: pairs(lambda x, y, z, c, h, k=k: (x, y + k, z, c, h)) for k in (1, 2, 3)}


def send(value, moves):
    return lax.ppermute(value, AXES, moves)


def pick(value, index, axis=0):
    return lax.dynamic_index_in_dim(value, index, axis, keepdims=False)


def dot(a, b, ca, cb, out=F32):
    return lax.dot_general(a, b, (((ca,), (cb,)), ((), ())), preferred_element_type=F32).astype(out)


def merge(stats, axis):
    stats = jnp.broadcast_to(stats[None], (8,) + stats.shape)
    stats = lax.all_to_all(stats, axis, 0, 0, tiled=True)
    tops, totals = stats[:, 0], stats[:, 1]
    best = jnp.max(tops, axis=0)
    return best, jnp.sum(totals * jnp.exp(tops - best), axis=0)


def row_major(value):
    return with_layout_constraint(value, Layout(major_to_minor=(0, 1)))


def compute(hidden_states, head_weight, teacher_logits, token_weight):
    vocab, dp, high = (lax.axis_index(a) for a in AXES)
    low, y = vocab // 4, vocab % 4
    z, core = dp // 2, dp % 2

    part = row_major(lax.dynamic_slice(teacher_logits, ((1 - high) * 1024, 0), (1024, 512)))
    other_part = row_major(send(part, HIGH))
    own_part = lax.dynamic_slice(teacher_logits, (high * 1024, 0), (1024, 512))

    logits = dot(hidden_states, head_weight, 1, 0)
    student_top = jnp.max(logits, axis=1)
    student_total = jnp.sum(jnp.exp(logits - student_top[:, None]), axis=1)
    late, student_total = lax.optimization_barrier((dp, student_total))
    piece = lax.dynamic_slice(hidden_states, (late * 128, (1 - high) * 2048), (128, 2048))
    piece = send(piece, HIGH)
    other_hidden = lax.all_gather(piece, "dp", axis=0, tiled=True)
    student_top, student_total = merge(jnp.stack([student_top, student_total]), "dp")

    first = jnp.where(high == 0, own_part, other_part)
    second = jnp.where(high == 0, other_part, own_part)
    teacher = jnp.concatenate([first, second], axis=1).astype(F32)
    teacher_top = jnp.max(teacher, axis=1)
    teacher_total = jnp.sum(jnp.exp(teacher - teacher_top[:, None]), axis=1)
    teacher_top, teacher_total = merge(jnp.stack([teacher_top, teacher_total]), "dp")
    tops, totals = merge(
        jnp.stack([jnp.stack([student_top, teacher_top]), jnp.stack([student_total, teacher_total])]),
        "vocab",
    )
    student_norm, teacher_norm = tops + jnp.log(totals)

    logit_grad = (
        token_weight[:, None]
        * (jnp.exp(logits - student_norm[:, None]) - jnp.exp(teacher - teacher_norm[:, None]))
    ).astype(BF16)
    other_grad = send(logit_grad, HIGH)

    rows = head_weight.reshape(2, 4, 4, 2, 64, 1024)
    theirs = pick(rows, 1 - core, 3).reshape(2, 1024, 1024)
    mine = pick(rows, core, 3).reshape(2, 1024, 1024)

    def cross(i):
        value = dot(theirs[i], logit_grad, 1, 1, BF16)
        return send(value, CORE)

    def join(i, got):
        here = dot(mine[i], logit_grad, 1, 1)
        return (here + got.astype(F32)).astype(BF16).reshape(4, 4, 64, 1024)

    def exchange(value, axis, place, moves):
        arrived = [send(pick(value, (place + k) % 4, axis), moves[k]) for k in (1, 2, 3)]
        return pick(value, place, axis).astype(F32) + sum(a.astype(F32) for a in arrived)

    got = [cross(i) for i in range(2)]
    a, b = (join(i, got[i]) for i in range(2))
    a = exchange(a, 1, z, Z)
    b = exchange(b, 0, y, Y)
    a = exchange(a.astype(BF16), 0, y, Y)
    b = exchange(b.astype(BF16), 0, z, Z)
    arrived = send(jnp.where(low == 0, b, a).astype(BF16), LOW)
    hidden_grad = (jnp.where(low == 0, a, b) + arrived.astype(F32)).astype(BF16).T

    own_hidden = lax.dynamic_slice(hidden_states, (0, high * 2048), (1024, 2048))
    weight_grad = lax.optimization_barrier(dot(own_hidden, logit_grad, 0, 0))
    weight_grad = (weight_grad + dot(other_hidden, other_grad, 0, 0)).astype(BF16)
    return hidden_grad, weight_grad


def solution(mesh):
    return jax.shard_map(
        compute,
        mesh=mesh,
        in_specs=(
            P("teacher", None),
            P(None, ("vocab", "dp")),
            P(None, ("vocab", "dp", "teacher")),
            P("teacher"),
        ),
        out_specs=(P("teacher", ("vocab", "dp")), P("teacher", ("vocab", "dp"))),
        check_vma=False,
    )
```

profile of v0, /device:TPU:1, one launch (start us, length us, event | category | flops | bytes accessed | tf_op | source)
XLA Modules:
  0.0 186.9 jit_solution(941560264081063721)
XLA Ops:
  7.2 1.3 constant_dynamic-slice_fusion.3
  8.5 3.6 %collective-permute-start = (bf16[1024,512]{1,0:T(8,128)(2,1)S(1)}, bf16[1024,512]{1,0:T(8,128)(2,1)S(1)}, u32[]{:S(2)}, u32[]{:S(2)}) collective-permute-start(bf16[1024,512]{1,0:T(8,128)(2,1)S(1)} %constant_dynamic-slice_fusion.3), channel_id=1, source_target_pairs={{0,1},{1,0},{2,3},{3,2},{4,5},{5,4},{6,7},{7,6},{8,9},{9,8},{10,11... | collective-permute-start | bytes 3145736 | tf_op jit(solution)/shard_map/ppermute | solution.py:34
  12.1 15.1 %fusion.26 = (f32[1024]{0:T(1024)S(1)}, f32[1024,1024]{0,1:T(8,128)}) fusion(bf16[1024,4096]{1,0:T(8,128)(2,1)} %param.4, bf16[4096,1024]{1,0:T(8,128)(2,1)} %param.5), kind=kOutput, calls=%fused_computation.74 | convolution fusion | flops 8590982144 | bytes 20975616 | tf_op jit(solution)/shard_map/dot_general | solution.py:42
  27.2 2.8 %exponential_reduce_fusion = f32[1024]{0:T(1024)S(1)} fusion(f32[1024,1024]{0,1:T(8,128)} %get-tuple-element.37, f32[1024]{0:T(1024)S(1)} %get-tuple-element.36), kind=kLoop, calls=%fused_computation.13 | loop fusion | flops 2096128 | bytes 4202496 | tf_op jit(solution)/shard_map/reduce_sum | solution.py:68
  30.0 0.6 broadcast_in_dim.6
  30.7 6.3 %all-to-all-start = ((f32[8,2,1024]{2,1,0:T(2,128)}), f32[8,2,1024]{2,1,0:T(2,128)S(1)}, u32[]{:S(2)}, u32[]{:S(2)}) async-start(f32[8,2,1024]{2,1,0:T(2,128)} %broadcast_in_dim.6), calls=%async_computation | async-start | bytes 131072 | tf_op jit(solution)/shard_map/all_to_all | solution.py:47
  36.9 0.0 collective-permute-done
  36.9 2.2 %fusion.23 = (bf16[1024]{0:T(1024)(128)(2,1)S(1)}, bf16[1024,512]{1,0:T(8,128)(2,1)S(1)}, bf16[1024]{0:T(1024)(128)(2,1)S(1)}, bf16[1024,512]{1,0:T(8,128)(2,1)S(1)}) fusion(bf16[1024,512]{1,0:T(8,128)(2,1)S(1)} %collective-permute-done, bf16[2048,512]{1,0:T(8,128)(2,1)} %param.6, s32[]{:T(128)S(6)} %select_n.140, pred[]{:T(512)S(6)} %eq.24), kind=kLoop, calls=%fused_computation.71 | loop fusion | flops 2095104 | bytes 4198405 | tf_op jit(solution)/shard_map/reduce_max | solution.py:78
  39.1 0.9 fusion.1
  40.0 1.8 all-to-all-done
  41.8 0.6 broadcast_in_dim.7
  42.4 4.0 %all-to-all-start.1 = ((f32[8,2,1024]{2,1,0:T(2,128)}), f32[8,2,1024]{2,1,0:T(2,128)S(1)}, u32[]{:S(2)}, u32[]{:S(2)}) async-start(f32[8,2,1024]{2,1,0:T(2,128)} %broadcast_in_dim.7), calls=%async_computation.1 | async-start | bytes 131072 | tf_op jit(solution)/shard_map/all_to_all | solution.py:47
  46.5 1.1 dynamic_slice.91
  47.5 1.9 %collective-permute-start.16 = (bf16[128,2048]{1,0:T(8,128)(2,1)S(1)}, bf16[128,2048]{1,0:T(8,128)(2,1)S(1)}, u32[]{:S(2)}, u32[]{:S(2)}) collective-permute-start(bf16[128,2048]{1,0:T(8,128)(2,1)S(1)} %dynamic_slice.91), channel_id=1, source_target_pairs={{0,1},{1,0},{2,3},{3,2},{4,5},{5,4},{6,7},{7,6},{8,9},{9,8},{10,11... | collective-permute-start | bytes 1572872 | tf_op jit(solution)/shard_map/ppermute | solution.py:34
  49.4 1.9 %all-to-all-done.1 = f32[8,2,1024]{2,1,0:T(2,128)S(1)} async-done(((f32[8,2,1024]{2,1,0:T(2,128)}), f32[8,2,1024]{2,1,0:T(2,128)S(1)}, u32[]{:S(2)}, u32[]{:S(2)}) %all-to-all-start.1) | async-done | bytes 65568 | tf_op jit(solution)/shard_map/all_to_all | solution.py:47
  51.3 0.1 slice_reduce_fusion
  51.6 0.7 broadcast_in_dim.8
  52.3 4.2 %all-to-all-start.2 = ((f32[8,2,2,1024]{3,2,1,0:T(2,128)}), f32[8,2,2,1024]{3,2,1,0:T(2,128)S(1)}, u32[]{:S(2)}, u32[]{:S(2)}) async-start(f32[8,2,2,1024]{3,2,1,0:T(2,128)} %broadcast_in_dim.8), calls=%async_computation.2 | async-start | bytes 262144 | tf_op jit(solution)/shard_map/all_to_all | solution.py:47
  56.5 0.2 all-gather.2.cloned.1.call-start
  56.7 7.5 %constant_dynamic-slice_fusion.2 = (bf16[1,4,4,1,64,1024]{5,4,3,2,1,0:T(8,128)(2,1)}, bf16[1,4,4,1,64,1024]{5,4,3,2,1,0:T(8,128)(2,1)}, bf16[1,4,4,1,64,1024]{5,...) fusion(bf16[2,4,4,2,64,1024]{5,4,3,2,1,0:T(8,128)(2,1)} %bitcast.121, s32[]{:T(128)S(6)} %add.212, s32[]{:T(128)S(6)} %select_n.144, ...), kind=kLoop, calls=%fused_computation.65 | loop fusion | bytes 16777228 | tf_op jit(solution)/shard_map/slice | solution.py:98
  64.2 5.4 %copy.18 = f32[1024,1024]{1,0:T(8,128)} copy(f32[1024,1024]{0,1:T(8,128)} %get-tuple-element.37) | data formatting | bytes 8388608 | tf_op jit(solution)/shard_map/dot_general | solution.py:42
  69.6 0.8 copy-done.8
  70.4 0.0 all-gather.2.cloned.1.call-update
  70.5 0.1 fusion.12
  70.6 3.5 %fusion.5 = bf16[1024,1024]{1,0:T(8,128)(2,1)S(1)} fusion(f32[1024,1024]{1,0:T(8,128)} %copy.18, f32[1024]{0:T(1024)S(1)} %bitcast.134, f32[1024]{0:T(1024)S(1)} %bitcast.133, f32[1024]{0:T(1024)S(1)} %copy-done.10, bf16[1024,512]{1,0:T(8,128)(2,1)S(1)} %get-tuple-element.7, bf16[1024,512]{1,0:T(8,128)(2,1)S(1)} %get-tuple-element.15), kind=kLoop, calls=%fused_computation.8 | loop fusion | flops 9437184 | bytes 8400896 | tf_op jit(solution)/shard_map/convert_element_type | solution.py:90
  74.1 3.7 %convolution_convert_fusion.1 = bf16[1024,1024]{1,0:T(8,128)(2,1)} fusion(bf16[1024,1024]{1,0:T(8,128)(2,1)S(1)} %bitcast.125, bf16[1024,1024]{1,0:T(8,128)(2,1)S(1)} %fusion.5), kind=kOutput, calls=%fused_computation.16 | convolution fusion | flops 2148532224 | bytes 6291456 | tf_op jit(solution)/shard_map/dot_general | solution.py:42
  77.8 1.1 collective-permute-start.1
  78.9 3.7 %convolution_convert_fusion = bf16[1024,1024]{1,0:T(8,128)(2,1)} fusion(bf16[1024,1024]{1,0:T(8,128)(2,1)S(1)} %bitcast.124, bf16[1024,1024]{1,0:T(8,128)(2,1)S(1)} %fusion.5), kind=kOutput, calls=%fused_computation.15 | convolution fusion | flops 2148532224 | bytes 6291456 | tf_op jit(solution)/shard_map/dot_general | solution.py:42
  82.6 0.0 collective-permute-start.8
  82.6 1.2 collective-permute-done.1
  83.7 4.7 %add_convert_fusion.2 = bf16[1024,1024]{1,0:T(8,128)(2,1)S(1)} fusion(bf16[1024,1024]{1,0:T(8,128)(2,1)} %collective-permute-done.1, bf16[1024,1024]{1,0:T(8,128)(2,1)S(1)} %bitcast.123, bf16[1024,1024]{1,0:T(8,128)(2,1)} %copy-done), kind=kOutput, calls=%fused_computation.12 | convolution fusion | flops 2150629376 | bytes 8388608 | tf_op jit(solution)/shard_map/dot_general | solution.py:42
  88.5 0.0 copy-start.7
  88.5 1.0 dynamic-slice_bitcast_fusion.5
  89.5 0.2 collective-permute-start.2
  89.7 2.5 %collective-permute-start.4 = (bf16[4,64,1024]{2,1,0:T(8,128)(2,1)}, bf16[4,64,1024]{2,1,0:T(8,128)(2,1)}, u32[]{:S(2)}, u32[]{:S(2)}) collective-permute-start(bf16[4,64,1024]{2,1,0:T(8,128)(2,1)} %get-tuple-element.20), channel_id=1, source_target_pairs={{0,12},{1,13},{2,14},{3,15},{4,0},{5,1},{6,2},{7,3},{8,4},{9,5},{1... | collective-permute-start | bytes 1572872 | tf_op jit(solution)/shard_map/ppermute | solution.py:34
  92.2 0.0 collective-permute-start.3
  92.2 4.0 %add_convert_fusion.1 = bf16[1024,1024]{1,0:T(8,128)(2,1)S(1)} fusion(bf16[1024,1024]{1,0:T(8,128)(2,1)} %collective-permute-done.8, bf16[1024,1024]{1,0:T(8,128)(2,1)S(1)} %bitcast.122, bf16[1024,1024]{1,0:T(8,128)(2,1)S(1)} %copy-done.1), kind=kOutput, calls=%fused_computation.11 | convolution fusion | flops 2150629376 | bytes 8388608 | tf_op jit(solution)/shard_map/dot_general | solution.py:42
  96.2 1.3 copy-done.6
  97.6 1.2 dynamic-slice_bitcast_fusion.2
  98.7 1.5 collective-permute-start.9
  100.3 1.2 collective-permute-start.11
  101.5 10.8 %collective-permute-done.2 = bf16[4,64,1024]{2,1,0:T(8,128)(2,1)S(1)} collective-permute-done((bf16[4,64,1024]{2,1,0:T(8,128)(2,1)S(1)}, bf16[4,64,1024]{2,1,0:T(8,128)(2,1)S(1)}, u32[]{:S(2)}, u32[]{:S(2)}) %collective-permute-start.2) | collective-permute-done | bytes 524320 | tf_op jit(solution)/shard_map/ppermute | solution.py:34
  112.2 0.8 copy-done.9
  113.0 2.6 %collective-permute-start.10 = (bf16[4,64,1024]{2,1,0:T(8,128)(2,1)S(1)}, bf16[4,64,1024]{2,1,0:T(8,128)(2,1)}, u32[]{:S(2)}, u32[]{:S(2)}) collective-permute-start(bf16[4,64,1024]{2,1,0:T(8,128)(2,1)S(1)} %get-tuple-element.18), channel_id=1, source_target_pairs={{0,32},{1,33},{2,34},{3,35},{4,36},{5,37},{6,38},{7,39},{8,40},{9,... | collective-permute-start | bytes 1572872 | tf_op jit(solution)/shard_map/ppermute | solution.py:34
  115.7 2.7 %collective-permute-start.17 = (bf16[1024,1024]{1,0:T(8,128)(2,1)S(1)}, bf16[1024,1024]{1,0:T(8,128)(2,1)}, u32[]{:S(2)}, u32[]{:S(2)}) collective-permute-start(bf16[1024,1024]{1,0:T(8,128)(2,1)S(1)} %copy-done.1), channel_id=1, source_target_pairs={{0,1},{1,0},{2,3},{3,2},{4,5},{5,4},{6,7},{7,6},{8,9},{9,8},{10,11... | collective-permute-start | bytes 6291464 | tf_op jit(solution)/shard_map/ppermute | solution.py:34
  118.4 5.3 %collective-permute-done.3 = bf16[4,64,1024]{2,1,0:T(8,128)(2,1)} collective-permute-done((bf16[4,64,1024]{2,1,0:T(8,128)(2,1)S(1)}, bf16[4,64,1024]{2,1,0:T(8,128)(2,1)}, u32[]{:S(2)}, u32[]{:S(2)}) %collective-permute-start.3) | collective-permute-done | bytes 524320 | tf_op jit(solution)/shard_map/ppermute | solution.py:34
  123.7 1.9 %fusion.9 = bf16[4,64,1024]{2,1,0:T(8,128)(2,1)S(1)} fusion(bf16[4,64,1024]{2,1,0:T(8,128)(2,1)} %collective-permute-done.4, bf16[4,64,1024]{2,1,0:T(8,128)(2,1)} %collective-permute-done.3, bf16[4,64,1024]{2,1,0:T(8,128)(2,1)} %copy-done.9, bf16[4,4,64,1024]{3,2,1,0:T(8,128)(2,1)} %bitcast.129, s32[]{:T(128)S(6)} %select_n.146), kind=kLoop, calls=%fused_computation.20 | loop fusion | flops 2097152 | bytes 2621444 | tf_op jit(solution)/shard_map/convert_element_type | solution.py:113
  125.6 0.7 dynamic-slice_bitcast_fusion.11
  126.3 1.2 collective-permute-start.5
  127.5 1.5 collective-permute-start.7
  129.0 1.5 collective-permute-start.6
  130.5 1.9 %fusion.8 = bf16[4,64,1024]{2,1,0:T(8,128)(2,1)S(1)} fusion(bf16[4,64,1024]{2,1,0:T(8,128)(2,1)} %collective-permute-done.11, bf16[4,64,1024]{2,1,0:T(8,128)(2,1)} %collective-permute-done.10, bf16[4,64,1024]{2,1,0:T(8,128)(2,1)} %collective-permute-done.9, bf16[4,4,64,1024]{3,2,1,0:T(8,128)(2,1)} %bitcast.127, s32[]{:T(128)S(6)} %select_n.154), kind=kLoop, calls=%fused_computation.18 | loop fusion | flops 2097152 | bytes 2621444 | tf_op jit(solution)/shard_map/convert_element_type | solution.py:114
  132.4 0.8 dynamic-slice_bitcast_fusion.8
  133.1 0.7 collective-permute-start.12
  133.8 2.0 %collective-permute-start.14 = (bf16[64,1024]{1,0:T(8,128)(2,1)}, bf16[64,1024]{1,0:T(8,128)(2,1)}, u32[]{:S(2)}, u32[]{:S(2)}) collective-permute-start(bf16[64,1024]{1,0:T(8,128)(2,1)} %get-tuple-element.23), channel_id=1, source_target_pairs={{0,12},{1,13},{2,14},{3,15},{4,0},{5,1},{6,2},{7,3},{8,4},{9,5},{1... | collective-permute-start | bytes 393224 | tf_op jit(solution)/shard_map/ppermute | solution.py:34
  135.8 2.9 %collective-permute-done.12 = bf16[64,1024]{1,0:T(8,128)(2,1)} collective-permute-done((bf16[64,1024]{1,0:T(8,128)(2,1)}, bf16[64,1024]{1,0:T(8,128)(2,1)}, u32[]{:S(2)}, u32[]{:S(2)}) %collective-permute-start.12) | collective-permute-done | bytes 131104 | tf_op jit(solution)/shard_map/ppermute | solution.py:34
  138.8 0.9 collective-permute-done.14
  139.7 2.1 %collective-permute-done.13 = bf16[64,1024]{1,0:T(8,128)(2,1)} collective-permute-done((bf16[64,1024]{1,0:T(8,128)(2,1)}, bf16[64,1024]{1,0:T(8,128)(2,1)}, u32[]{:S(2)}, u32[]{:S(2)}) %collective-permute-start.13) | collective-permute-done | bytes 131104 | tf_op jit(solution)/shard_map/ppermute | solution.py:34
  141.8 1.2 select_convert_fusion
  143.0 1.3 collective-permute-start.15
  144.3 9.0 %fusion.6 = f32[2048,1024]{1,0:T(8,128)} fusion(bf16[1024,1024]{1,0:T(8,128)(2,1)S(1)} %copy-done.1, bf16[1024,4096]{1,0:T(8,128)(2,1)} %param.4, s32[]{:T(128)S(6)} %select_n.163), kind=kOutput, calls=%fused_computation.9 | convolution fusion | flops 4294967296 | bytes 14680068 | tf_op jit(solution)/shard_map/dot_general | solution.py:42
  153.3 13.0 %collective-permute-done.15 = bf16[64,1024]{1,0:T(8,128)(2,1)S(1)} collective-permute-done((bf16[64,1024]{1,0:T(8,128)(2,1)S(1)}, bf16[64,1024]{1,0:T(8,128)(2,1)S(1)}, u32[]{:S(2)}, u32[]{:S(2)}) %collective-permute-start.15) | collective-permute-done | bytes 131104 | tf_op jit(solution)/shard_map/ppermute | solution.py:34
  166.3 1.9 %fusion.10 = bf16[1024,64]{0,1:T(8,128)(2,1)} fusion(bf16[64,1024]{1,0:T(8,128)(2,1)S(1)} %collective-permute-done.15, pred[]{:T(512)S(6)} %eq.23, bf16[64,1024]{1,0:T(8,128)(2,1)S(1)} %collective-permute-done.7, bf16[64,1024]{1,0:T(8,128)(2,1)S(1)} %collective-permute-done.6, bf16[64,1024]{1,0:T(8,128)(2,1)S(1)} %collective-permute-done.5, ...), kind=kLoop, calls=%fused_computation.33 | loop fusion | flops 1179648 | bytes 1310729 | tf_op jit(solution)/shard_map/transpose | solution.py:116
  168.2 11.8 %add_convert_fusion = bf16[2048,1024]{1,0:T(8,128)(2,1)} fusion(f32[2048,1024]{1,0:T(8,128)} %fusion.6, bf16[1024,2048]{1,0:T(8,128)(2,1)} %all-gather.2.cloned.1.call-done, bf16[1024,1024]{1,0:T(8,128)(2,1)} %collective-permute-done.17), kind=kOutput, calls=%fused_computation | convolution fusion | flops 4299161600 | bytes 18874368 | tf_op jit(solution)/shard_map/dot_general | solution.py:42
  (42 shorter events, 0.3 us)
Async XLA Ops:
  8.5 28.5 %collective-permute-start = (bf16[1024,512]{1,0:T(8,128)(2,1)S(1)}, bf16[1024,512]{1,0:T(8,128)(2,1)S(1)}, u32[]{:S(2)}, u32[]{:S(2)}) collective-permute-start(bf16[1024,512]{1,0:T(8,128)(2,1)S(1)} %constant_dynamic-slice_fusion.3), channel_id=1, source_target_pairs={{0,1},{1,0},{2,3},{3,2},{4,5},{5,4},{6,7},{7,6},{8,9},{9,8},{10,11... | collective-permute-start | bytes 3145736 | tf_op jit(solution)/shard_map/ppermute | solution.py:34
  30.7 11.1 %all-to-all-start = ((f32[8,2,1024]{2,1,0:T(2,128)}), f32[8,2,1024]{2,1,0:T(2,128)S(1)}, u32[]{:S(2)}, u32[]{:S(2)}) async-start(f32[8,2,1024]{2,1,0:T(2,128)} %broadcast_in_dim.6), calls=%async_computation | async-start | bytes 131072 | tf_op jit(solution)/shard_map/all_to_all | solution.py:47
  42.4 8.9 %all-to-all-start.1 = ((f32[8,2,1024]{2,1,0:T(2,128)}), f32[8,2,1024]{2,1,0:T(2,128)S(1)}, u32[]{:S(2)}, u32[]{:S(2)}) async-start(f32[8,2,1024]{2,1,0:T(2,128)} %broadcast_in_dim.7), calls=%async_computation.1 | async-start | bytes 131072 | tf_op jit(solution)/shard_map/all_to_all | solution.py:47
  47.5 22.1 %collective-permute-start.16 = (bf16[128,2048]{1,0:T(8,128)(2,1)S(1)}, bf16[128,2048]{1,0:T(8,128)(2,1)S(1)}, u32[]{:S(2)}, u32[]{:S(2)}) collective-permute-start(bf16[128,2048]{1,0:T(8,128)(2,1)S(1)} %dynamic_slice.91), channel_id=1, source_target_pairs={{0,1},{1,0},{2,3},{3,2},{4,5},{5,4},{6,7},{7,6},{8,9},{9,8},{10,11... | collective-permute-start | bytes 1572872 | tf_op jit(solution)/shard_map/ppermute | solution.py:34
  52.3 18.2 %all-to-all-start.2 = ((f32[8,2,2,1024]{3,2,1,0:T(2,128)}), f32[8,2,2,1024]{3,2,1,0:T(2,128)S(1)}, u32[]{:S(2)}, u32[]{:S(2)}) async-start(f32[8,2,2,1024]{3,2,1,0:T(2,128)} %broadcast_in_dim.8), calls=%async_computation.2 | async-start | bytes 262144 | tf_op jit(solution)/shard_map/all_to_all | solution.py:47
  56.5 111.7 %all-gather.2.cloned.1.call-start = ((), (), s32[]{:S(2)}) async-start(), calls=%async_computation.3 | async-start | bytes 4718592 | tf_op jit(solution)/shard_map/all_gather | solution.py:72
  64.2 6.4 %copy-start.10 = (f32[1024]{0:T(1024)S(1)}, f32[1024]{0:T(1024)}, u32[]{:S(2)}) copy-start(f32[1024]{0:T(1024)} %param.7) | copy-start | bytes 12292
  69.6 0.8 copy-start.8
  70.6 3.5 %copy-start.5 = (bf16[1,4,4,1,64,1024]{5,4,3,2,1,0:T(8,128)(2,1)S(1)}, bf16[1,4,4,1,64,1024]{5,4,3,2,1,0:T(8,128)(2,1)}, u32[]{:S(2)}) copy-start(bf16[1,4,4,1,64,1024]{5,4,3,2,1,0:T(8,128)(2,1)} %get-tuple-element.11) | copy-start | bytes 6291460
  74.1 4.8 %copy-start = (bf16[1024,1024]{1,0:T(8,128)(2,1)}, bf16[1024,1024]{1,0:T(8,128)(2,1)S(1)}, u32[]{:S(2)}) copy-start(bf16[1024,1024]{1,0:T(8,128)(2,1)S(1)} %fusion.5) | copy-start | bytes 6291460
  74.1 4.8 %copy-start.4 = (bf16[1,4,4,1,64,1024]{5,4,3,2,1,0:T(8,128)(2,1)S(1)}, bf16[1,4,4,1,64,1024]{5,4,3,2,1,0:T(8,128)(2,1)}, u32[]{:S(2)}) copy-start(bf16[1,4,4,1,64,1024]{5,4,3,2,1,0:T(8,128)(2,1)} %get-tuple-element.10) | copy-start | bytes 6291460
  77.8 5.9 %collective-permute-start.1 = (bf16[1024,1024]{1,0:T(8,128)(2,1)}, bf16[1024,1024]{1,0:T(8,128)(2,1)}, u32[]{:S(2)}, u32[]{:S(2)}) collective-permute-start(bf16[1024,1024]{1,0:T(8,128)(2,1)} %convolution_convert_fusion.1), channel_id=1, source_target_pairs={{0,2},{1,3},{2,0},{3,1},{4,6},{5,7},{6,4},{7,5},{8,10},{9,11},{10,... | collective-permute-start | bytes 6291464 | tf_op jit(solution)/shard_map/ppermute | solution.py:34
  78.9 4.9 %copy-start.3 = (bf16[1,4,4,1,64,1024]{5,4,3,2,1,0:T(8,128)(2,1)S(1)}, bf16[1,4,4,1,64,1024]{5,4,3,2,1,0:T(8,128)(2,1)}, u32[]{:S(2)}) copy-start(bf16[1,4,4,1,64,1024]{5,4,3,2,1,0:T(8,128)(2,1)} %get-tuple-element.12) | copy-start | bytes 6291460
  82.6 9.6 %collective-permute-start.8 = (bf16[1024,1024]{1,0:T(8,128)(2,1)}, bf16[1024,1024]{1,0:T(8,128)(2,1)}, u32[]{:S(2)}, u32[]{:S(2)}) collective-permute-start(bf16[1024,1024]{1,0:T(8,128)(2,1)} %convolution_convert_fusion), channel_id=1, source_target_pairs={{0,2},{1,3},{2,0},{3,1},{4,6},{5,7},{6,4},{7,5},{8,10},{9,11},{10,... | collective-permute-start | bytes 6291464 | tf_op jit(solution)/shard_map/ppermute | solution.py:34
  83.7 8.4 %copy-start.2 = (bf16[1,4,4,1,64,1024]{5,4,3,2,1,0:T(8,128)(2,1)S(1)}, bf16[1,4,4,1,64,1024]{5,4,3,2,1,0:T(8,128)(2,1)}, u32[]{:S(2)}) copy-start(bf16[1,4,4,1,64,1024]{5,4,3,2,1,0:T(8,128)(2,1)} %get-tuple-element.13) | copy-start | bytes 6291460
  88.5 3.7 %copy-start.7 = (bf16[1024,1024]{1,0:T(8,128)(2,1)}, bf16[1024,1024]{1,0:T(8,128)(2,1)S(1)}, u32[]{:S(2)}) copy-start(bf16[1024,1024]{1,0:T(8,128)(2,1)S(1)} %add_convert_fusion.2) | copy-start | bytes 6291460
  88.5 3.7 %copy-start.1 = (bf16[1024,1024]{1,0:T(8,128)(2,1)S(1)}, bf16[1024,1024]{1,0:T(8,128)(2,1)}, u32[]{:S(2)}) copy-start(bf16[1024,1024]{1,0:T(8,128)(2,1)} %copy-done) | copy-start | bytes 6291460
  89.5 22.7 %collective-permute-start.2 = (bf16[4,64,1024]{2,1,0:T(8,128)(2,1)S(1)}, bf16[4,64,1024]{2,1,0:T(8,128)(2,1)S(1)}, u32[]{:S(2)}, u32[]{:S(2)}) collective-permute-start(bf16[4,64,1024]{2,1,0:T(8,128)(2,1)S(1)} %get-tuple-element.19), channel_id=1, source_target_pairs={{0,4},{1,5},{2,6},{3,7},{4,8},{5,9},{6,10},{7,11},{8,12},{9,13},{1... | collective-permute-start | bytes 1572872 | tf_op jit(solution)/shard_map/ppermute | solution.py:34
  89.7 26.0 %collective-permute-start.4 = (bf16[4,64,1024]{2,1,0:T(8,128)(2,1)}, bf16[4,64,1024]{2,1,0:T(8,128)(2,1)}, u32[]{:S(2)}, u32[]{:S(2)}) collective-permute-start(bf16[4,64,1024]{2,1,0:T(8,128)(2,1)} %get-tuple-element.20), channel_id=1, source_target_pairs={{0,12},{1,13},{2,14},{3,15},{4,0},{5,1},{6,2},{7,3},{8,4},{9,5},{1... | collective-permute-start | bytes 1572872 | tf_op jit(solution)/shard_map/ppermute | solution.py:34
  92.2 31.5 %collective-permute-start.3 = (bf16[4,64,1024]{2,1,0:T(8,128)(2,1)S(1)}, bf16[4,64,1024]{2,1,0:T(8,128)(2,1)}, u32[]{:S(2)}, u32[]{:S(2)}) collective-permute-start(bf16[4,64,1024]{2,1,0:T(8,128)(2,1)S(1)} %get-tuple-element.21), channel_id=1, source_target_pairs={{0,8},{1,9},{2,10},{3,11},{4,12},{5,13},{6,14},{7,15},{8,0},{9,1},... | collective-permute-start | bytes 1572872 | tf_op jit(solution)/shard_map/ppermute | solution.py:34
  96.2 1.3 copy-start.6
  98.7 28.7 %collective-permute-start.9 = (bf16[4,64,1024]{2,1,0:T(8,128)(2,1)}, bf16[4,64,1024]{2,1,0:T(8,128)(2,1)}, u32[]{:S(2)}, u32[]{:S(2)}) collective-permute-start(bf16[4,64,1024]{2,1,0:T(8,128)(2,1)} %get-tuple-element.16), channel_id=1, source_target_pairs={{0,16},{1,17},{2,18},{3,19},{4,20},{5,21},{6,22},{7,23},{8,24},{9,... | collective-permute-start | bytes 1572872 | tf_op jit(solution)/shard_map/ppermute | solution.py:34
  100.3 28.7 %collective-permute-start.11 = (bf16[4,64,1024]{2,1,0:T(8,128)(2,1)}, bf16[4,64,1024]{2,1,0:T(8,128)(2,1)}, u32[]{:S(2)}, u32[]{:S(2)}) collective-permute-start(bf16[4,64,1024]{2,1,0:T(8,128)(2,1)} %get-tuple-element.17), channel_id=1, source_target_pairs={{0,48},{1,49},{2,50},{3,51},{4,52},{5,53},{6,54},{7,55},{8,56},{9,... | collective-permute-start | bytes 1572872 | tf_op jit(solution)/shard_map/ppermute | solution.py:34
  112.2 0.8 copy-start.9
  113.0 17.5 %collective-permute-start.10 = (bf16[4,64,1024]{2,1,0:T(8,128)(2,1)S(1)}, bf16[4,64,1024]{2,1,0:T(8,128)(2,1)}, u32[]{:S(2)}, u32[]{:S(2)}) collective-permute-start(bf16[4,64,1024]{2,1,0:T(8,128)(2,1)S(1)} %get-tuple-element.18), channel_id=1, source_target_pairs={{0,32},{1,33},{2,34},{3,35},{4,36},{5,37},{6,38},{7,39},{8,40},{9,... | collective-permute-start | bytes 1572872 | tf_op jit(solution)/shard_map/ppermute | solution.py:34
  115.7 52.5 %collective-permute-start.17 = (bf16[1024,1024]{1,0:T(8,128)(2,1)S(1)}, bf16[1024,1024]{1,0:T(8,128)(2,1)}, u32[]{:S(2)}, u32[]{:S(2)}) collective-permute-start(bf16[1024,1024]{1,0:T(8,128)(2,1)S(1)} %copy-done.1), channel_id=1, source_target_pairs={{0,1},{1,0},{2,3},{3,2},{4,5},{5,4},{6,7},{7,6},{8,9},{9,8},{10,11... | collective-permute-start | bytes 6291464 | tf_op jit(solution)/shard_map/ppermute | solution.py:34
  126.3 7.5 %collective-permute-start.5 = (bf16[64,1024]{1,0:T(8,128)(2,1)S(1)}, bf16[64,1024]{1,0:T(8,128)(2,1)S(1)}, u32[]{:S(2)}, u32[]{:S(2)}) collective-permute-start(bf16[64,1024]{1,0:T(8,128)(2,1)S(1)} %get-tuple-element.25), channel_id=1, source_target_pairs={{0,16},{1,17},{2,18},{3,19},{4,20},{5,21},{6,22},{7,23},{8,24},{9,... | collective-permute-start | bytes 393224 | tf_op jit(solution)/shard_map/ppermute | solution.py:34
  127.5 8.3 %collective-permute-start.7 = (bf16[64,1024]{1,0:T(8,128)(2,1)S(1)}, bf16[64,1024]{1,0:T(8,128)(2,1)S(1)}, u32[]{:S(2)}, u32[]{:S(2)}) collective-permute-start(bf16[64,1024]{1,0:T(8,128)(2,1)S(1)} %get-tuple-element.26), channel_id=1, source_target_pairs={{0,48},{1,49},{2,50},{3,51},{4,52},{5,53},{6,54},{7,55},{8,56},{9,... | collective-permute-start | bytes 393224 | tf_op jit(solution)/shard_map/ppermute | solution.py:34
  129.0 6.9 %collective-permute-start.6 = (bf16[64,1024]{1,0:T(8,128)(2,1)}, bf16[64,1024]{1,0:T(8,128)(2,1)S(1)}, u32[]{:S(2)}, u32[]{:S(2)}) collective-permute-start(bf16[64,1024]{1,0:T(8,128)(2,1)} %get-tuple-element.27), channel_id=1, source_target_pairs={{0,32},{1,33},{2,34},{3,35},{4,36},{5,37},{6,38},{7,39},{8,40},{9,... | collective-permute-start | bytes 393224 | tf_op jit(solution)/shard_map/ppermute | solution.py:34
  133.1 5.6 %collective-permute-start.12 = (bf16[64,1024]{1,0:T(8,128)(2,1)}, bf16[64,1024]{1,0:T(8,128)(2,1)}, u32[]{:S(2)}, u32[]{:S(2)}) collective-permute-start(bf16[64,1024]{1,0:T(8,128)(2,1)} %get-tuple-element.22), channel_id=1, source_target_pairs={{0,4},{1,5},{2,6},{3,7},{4,8},{5,9},{6,10},{7,11},{8,12},{9,13},{1... | collective-permute-start | bytes 393224 | tf_op jit(solution)/shard_map/ppermute | solution.py:34
  133.8 5.9 %collective-permute-start.14 = (bf16[64,1024]{1,0:T(8,128)(2,1)}, bf16[64,1024]{1,0:T(8,128)(2,1)}, u32[]{:S(2)}, u32[]{:S(2)}) collective-permute-start(bf16[64,1024]{1,0:T(8,128)(2,1)} %get-tuple-element.23), channel_id=1, source_target_pairs={{0,12},{1,13},{2,14},{3,15},{4,0},{5,1},{6,2},{7,3},{8,4},{9,5},{1... | collective-permute-start | bytes 393224 | tf_op jit(solution)/shard_map/ppermute | solution.py:34
  135.8 6.0 %collective-permute-start.13 = (bf16[64,1024]{1,0:T(8,128)(2,1)}, bf16[64,1024]{1,0:T(8,128)(2,1)}, u32[]{:S(2)}, u32[]{:S(2)}) collective-permute-start(bf16[64,1024]{1,0:T(8,128)(2,1)} %get-tuple-element.24), channel_id=1, source_target_pairs={{0,8},{1,9},{2,10},{3,11},{4,12},{5,13},{6,14},{7,15},{8,0},{9,1},... | collective-permute-start | bytes 393224 | tf_op jit(solution)/shard_map/ppermute | solution.py:34
  143.0 23.3 %collective-permute-start.15 = (bf16[64,1024]{1,0:T(8,128)(2,1)S(1)}, bf16[64,1024]{1,0:T(8,128)(2,1)S(1)}, u32[]{:S(2)}, u32[]{:S(2)}) collective-permute-start(bf16[64,1024]{1,0:T(8,128)(2,1)S(1)} %select_convert_fusion), channel_id=1, source_target_pairs={{0,64},{1,65},{2,66},{3,67},{4,68},{5,69},{6,70},{7,71},{8,72},{9,... | collective-permute-start | bytes 393224 | tf_op jit(solution)/shard_map/ppermute | solution.py:34
Sparse Core Ops, SparseCore 0:
  70.6 39.9 all-gather.1
where the time goes:
time: 188 us; the launch traced here: 187 us
  matrix products  52.1 us (28%)
  starting transfers between devices  40.2 us (21%)
  waiting for transfers between devices  39.9 us (21%)
  local copies, waits for them, and re-layouts  23.8 us (13%)
  other arithmetic  16.5 us (9%)
  between operations  14.3 us (8%)
    dot_general x7, matrix products, dot(): lax.dot_general(a, b, (((ca,), (cb,)), ((), ())), preferred_element_type=...  52.1 us
    ppermute x18, waiting for transfers between devices, send(): return lax.ppermute(value, AXES, moves)  36.2 us
    ppermute x18, starting transfers between devices, send(): return lax.ppermute(value, AXES, moves)  25.5 us
    all_to_all x3, starting transfers between devices, merge(): stats = lax.all_to_all(stats, axis, 0, 0, tiled=True)  14.5 us
    slice x1, local copies, waits for them, and re-layouts, cross(): value = dot(theirs[i], logit_grad, 1, 1, BF16)  7.52 us
    dot_general x1, local copies, waits for them, and re-layouts, dot(): lax.dot_general(a, b, (((ca,), (cb,)), ((), ())), preferred_element_type=...  5.37 us
  transfers between devices with their start and end apart: 22, of which 9 were waited for; matrix products, arithmetic and copies ran while one was open for 41% of the time, Pallas kernels for 0%

commit v1 on v0

--- a/solution.py
+++ b/solution.py
@@ -63,61 +63,60 @@
     other_part = row_major(send(part, HIGH))
     own_part = lax.dynamic_slice(teacher_logits, (high * 1024, 0), (1024, 512))
 
-    logits = dot(hidden_states, head_weight, 1, 0)
+    logits = row_major(dot(hidden_states, head_weight, 1, 0))
     student_top = jnp.max(logits, axis=1)
     student_total = jnp.sum(jnp.exp(logits - student_top[:, None]), axis=1)
-    late, student_total = lax.optimization_barrier((dp, student_total))
-    piece = lax.dynamic_slice(hidden_states, (late * 128, (1 - high) * 2048), (128, 2048))
-    piece = send(piece, HIGH)
-    other_hidden = lax.all_gather(piece, "dp", axis=0, tiled=True)
-    student_top, student_total = merge(jnp.stack([student_top, student_total]), "dp")
-
     first = jnp.where(high == 0, own_part, other_part)
     second = jnp.where(high == 0, other_part, own_part)
     teacher = jnp.concatenate([first, second], axis=1).astype(F32)
     teacher_top = jnp.max(teacher, axis=1)
     teacher_total = jnp.sum(jnp.exp(teacher - teacher_top[:, None]), axis=1)
-    teacher_top, teacher_total = merge(jnp.stack([teacher_top, teacher_total]), "dp")
-    tops, totals = merge(
-        jnp.stack([jnp.stack([student_top, teacher_top]), jnp.stack([student_total, teacher_total])]),
-        "vocab",
+    stats = jnp.stack(
+        [jnp.stack([student_top, teacher_top]), jnp.stack([student_total, teacher_total])]
     )
+    late_core, stats = lax.optimization_barrier((core, stats))
+    stats = jnp.stack(merge(stats, "dp"))
+    late_dp, stats = lax.optimization_barrier((dp, stats))
+    rows = head_weight.reshape(2, 4, 4, 2, 64, 1024)
+    own_rows = pick(rows, late_core, 3).reshape(2, 1024, 1024)
+    theirs = pick(rows, 1 - late_core, 3).reshape(2048, 1024)
+    own_rows, theirs, stats = lax.optimization_barrier((own_rows, theirs, stats))
+    partner_rows = send(theirs, CORE).reshape(2, 1024, 1024)
+    tops, totals = merge(stats, "vocab")
+
+    piece = lax.dynamic_slice(hidden_states, (late_dp * 128, (1 - high) * 2048), (128, 2048))
+    piece = send(piece, HIGH)
+    piece, tops = lax.optimization_barrier((piece, tops))
+    other_hidden = lax.all_gather(piece, "dp", axis=0, tiled=True)
+
     student_norm, teacher_norm = tops + jnp.log(totals)
 
     logit_grad = (
         token_weight[:, None]
         * (jnp.exp(logits - student_norm[:, None]) - jnp.exp(teacher - teacher_norm[:, None]))
     ).astype(BF16)
+    partner_grad = send(logit_grad, CORE)
     other_grad = send(logit_grad, HIGH)
 
-    rows = head_weight.reshape(2, 4, 4, 2, 64, 1024)
-    theirs = pick(rows, 1 - core, 3).reshape(2, 1024, 1024)
-    mine = pick(rows, core, 3).reshape(2, 1024, 1024)
-
-    def cross(i):
-        value = dot(theirs[i], logit_grad, 1, 1, BF16)
-        return send(value, CORE)
-
-    def join(i, got):
-        here = dot(mine[i], logit_grad, 1, 1)
-        return (here + got.astype(F32)).astype(BF16).reshape(4, 4, 64, 1024)
+    def partial(i):
+        here = lax.optimization_barrier(dot(own_rows[i], logit_grad, 1, 1))
+        here = here + dot(partner_rows[i], partner_grad, 1, 1)
+        return here.astype(BF16).reshape(4, 4, 64, 1024)
 
     def exchange(value, axis, place, moves):
         arrived = [send(pick(value, (place + k) % 4, axis), moves[k]) for k in (1, 2, 3)]
         return pick(value, place, axis).astype(F32) + sum(a.astype(F32) for a in arrived)
 
-    got = [cross(i) for i in range(2)]
-    a, b = (join(i, got[i]) for i in range(2))
-    a = exchange(a, 1, z, Z)
-    b = exchange(b, 0, y, Y)
+    a = exchange(partial(0), 1, z, Z)
+    b = exchange(partial(1), 0, y, Y)
     a = exchange(a.astype(BF16), 0, y, Y)
     b = exchange(b.astype(BF16), 0, z, Z)
     arrived = send(jnp.where(low == 0, b, a).astype(BF16), LOW)
     hidden_grad = (jnp.where(low == 0, a, b) + arrived.astype(F32)).astype(BF16).T
 
     own_hidden = lax.dynamic_slice(hidden_states, (0, high * 2048), (1024, 2048))
-    weight_grad = lax.optimization_barrier(dot(own_hidden, logit_grad, 0, 0))
-    weight_grad = (weight_grad + dot(other_hidden, other_grad, 0, 0)).astype(BF16)
+    own_share = lax.optimization_barrier(dot(own_hidden, logit_grad, 0, 0))
+    weight_grad = (own_share + dot(other_hidden, other_grad, 0, 0)).astype(BF16)
     return hidden_grad, weight_grad
 
 

time: 188 us -> 198 us (1.053)
  the two profiles are of different devices: /device:TPU:1 before, /device:TPU:32 now
where the time goes in v1:
time: 198 us; the launch traced here: 197 us
  matrix products  54.3 us (27%)
  waiting for transfers between devices  48.1 us (24%)
  starting transfers between devices  30.5 us (15%)
  other arithmetic  17.6 us (9%)
  blocking collectives  16.6 us (8%)
  local copies, waits for them, and re-layouts  16.1 us (8%)
  between operations  14.2 us (7%)
    dot_general x7, matrix products, dot(): lax.dot_general(a, b, (((ca,), (cb,)), ((), ())), preferred_element_type=...  54.3 us
    ppermute x18, waiting for transfers between devices, send(): return lax.ppermute(value, AXES, moves)  48 us
    ppermute x18, starting transfers between devices, send(): return lax.ppermute(value, AXES, moves)  25.1 us
    all_to_all x1, blocking collectives, merge(): stats = lax.all_to_all(stats, axis, 0, 0, tiled=True)  16.6 us
    dynamic_slice x1, local copies, waits for them, and re-layouts, pick(): return lax.dynamic_index_in_dim(value, index, axis, keepdims=False)  8.47 us
    all_to_all x1, starting transfers between devices, merge(): stats = lax.all_to_all(stats, axis, 0, 0, tiled=True)  5.42 us
    convert_element_type x1, other arithmetic, compute(): logit_grad = (token_weight[:, None] * (jnp.exp(logits - student_norm[:, N...  4.3 us
  transfers between devices with their start and end apart: 20, of which 10 were waited for; matrix products, arithmetic and copies ran while one was open for 35% of the time, Pallas kernels for 0%

profile of v1, /device:TPU:32, one launch (start us, length us, event | category | flops | bytes accessed | tf_op | source)
XLA Modules:
  0.0 197.5 jit_solution(10400107071569975256)
XLA Ops:
  7.2 1.3 constant_dynamic-slice_fusion.2
  8.5 3.1 %collective-permute-start = (bf16[1024,512]{1,0:T(8,128)(2,1)S(1)}, bf16[1024,512]{1,0:T(8,128)(2,1)S(1)}, u32[]{:S(2)}, u32[]{:S(2)}) collective-permute-start(bf16[1024,512]{1,0:T(8,128)(2,1)S(1)} %constant_dynamic-slice_fusion.2), channel_id=1, source_target_pairs={{0,1},{1,0},{2,3},{3,2},{4,5},{5,4},{6,7},{7,6},{8,9},{9,8},{10,11... | collective-permute-start | bytes 3145736 | tf_op jit(solution)/shard_map/ppermute | solution.py:34
  11.6 15.0 %fusion.31 = (f32[1024]{0:T(1024)S(1)}, f32[1024,1024]{1,0:T(8,128)}) fusion(bf16[1024,4096]{1,0:T(8,128)(2,1)} %param.4, bf16[4096,1024]{1,0:T(8,128)(2,1)} %param.5), kind=kOutput, calls=%fused_computation.73 | convolution fusion | flops 8590982144 | bytes 20975616 | tf_op jit(solution)/shard_map/dot_general | solution.py:42
  26.6 3.1 %exponential_reduce_fusion = f32[1024]{0:T(1024)S(1)} fusion(f32[1024,1024]{1,0:T(8,128)} %get-tuple-element.43, f32[1024]{0:T(1024)S(1)} %get-tuple-element.42), kind=kLoop, calls=%fused_computation.13 | loop fusion | flops 2096128 | bytes 4202496 | tf_op jit(solution)/shard_map/reduce_sum | solution.py:68
  29.7 5.3 %collective-permute-done = bf16[1024,512]{1,0:T(8,128)(2,1)S(1)} collective-permute-done((bf16[1024,512]{1,0:T(8,128)(2,1)S(1)}, bf16[1024,512]{1,0:T(8,128)(2,1)S(1)}, u32[]{:S(2)}, u32[]{:S(2)}) %collective-permute-start) | collective-permute-done | bytes 1048608 | tf_op jit(solution)/shard_map/ppermute | solution.py:34
  35.0 2.2 %fusion.28 = (bf16[1024]{0:T(1024)(128)(2,1)S(1)}, bf16[1024,512]{1,0:T(8,128)(2,1)S(1)}, bf16[1024]{0:T(1024)(128)(2,1)S(1)}, bf16[1024,512]{1,0:T(8,128)(2,1)S(1)}) fusion(bf16[1024,512]{1,0:T(8,128)(2,1)S(1)} %collective-permute-done, bf16[2048,512]{1,0:T(8,128)(2,1)} %param.6, s32[]{:T(128)S(6)} %select_n.139, pred[]{:T(512)S(6)} %eq.24), kind=kLoop, calls=%fused_computation.70 | loop fusion | flops 2095104 | bytes 4198405 | tf_op jit(solution)/shard_map/reduce_max | solution.py:72
  37.1 0.9 fusion.1
  38.1 0.7 broadcast_in_dim.4
  38.8 5.4 %all-to-all-start = ((f32[8,2,2,1024]{3,2,1,0:T(2,128)}), f32[8,2,2,1024]{3,2,1,0:T(2,128)S(1)}, u32[]{:S(2)}, u32[]{:S(2)}) async-start(f32[8,2,2,1024]{3,2,1,0:T(2,128)} %broadcast_in_dim.4), calls=%async_computation | async-start | bytes 262144 | tf_op jit(solution)/shard_map/all_to_all | solution.py:47
  44.2 8.5 %constant_dynamic-slice_fusion = (bf16[2,4,4,1,64,1024]{5,4,3,2,1,0:T(8,128)(2,1)}, bf16[2,4,4,1,64,1024]{5,4,3,2,1,0:T(8,128)(2,1)}) fusion(bf16[2,4,4,2,64,1024]{5,4,3,2,1,0:T(8,128)(2,1)} %bitcast.114, s32[]{:T(128)S(6)} %select_n.144, s32[]{:T(128)S(6)} %select_n.143), kind=kLoop, calls=%fused_computation.66 | loop fusion | bytes 16777224 | tf_op jit(solution)/shard_map/jit(dynamic_index_in_dim)/dynamic_slice | solution.py:38
  52.7 0.0 all-to-all-done
  52.7 0.1 fusion.24
  52.8 0.2 collective-permute-start.2
  53.0 1.1 dynamic_slice.74
  54.1 3.1 %collective-permute-start.1 = (bf16[128,2048]{1,0:T(8,128)(2,1)S(1)}, bf16[128,2048]{1,0:T(8,128)(2,1)S(1)}, u32[]{:S(2)}, u32[]{:S(2)}) collective-permute-start(bf16[128,2048]{1,0:T(8,128)(2,1)S(1)} %dynamic_slice.74), channel_id=1, source_target_pairs={{0,1},{1,0},{2,3},{3,2},{4,5},{5,4},{6,7},{7,6},{8,9},{9,8},{10,11... | collective-permute-start | bytes 1572872 | tf_op jit(solution)/shard_map/ppermute | solution.py:34
  57.2 16.6 %all_to_all.10 = f32[8,2,2,1024]{3,2,1,0:T(2,128)S(1)} all-to-all(f32[8,2,2,1024]{3,2,1,0:T(2,128)S(1)} %broadcast_in_dim.5), channel_id=1, replica_groups=mesh['vocab'=8,'dp'=8,'teacher'=2] {'vocab'}, dimensions={0} | all-to-all | bytes 262144 | tf_op jit(solution)/shard_map/all_to_all | solution.py:47
  73.8 0.1 fusion.22
  73.9 0.0 collective-permute-done.1
  73.9 0.8 copy-done.2
  74.7 0.0 all-gather.2.cloned.1.call-update
  74.8 4.3 %fusion.5 = bf16[1024,1024]{1,0:T(8,128)(2,1)} fusion(f32[1024,1024]{1,0:T(8,128)} %get-tuple-element.43, f32[1024]{0:T(1024)S(1)} %bitcast.122, f32[1024]{0:T(1024)S(1)} %bitcast.121, f32[1024]{0:T(1024)S(1)} %copy-done.4, bf16[1024,512]{1,0:T(8,128)(2,1)S(1)} %get-tuple-element.21, bf16[1024,512]{1,0:T(8,128)(2,1)S(1)} %get-tuple-element.27), kind=kLoop, calls=%fused_computation.8 | loop fusion | flops 9437184 | bytes 8400896 | tf_op jit(solution)/shard_map/convert_element_type | solution.py:97
  79.1 0.0 collective-permute-start.3
  79.1 4.7 %fusion.14 = f32[1024,1024]{1,0:T(8,128)S(1)} fusion(bf16[1024,1024]{1,0:T(8,128)(2,1)} %fusion.5, bf16[2,1024,1024]{2,1,0:T(8,128)(2,1)} %bitcast.116), kind=kOutput, calls=%fused_computation.21 | convolution fusion | flops 2147483648 | bytes 8388608 | tf_op jit(solution)/shard_map/dot_general | solution.py:42
  83.8 4.0 %fusion.12 = f32[1024,1024]{1,0:T(8,128)S(1)} fusion(bf16[1024,1024]{1,0:T(8,128)(2,1)} %fusion.5, bf16[2,1024,1024]{2,1,0:T(8,128)(2,1)S(1)} %bitcast.117), kind=kOutput, calls=%fused_computation.19 | convolution fusion | flops 2147483648 | bytes 8388608 | tf_op jit(solution)/shard_map/dot_general | solution.py:42
  87.9 0.0 collective-permute-done.3
  87.9 0.0 collective-permute-done.2
  87.9 4.0 %fusion.10 = f32[1024,1024]{1,0:T(8,128)S(1)} fusion(bf16[1024,1024]{1,0:T(8,128)(2,1)S(1)} %collective-permute-done.3, bf16[2048,1024]{1,0:T(8,128)(2,1)} %collective-permute-done.2), kind=kOutput, calls=%fused_computation.16 | convolution fusion | flops 2147483648 | bytes 8388608 | tf_op jit(solution)/shard_map/dot_general | solution.py:42
  91.9 1.1 add_convert_fusion.2
  93.1 0.0 copy-start
  93.1 1.1 dynamic-slice_bitcast_fusion.5
  94.1 0.1 collective-permute-start.6
  94.2 2.9 %collective-permute-start.5 = (bf16[4,64,1024]{2,1,0:T(8,128)(2,1)}, bf16[4,64,1024]{2,1,0:T(8,128)(2,1)}, u32[]{:S(2)}, u32[]{:S(2)}) collective-permute-start(bf16[4,64,1024]{2,1,0:T(8,128)(2,1)} %get-tuple-element.33), channel_id=1, source_target_pairs={{0,8},{1,9},{2,10},{3,11},{4,12},{5,13},{6,14},{7,15},{8,0},{9,1},... | collective-permute-start | bytes 1572872 | tf_op jit(solution)/shard_map/ppermute | solution.py:34
  97.1 1.8 collective-permute-start.4
  98.9 4.0 %fusion.8 = f32[1024,1024]{1,0:T(8,128)S(1)} fusion(bf16[1024,1024]{1,0:T(8,128)(2,1)S(1)} %collective-permute-done.3, bf16[2048,1024]{1,0:T(8,128)(2,1)} %collective-permute-done.2), kind=kOutput, calls=%fused_computation.14 | convolution fusion | flops 2147483648 | bytes 8388608 | tf_op jit(solution)/shard_map/dot_general | solution.py:42
  102.9 1.1 add_convert_fusion.1
  104.0 1.2 dynamic-slice_bitcast_fusion.2
  105.2 0.9 collective-permute-start.12
  106.1 1.8 collective-permute-start.11
  108.0 5.9 %collective-permute-done.6 = bf16[4,64,1024]{2,1,0:T(8,128)(2,1)S(1)} collective-permute-done((bf16[4,64,1024]{2,1,0:T(8,128)(2,1)S(1)}, bf16[4,64,1024]{2,1,0:T(8,128)(2,1)S(1)}, u32[]{:S(2)}, u32[]{:S(2)}) %collective-permute-start.6) | collective-permute-done | bytes 524320 | tf_op jit(solution)/shard_map/ppermute | solution.py:34
  113.8 0.8 copy-done.3
  114.6 1.5 collective-permute-start.10
  116.1 9.8 %collective-permute-done.5 = bf16[4,64,1024]{2,1,0:T(8,128)(2,1)} collective-permute-done((bf16[4,64,1024]{2,1,0:T(8,128)(2,1)}, bf16[4,64,1024]{2,1,0:T(8,128)(2,1)}, u32[]{:S(2)}, u32[]{:S(2)}) %collective-permute-start.5) | collective-permute-done | bytes 524320 | tf_op jit(solution)/shard_map/ppermute | solution.py:34
  125.8 3.0 %collective-permute-start.17 = (bf16[1024,1024]{1,0:T(8,128)(2,1)}, bf16[1024,1024]{1,0:T(8,128)(2,1)}, u32[]{:S(2)}, u32[]{:S(2)}) collective-permute-start(bf16[1024,1024]{1,0:T(8,128)(2,1)} %fusion.5), channel_id=1, source_target_pairs={{0,1},{1,0},{2,3},{3,2},{4,5},{5,4},{6,7},{7,6},{8,9},{9,8},{10,11... | collective-permute-start | bytes 6291464 | tf_op jit(solution)/shard_map/ppermute | solution.py:34
  128.8 1.9 fusion.19
  130.7 0.7 dynamic-slice_bitcast_fusion.11
  131.4 2.7 %collective-permute-start.9 = (bf16[64,1024]{1,0:T(8,128)(2,1)S(1)}, bf16[64,1024]{1,0:T(8,128)(2,1)S(1)}, u32[]{:S(2)}, u32[]{:S(2)}) collective-permute-start(bf16[64,1024]{1,0:T(8,128)(2,1)S(1)} %get-tuple-element.38), channel_id=1, source_target_pairs={{0,48},{1,49},{2,50},{3,51},{4,52},{5,53},{6,54},{7,55},{8,56},{9,... | collective-permute-start | bytes 393224 | tf_op jit(solution)/shard_map/ppermute | solution.py:34
  134.2 0.8 collective-permute-start.8
  135.0 0.9 collective-permute-start.7
  135.9 1.7 fusion.18
  137.6 0.1 collective-permute-start.15
  137.7 2.0 collective-permute-done.9
  139.7 1.4 collective-permute-start.14
  141.0 0.9 collective-permute-done.8
  141.9 1.4 collective-permute-done.7
  143.3 0.5 collective-permute-done.15
  143.8 2.3 %collective-permute-done.14 = bf16[64,1024]{1,0:T(8,128)(2,1)S(1)} collective-permute-done((bf16[64,1024]{1,0:T(8,128)(2,1)S(1)}, bf16[64,1024]{1,0:T(8,128)(2,1)S(1)}, u32[]{:S(2)}, u32[]{:S(2)}) %collective-permute-start.14) | collective-permute-done | bytes 131104 | tf_op jit(solution)/shard_map/ppermute | solution.py:34
  146.1 0.8 collective-permute-done.13
  146.9 0.2 select_convert_fusion
  147.1 0.9 collective-permute-start.16
  147.9 10.7 %fusion.6 = f32[2048,1024]{1,0:T(8,128)} fusion(bf16[1024,1024]{1,0:T(8,128)(2,1)} %fusion.5, bf16[1024,4096]{1,0:T(8,128)(2,1)} %param.4, s32[]{:T(128)S(6)} %select_n.165), kind=kOutput, calls=%fused_computation.9 | convolution fusion | flops 4294967296 | bytes 14680068 | tf_op jit(solution)/shard_map/dot_general | solution.py:42
  158.6 19.3 %collective-permute-done.16 = bf16[64,1024]{1,0:T(8,128)(2,1)S(1)} collective-permute-done((bf16[64,1024]{1,0:T(8,128)(2,1)S(1)}, bf16[64,1024]{1,0:T(8,128)(2,1)S(1)}, u32[]{:S(2)}, u32[]{:S(2)}) %collective-permute-start.16) | collective-permute-done | bytes 131104 | tf_op jit(solution)/shard_map/ppermute | solution.py:34
  177.9 0.8 fusion.20
  178.8 0.0 collective-permute-done.17
  178.8 11.8 %add_convert_fusion = bf16[2048,1024]{1,0:T(8,128)(2,1)} fusion(f32[2048,1024]{1,0:T(8,128)} %fusion.6, bf16[1024,2048]{1,0:T(8,128)(2,1)} %all-gather.2.cloned.1.call-done, bf16[1024,1024]{1,0:T(8,128)(2,1)} %collective-permute-done.17), kind=kOutput, calls=%fused_computation | convolution fusion | flops 4299161600 | bytes 18874368 | tf_op jit(solution)/shard_map/dot_general | solution.py:42
  (24 shorter events, 0.2 us)
Async XLA Ops:
  8.5 26.5 %collective-permute-start = (bf16[1024,512]{1,0:T(8,128)(2,1)S(1)}, bf16[1024,512]{1,0:T(8,128)(2,1)S(1)}, u32[]{:S(2)}, u32[]{:S(2)}) collective-permute-start(bf16[1024,512]{1,0:T(8,128)(2,1)S(1)} %constant_dynamic-slice_fusion.2), channel_id=1, source_target_pairs={{0,1},{1,0},{2,3},{3,2},{4,5},{5,4},{6,7},{7,6},{8,9},{9,8},{10,11... | collective-permute-start | bytes 3145736 | tf_op jit(solution)/shard_map/ppermute | solution.py:34
  38.8 13.9 %all-to-all-start = ((f32[8,2,2,1024]{3,2,1,0:T(2,128)}), f32[8,2,2,1024]{3,2,1,0:T(2,128)S(1)}, u32[]{:S(2)}, u32[]{:S(2)}) async-start(f32[8,2,2,1024]{3,2,1,0:T(2,128)} %broadcast_in_dim.4), calls=%async_computation | async-start | bytes 262144 | tf_op jit(solution)/shard_map/all_to_all | solution.py:47
  44.2 134.6 %all-gather.2.cloned.1.call-start = ((), (), s32[]{:S(2)}) async-start(), calls=%async_computation.2 | async-start | bytes 4718592 | tf_op jit(solution)/shard_map/all_gather | solution.py:90
  44.2 30.6 %copy-start.4 = (f32[1024]{0:T(1024)S(1)}, f32[1024]{0:T(1024)}, u32[]{:S(2)}) copy-start(f32[1024]{0:T(1024)} %param.7) | copy-start | bytes 12292
  52.8 35.1 %collective-permute-start.2 = (bf16[2048,1024]{1,0:T(8,128)(2,1)}, bf16[2048,1024]{1,0:T(8,128)(2,1)}, u32[]{:S(2)}, u32[]{:S(2)}) collective-permute-start(bf16[2048,1024]{1,0:T(8,128)(2,1)} %bitcast.115), channel_id=1, source_target_pairs={{0,2},{1,3},{2,0},{3,1},{4,6},{5,7},{6,4},{7,5},{8,10},{9,11},{10,... | collective-permute-start | bytes 12582920 | tf_op jit(solution)/shard_map/ppermute | solution.py:34
  54.1 19.9 %collective-permute-start.1 = (bf16[128,2048]{1,0:T(8,128)(2,1)S(1)}, bf16[128,2048]{1,0:T(8,128)(2,1)S(1)}, u32[]{:S(2)}, u32[]{:S(2)}) collective-permute-start(bf16[128,2048]{1,0:T(8,128)(2,1)S(1)} %dynamic_slice.74), channel_id=1, source_target_pairs={{0,1},{1,0},{2,3},{3,2},{4,5},{5,4},{6,7},{7,6},{8,9},{9,8},{10,11... | collective-permute-start | bytes 1572872 | tf_op jit(solution)/shard_map/ppermute | solution.py:34
  73.9 0.8 copy-start.2
  79.1 8.8 %collective-permute-start.3 = (bf16[1024,1024]{1,0:T(8,128)(2,1)}, bf16[1024,1024]{1,0:T(8,128)(2,1)S(1)}, u32[]{:S(2)}, u32[]{:S(2)}) collective-permute-start(bf16[1024,1024]{1,0:T(8,128)(2,1)} %fusion.5), channel_id=1, source_target_pairs={{0,2},{1,3},{2,0},{3,1},{4,6},{5,7},{6,4},{7,5},{8,10},{9,11},{10,... | collective-permute-start | bytes 6291464 | tf_op jit(solution)/shard_map/ppermute | solution.py:34
  79.1 4.7 %copy-start.1 = (bf16[2,4,4,1,64,1024]{5,4,3,2,1,0:T(8,128)(2,1)S(1)}, bf16[2,4,4,1,64,1024]{5,4,3,2,1,0:T(8,128)(2,1)}, u32[]{:S(2)}) copy-start(bf16[2,4,4,1,64,1024]{5,4,3,2,1,0:T(8,128)(2,1)} %get-tuple-element.25) | copy-start | bytes 12582916
  93.1 9.8 %copy-start = (bf16[1024,1024]{1,0:T(8,128)(2,1)}, bf16[1024,1024]{1,0:T(8,128)(2,1)S(1)}, u32[]{:S(2)}) copy-start(bf16[1024,1024]{1,0:T(8,128)(2,1)S(1)} %add_convert_fusion.2) | copy-start | bytes 6291460
  94.1 19.7 %collective-permute-start.6 = (bf16[4,64,1024]{2,1,0:T(8,128)(2,1)S(1)}, bf16[4,64,1024]{2,1,0:T(8,128)(2,1)S(1)}, u32[]{:S(2)}, u32[]{:S(2)}) collective-permute-start(bf16[4,64,1024]{2,1,0:T(8,128)(2,1)S(1)} %get-tuple-element.32), channel_id=1, source_target_pairs={{0,12},{1,13},{2,14},{3,15},{4,0},{5,1},{6,2},{7,3},{8,4},{9,5},{1... | collective-permute-start | bytes 1572872 | tf_op jit(solution)/shard_map/ppermute | solution.py:34
  94.2 31.6 %collective-permute-start.5 = (bf16[4,64,1024]{2,1,0:T(8,128)(2,1)}, bf16[4,64,1024]{2,1,0:T(8,128)(2,1)}, u32[]{:S(2)}, u32[]{:S(2)}) collective-permute-start(bf16[4,64,1024]{2,1,0:T(8,128)(2,1)} %get-tuple-element.33), channel_id=1, source_target_pairs={{0,8},{1,9},{2,10},{3,11},{4,12},{5,13},{6,14},{7,15},{8,0},{9,1},... | collective-permute-start | bytes 1572872 | tf_op jit(solution)/shard_map/ppermute | solution.py:34
  97.1 31.8 %collective-permute-start.4 = (bf16[4,64,1024]{2,1,0:T(8,128)(2,1)S(1)}, bf16[4,64,1024]{2,1,0:T(8,128)(2,1)}, u32[]{:S(2)}, u32[]{:S(2)}) collective-permute-start(bf16[4,64,1024]{2,1,0:T(8,128)(2,1)S(1)} %get-tuple-element.31), channel_id=1, source_target_pairs={{0,4},{1,5},{2,6},{3,7},{4,8},{5,9},{6,10},{7,11},{8,12},{9,13},{1... | collective-permute-start | bytes 1572872 | tf_op jit(solution)/shard_map/ppermute | solution.py:34
  105.2 29.0 %collective-permute-start.12 = (bf16[4,64,1024]{2,1,0:T(8,128)(2,1)}, bf16[4,64,1024]{2,1,0:T(8,128)(2,1)}, u32[]{:S(2)}, u32[]{:S(2)}) collective-permute-start(bf16[4,64,1024]{2,1,0:T(8,128)(2,1)} %get-tuple-element.29), channel_id=1, source_target_pairs={{0,48},{1,49},{2,50},{3,51},{4,52},{5,53},{6,54},{7,55},{8,56},{9,... | collective-permute-start | bytes 1572872 | tf_op jit(solution)/shard_map/ppermute | solution.py:34
  106.1 28.9 %collective-permute-start.11 = (bf16[4,64,1024]{2,1,0:T(8,128)(2,1)}, bf16[4,64,1024]{2,1,0:T(8,128)(2,1)}, u32[]{:S(2)}, u32[]{:S(2)}) collective-permute-start(bf16[4,64,1024]{2,1,0:T(8,128)(2,1)} %get-tuple-element.30), channel_id=1, source_target_pairs={{0,32},{1,33},{2,34},{3,35},{4,36},{5,37},{6,38},{7,39},{8,40},{9,... | collective-permute-start | bytes 1572872 | tf_op jit(solution)/shard_map/ppermute | solution.py:34
  113.8 0.8 copy-start.3
  114.6 21.3 %collective-permute-start.10 = (bf16[4,64,1024]{2,1,0:T(8,128)(2,1)S(1)}, bf16[4,64,1024]{2,1,0:T(8,128)(2,1)}, u32[]{:S(2)}, u32[]{:S(2)}) collective-permute-start(bf16[4,64,1024]{2,1,0:T(8,128)(2,1)S(1)} %get-tuple-element.28), channel_id=1, source_target_pairs={{0,16},{1,17},{2,18},{3,19},{4,20},{5,21},{6,22},{7,23},{8,24},{9,... | collective-permute-start | bytes 1572872 | tf_op jit(solution)/shard_map/ppermute | solution.py:34
  125.8 52.9 %collective-permute-start.17 = (bf16[1024,1024]{1,0:T(8,128)(2,1)}, bf16[1024,1024]{1,0:T(8,128)(2,1)}, u32[]{:S(2)}, u32[]{:S(2)}) collective-permute-start(bf16[1024,1024]{1,0:T(8,128)(2,1)} %fusion.5), channel_id=1, source_target_pairs={{0,1},{1,0},{2,3},{3,2},{4,5},{5,4},{6,7},{7,6},{8,9},{9,8},{10,11... | collective-permute-start | bytes 6291464 | tf_op jit(solution)/shard_map/ppermute | solution.py:34
  131.4 8.2 %collective-permute-start.9 = (bf16[64,1024]{1,0:T(8,128)(2,1)S(1)}, bf16[64,1024]{1,0:T(8,128)(2,1)S(1)}, u32[]{:S(2)}, u32[]{:S(2)}) collective-permute-start(bf16[64,1024]{1,0:T(8,128)(2,1)S(1)} %get-tuple-element.38), channel_id=1, source_target_pairs={{0,48},{1,49},{2,50},{3,51},{4,52},{5,53},{6,54},{7,55},{8,56},{9,... | collective-permute-start | bytes 393224 | tf_op jit(solution)/shard_map/ppermute | solution.py:34
  134.2 7.8 %collective-permute-start.8 = (bf16[64,1024]{1,0:T(8,128)(2,1)S(1)}, bf16[64,1024]{1,0:T(8,128)(2,1)S(1)}, u32[]{:S(2)}, u32[]{:S(2)}) collective-permute-start(bf16[64,1024]{1,0:T(8,128)(2,1)S(1)} %get-tuple-element.39), channel_id=1, source_target_pairs={{0,32},{1,33},{2,34},{3,35},{4,36},{5,37},{6,38},{7,39},{8,40},{9,... | collective-permute-start | bytes 393224 | tf_op jit(solution)/shard_map/ppermute | solution.py:34
  135.0 8.4 %collective-permute-start.7 = (bf16[64,1024]{1,0:T(8,128)(2,1)}, bf16[64,1024]{1,0:T(8,128)(2,1)S(1)}, u32[]{:S(2)}, u32[]{:S(2)}) collective-permute-start(bf16[64,1024]{1,0:T(8,128)(2,1)} %get-tuple-element.37), channel_id=1, source_target_pairs={{0,16},{1,17},{2,18},{3,19},{4,20},{5,21},{6,22},{7,23},{8,24},{9,... | collective-permute-start | bytes 393224 | tf_op jit(solution)/shard_map/ppermute | solution.py:34
  137.6 6.2 %collective-permute-start.15 = (bf16[64,1024]{1,0:T(8,128)(2,1)S(1)}, bf16[64,1024]{1,0:T(8,128)(2,1)S(1)}, u32[]{:S(2)}, u32[]{:S(2)}) collective-permute-start(bf16[64,1024]{1,0:T(8,128)(2,1)S(1)} %get-tuple-element.35), channel_id=1, source_target_pairs={{0,12},{1,13},{2,14},{3,15},{4,0},{5,1},{6,2},{7,3},{8,4},{9,5},{1... | collective-permute-start | bytes 393224 | tf_op jit(solution)/shard_map/ppermute | solution.py:34
  139.7 6.5 %collective-permute-start.14 = (bf16[64,1024]{1,0:T(8,128)(2,1)S(1)}, bf16[64,1024]{1,0:T(8,128)(2,1)S(1)}, u32[]{:S(2)}, u32[]{:S(2)}) collective-permute-start(bf16[64,1024]{1,0:T(8,128)(2,1)S(1)} %get-tuple-element.36), channel_id=1, source_target_pairs={{0,8},{1,9},{2,10},{3,11},{4,12},{5,13},{6,14},{7,15},{8,0},{9,1},... | collective-permute-start | bytes 393224 | tf_op jit(solution)/shard_map/ppermute | solution.py:34
  141.9 5.0 %collective-permute-start.13 = (bf16[64,1024]{1,0:T(8,128)(2,1)S(1)}, bf16[64,1024]{1,0:T(8,128)(2,1)S(1)}, u32[]{:S(2)}, u32[]{:S(2)}) collective-permute-start(bf16[64,1024]{1,0:T(8,128)(2,1)S(1)} %get-tuple-element.34), channel_id=1, source_target_pairs={{0,4},{1,5},{2,6},{3,7},{4,8},{5,9},{6,10},{7,11},{8,12},{9,13},{1... | collective-permute-start | bytes 393224 | tf_op jit(solution)/shard_map/ppermute | solution.py:34
  147.1 30.9 %collective-permute-start.16 = (bf16[64,1024]{1,0:T(8,128)(2,1)S(1)}, bf16[64,1024]{1,0:T(8,128)(2,1)S(1)}, u32[]{:S(2)}, u32[]{:S(2)}) collective-permute-start(bf16[64,1024]{1,0:T(8,128)(2,1)S(1)} %select_convert_fusion), channel_id=1, source_target_pairs={{0,64},{1,65},{2,66},{3,67},{4,68},{5,69},{6,70},{7,71},{8,72},{9,... | collective-permute-start | bytes 393224 | tf_op jit(solution)/shard_map/ppermute | solution.py:34
Sparse Core Ops, SparseCore 0:
  74.9 38.4 all-gather.1

commit v2 on v1

--- a/solution.py
+++ b/solution.py
@@ -42,8 +42,11 @@
     return lax.dot_general(a, b, (((ca,), (cb,)), ((), ())), preferred_element_type=F32).astype(out)
 
 
+def spread(stats):
+    return jnp.broadcast_to(stats[None], (8,) + stats.shape)
+
+
 def merge(stats, axis):
-    stats = jnp.broadcast_to(stats[None], (8,) + stats.shape)
     stats = lax.all_to_all(stats, axis, 0, 0, tiled=True)
     tops, totals = stats[:, 0], stats[:, 1]
     best = jnp.max(tops, axis=0)
@@ -66,6 +69,10 @@
     logits = row_major(dot(hidden_states, head_weight, 1, 0))
     student_top = jnp.max(logits, axis=1)
     student_total = jnp.sum(jnp.exp(logits - student_top[:, None]), axis=1)
+    late_dp, student_total = lax.optimization_barrier((dp, student_total))
+    piece = lax.dynamic_slice(hidden_states, (late_dp * 128, (1 - high) * 2048), (128, 2048))
+    piece = send(piece, HIGH)
+
     first = jnp.where(high == 0, own_part, other_part)
     second = jnp.where(high == 0, other_part, own_part)
     teacher = jnp.concatenate([first, second], axis=1).astype(F32)
@@ -74,21 +81,20 @@
     stats = jnp.stack(
         [jnp.stack([student_top, teacher_top]), jnp.stack([student_total, teacher_total])]
     )
-    late_core, stats = lax.optimization_barrier((core, stats))
+    late_core, stats = lax.optimization_barrier((core, spread(stats)))
     stats = jnp.stack(merge(stats, "dp"))
-    late_dp, stats = lax.optimization_barrier((dp, stats))
-    rows = head_weight.reshape(2, 4, 4, 2, 64, 1024)
-    own_rows = pick(rows, late_core, 3).reshape(2, 1024, 1024)
-    theirs = pick(rows, 1 - late_core, 3).reshape(2048, 1024)
-    own_rows, theirs, stats = lax.optimization_barrier((own_rows, theirs, stats))
-    partner_rows = send(theirs, CORE).reshape(2, 1024, 1024)
-    tops, totals = merge(stats, "vocab")
-
-    piece = lax.dynamic_slice(hidden_states, (late_dp * 128, (1 - high) * 2048), (128, 2048))
-    piece = send(piece, HIGH)
-    piece, tops = lax.optimization_barrier((piece, tops))
+    piece, stats = lax.optimization_barrier((piece, stats))
     other_hidden = lax.all_gather(piece, "dp", axis=0, tiled=True)
 
+    rows = head_weight.reshape(2, 4, 4, 2, 64, 1024)
+    theirs = pick(rows, 1 - late_core, 3).reshape(2048, 1024)
+    theirs, stats = lax.optimization_barrier((theirs, stats))
+    partner_rows = send(theirs, CORE).reshape(2, 1024, 1024)
+    stats = spread(stats)
+    later_core, stats, _ = lax.optimization_barrier((core, stats, theirs))
+    tops, totals = merge(stats, "vocab")
+    own_rows = pick(rows, later_core, 3).reshape(2, 1024, 1024)
+    own_rows, tops = lax.optimization_barrier((own_rows, tops))
     student_norm, teacher_norm = tops + jnp.log(totals)
 
     logit_grad = (

time: 198 us -> 186 us (0.939)
  blocking collectives: 16.6 us -> 0 us
  starting transfers between devices: 30.5 us -> 33.9 us
  local copies, waits for them, and re-layouts: 16.1 us -> 18.1 us
    all_to_all x1 -> x0, blocking collectives: 16.6 us -> none  [merge(): stats = lax.all_to_all(stats, axis, 0, 0, tiled=True)]
    all_to_all x1 -> x2, starting transfers between devices: 5.42 us -> 11 us  [merge(): stats = lax.all_to_all(stats, axis, 0, 0, tiled=True)]
    ppermute x18, waiting for transfers between devices: 48 us -> 45.3 us  [send(): return lax.ppermute(value, AXES, moves)]
    ppermute x18, starting transfers between devices: 25.1 us -> 22.8 us  [send(): return lax.ppermute(value, AXES, moves)]
    dynamic_slice x1 -> x2, local copies, waits for them, and re-layouts: 8.47 us -> 9.72 us  [pick(): return lax.dynamic_index_in_dim(value, index, axis, keepdims=False)]
  transfers between devices with their start and end apart: 20 -> 21, of which waited for: 10 -> 11; matrix products, arithmetic and copies ran while one was open for 35% -> 41% of each run, Pallas kernels for 0% -> 0%
where the time goes in v2:
time: 186 us; the launch traced here: 185 us
  matrix products  54.2 us (29%)
  waiting for transfers between devices  47 us (25%)
  starting transfers between devices  33.9 us (18%)
  local copies, waits for them, and re-layouts  18.1 us (10%)
  other arithmetic  17.6 us (9%)
  between operations  14.3 us (8%)
    dot_general x7, matrix products, dot(): lax.dot_general(a, b, (((ca,), (cb,)), ((), ())), preferred_element_type=...  54.2 us
    ppermute x18, waiting for transfers between devices, send(): return lax.ppermute(value, AXES, moves)  45.3 us
    ppermute x18, starting transfers between devices, send(): return lax.ppermute(value, AXES, moves)  22.8 us
    all_to_all x2, starting transfers between devices, merge(): stats = lax.all_to_all(stats, axis, 0, 0, tiled=True)  11 us
    dynamic_slice x2, local copies, waits for them, and re-layouts, pick(): return lax.dynamic_index_in_dim(value, index, axis, keepdims=False)  9.72 us
    convert_element_type x1, other arithmetic, compute(): logit_grad = (token_weight[:, None] * (jnp.exp(logits - student_norm[:, N...  4.3 us
  transfers between devices with their start and end apart: 21, of which 11 were waited for; matrix products, arithmetic and copies ran while one was open for 41% of the time, Pallas kernels for 0%

profile of v2, /device:TPU:32, one launch (start us, length us, event | category | flops | bytes accessed | tf_op | source)
XLA Modules:
  0.0 185.0 jit_solution(10430246619279703940)
XLA Ops:
  7.2 1.3 constant_dynamic-slice_fusion.2
  8.5 3.1 %collective-permute-start = (bf16[1024,512]{1,0:T(8,128)(2,1)S(1)}, bf16[1024,512]{1,0:T(8,128)(2,1)S(1)}, u32[]{:S(2)}, u32[]{:S(2)}) collective-permute-start(bf16[1024,512]{1,0:T(8,128)(2,1)S(1)} %constant_dynamic-slice_fusion.2), channel_id=1, source_target_pairs={{0,1},{1,0},{2,3},{3,2},{4,5},{5,4},{6,7},{7,6},{8,9},{9,8},{10,11... | collective-permute-start | bytes 3145736 | tf_op jit(solution)/shard_map/ppermute | solution.py:34
  11.6 15.0 %fusion.31 = (f32[1024]{0:T(1024)S(1)}, f32[1024,1024]{1,0:T(8,128)}) fusion(bf16[1024,4096]{1,0:T(8,128)(2,1)} %param.4, bf16[4096,1024]{1,0:T(8,128)(2,1)} %param.5), kind=kOutput, calls=%fused_computation.73 | convolution fusion | flops 8590982144 | bytes 20975616 | tf_op jit(solution)/shard_map/dot_general | solution.py:42
  26.6 3.1 %exponential_reduce_fusion = f32[1024]{0:T(1024)S(1)} fusion(f32[1024,1024]{1,0:T(8,128)} %get-tuple-element.47, f32[1024]{0:T(1024)S(1)} %get-tuple-element.46), kind=kLoop, calls=%fused_computation.13 | loop fusion | flops 2096128 | bytes 4202496 | tf_op jit(solution)/shard_map/reduce_sum | solution.py:71
  29.7 1.9 %dynamic_slice.73 = bf16[128,2048]{1,0:T(8,128)(2,1)} dynamic-slice(bf16[1024,4096]{1,0:T(8,128)(2,1)} %param.4, s32[]{:T(128)S(6)} %select_n.144, s32[]{:T(128)S(6)} %select_n.145), dynamic_slice_sizes={128,2048} | dynamic-slice | bytes 1048580 | tf_op jit(solution)/shard_map/dynamic_slice | solution.py:73
  31.6 0.5 collective-permute-start.1
  32.1 3.0 %collective-permute-done = bf16[1024,512]{1,0:T(8,128)(2,1)S(1)} collective-permute-done((bf16[1024,512]{1,0:T(8,128)(2,1)S(1)}, bf16[1024,512]{1,0:T(8,128)(2,1)S(1)}, u32[]{:S(2)}, u32[]{:S(2)}) %collective-permute-start) | collective-permute-done | bytes 1048608 | tf_op jit(solution)/shard_map/ppermute | solution.py:34
  35.1 2.2 %fusion.28 = (bf16[1024]{0:T(1024)(128)(2,1)S(1)}, bf16[1024,512]{1,0:T(8,128)(2,1)S(1)}, bf16[1024]{0:T(1024)(128)(2,1)S(1)}, bf16[1024,512]{1,0:T(8,128)(2,1)S(1)}) fusion(bf16[1024,512]{1,0:T(8,128)(2,1)S(1)} %collective-permute-done, bf16[2048,512]{1,0:T(8,128)(2,1)} %param.6, s32[]{:T(128)S(6)} %select_n.139, pred[]{:T(512)S(6)} %eq.24), kind=kLoop, calls=%fused_computation.70 | loop fusion | flops 2095104 | bytes 4198405 | tf_op jit(solution)/shard_map/reduce_max | solution.py:79
  37.3 0.9 fusion.1
  38.2 0.7 broadcast_in_dim.4
  38.9 5.4 %all-to-all-start = ((f32[8,2,2,1024]{3,2,1,0:T(2,128)}), f32[8,2,2,1024]{3,2,1,0:T(2,128)S(1)}, u32[]{:S(2)}, u32[]{:S(2)}) async-start(f32[8,2,2,1024]{3,2,1,0:T(2,128)} %broadcast_in_dim.4), calls=%async_computation | async-start | bytes 262144 | tf_op jit(solution)/shard_map/all_to_all | solution.py:50
  44.3 4.9 %constant_dynamic-slice_fusion.1 = bf16[2,4,4,1,64,1024]{5,4,3,2,1,0:T(8,128)(2,1)} fusion(bf16[2,4,4,2,64,1024]{5,4,3,2,1,0:T(8,128)(2,1)} %bitcast.114, s32[]{:T(128)S(6)} %select_n.143), kind=kLoop, calls=%fused_computation.67 | loop fusion | bytes 8388612 | tf_op jit(solution)/shard_map/jit(dynamic_index_in_dim)/dynamic_slice | solution.py:38
  49.2 0.0 all-to-all-done
  49.3 0.1 fusion.24
  49.4 0.2 collective-permute-start.2
  49.6 0.7 broadcast_in_dim.5
  50.2 5.6 %all-to-all-start.1 = ((f32[8,2,2,1024]{3,2,1,0:T(2,128)}), f32[8,2,2,1024]{3,2,1,0:T(2,128)S(1)}, u32[]{:S(2)}, u32[]{:S(2)}) async-start(f32[8,2,2,1024]{3,2,1,0:T(2,128)} %broadcast_in_dim.5), calls=%async_computation.1 | async-start | bytes 262144 | tf_op jit(solution)/shard_map/all_to_all | solution.py:50
  55.9 0.0 all-gather.2.cloned.1.call-start
  55.9 0.7 all-gather.2.cloned.1.call-update
  56.6 0.0 copy-start.3
  56.6 4.8 %constant_dynamic-slice_fusion = bf16[2,4,4,1,64,1024]{5,4,3,2,1,0:T(8,128)(2,1)} fusion(bf16[2,4,4,2,64,1024]{5,4,3,2,1,0:T(8,128)(2,1)} %bitcast.115, s32[]{:T(128)S(6)} %select_n.146), kind=kLoop, calls=%fused_computation.66 | loop fusion | bytes 8388612 | tf_op jit(solution)/shard_map/jit(dynamic_index_in_dim)/dynamic_slice | solution.py:38
  61.5 1.0 all-to-all-done.1
  62.5 0.1 fusion.22
  62.6 4.3 %fusion.5 = bf16[1024,1024]{1,0:T(8,128)(2,1)} fusion(f32[1024,1024]{1,0:T(8,128)} %get-tuple-element.47, f32[1024]{0:T(1024)S(1)} %bitcast.123, f32[1024]{0:T(1024)S(1)} %bitcast.122, f32[1024]{0:T(1024)S(1)} %copy-done.3, bf16[1024,512]{1,0:T(8,128)(2,1)S(1)} %get-tuple-element.27, bf16[1024,512]{1,0:T(8,128)(2,1)S(1)} %get-tuple-element.31), kind=kLoop, calls=%fused_computation.8 | loop fusion | flops 9437184 | bytes 8400896 | tf_op jit(solution)/shard_map/convert_element_type | solution.py:103
  66.9 0.0 collective-permute-start.3
  66.9 4.7 %fusion.14 = f32[1024,1024]{1,0:T(8,128)S(1)} fusion(bf16[1024,1024]{1,0:T(8,128)(2,1)} %fusion.5, bf16[2,1024,1024]{2,1,0:T(8,128)(2,1)} %bitcast.117), kind=kOutput, calls=%fused_computation.21 | convolution fusion | flops 2147483648 | bytes 8388608 | tf_op jit(solution)/shard_map/dot_general | solution.py:42
  71.7 4.0 %fusion.12 = f32[1024,1024]{1,0:T(8,128)S(1)} fusion(bf16[1024,1024]{1,0:T(8,128)(2,1)} %fusion.5, bf16[2,1024,1024]{2,1,0:T(8,128)(2,1)S(1)} %bitcast.118), kind=kOutput, calls=%fused_computation.19 | convolution fusion | flops 2147483648 | bytes 8388608 | tf_op jit(solution)/shard_map/dot_general | solution.py:42
  75.7 4.0 %fusion.10 = f32[1024,1024]{1,0:T(8,128)S(1)} fusion(bf16[1024,1024]{1,0:T(8,128)(2,1)S(1)} %collective-permute-done.3, bf16[2048,1024]{1,0:T(8,128)(2,1)} %collective-permute-done.2), kind=kOutput, calls=%fused_computation.16 | convolution fusion | flops 2147483648 | bytes 8388608 | tf_op jit(solution)/shard_map/dot_general | solution.py:42
  79.7 1.1 add_convert_fusion.2
  80.8 0.0 copy-start
  80.8 1.1 dynamic-slice_bitcast_fusion.5
  81.9 1.3 collective-permute-start.6
  83.2 1.6 collective-permute-start.5
  84.8 1.8 collective-permute-start.4
  86.7 4.0 %fusion.8 = f32[1024,1024]{1,0:T(8,128)S(1)} fusion(bf16[1024,1024]{1,0:T(8,128)(2,1)S(1)} %collective-permute-done.3, bf16[2048,1024]{1,0:T(8,128)(2,1)} %collective-permute-done.2), kind=kOutput, calls=%fused_computation.14 | convolution fusion | flops 2147483648 | bytes 8388608 | tf_op jit(solution)/shard_map/dot_general | solution.py:42
  90.6 1.1 add_convert_fusion.1
  91.8 1.2 dynamic-slice_bitcast_fusion.2
  92.9 2.3 %collective-permute-start.12 = (bf16[4,64,1024]{2,1,0:T(8,128)(2,1)}, bf16[4,64,1024]{2,1,0:T(8,128)(2,1)}, u32[]{:S(2)}, u32[]{:S(2)}) collective-permute-start(bf16[4,64,1024]{2,1,0:T(8,128)(2,1)} %get-tuple-element.33), channel_id=1, source_target_pairs={{0,48},{1,49},{2,50},{3,51},{4,52},{5,53},{6,54},{7,55},{8,56},{9,... | collective-permute-start | bytes 1572872 | tf_op jit(solution)/shard_map/ppermute | solution.py:34
  95.2 0.9 collective-permute-start.11
  96.1 5.2 %collective-permute-done.6 = bf16[4,64,1024]{2,1,0:T(8,128)(2,1)S(1)} collective-permute-done((bf16[4,64,1024]{2,1,0:T(8,128)(2,1)S(1)}, bf16[4,64,1024]{2,1,0:T(8,128)(2,1)S(1)}, u32[]{:S(2)}, u32[]{:S(2)}) %collective-permute-start.6) | collective-permute-done | bytes 524320 | tf_op jit(solution)/shard_map/ppermute | solution.py:34
  101.4 0.8 copy-done.2
  102.2 1.5 collective-permute-start.10
  103.6 9.8 %collective-permute-done.5 = bf16[4,64,1024]{2,1,0:T(8,128)(2,1)} collective-permute-done((bf16[4,64,1024]{2,1,0:T(8,128)(2,1)}, bf16[4,64,1024]{2,1,0:T(8,128)(2,1)}, u32[]{:S(2)}, u32[]{:S(2)}) %collective-permute-start.5) | collective-permute-done | bytes 524320 | tf_op jit(solution)/shard_map/ppermute | solution.py:34
  113.4 3.0 %collective-permute-start.17 = (bf16[1024,1024]{1,0:T(8,128)(2,1)}, bf16[1024,1024]{1,0:T(8,128)(2,1)}, u32[]{:S(2)}, u32[]{:S(2)}) collective-permute-start(bf16[1024,1024]{1,0:T(8,128)(2,1)} %fusion.5), channel_id=1, source_target_pairs={{0,1},{1,0},{2,3},{3,2},{4,5},{5,4},{6,7},{7,6},{8,9},{9,8},{10,11... | collective-permute-start | bytes 6291464 | tf_op jit(solution)/shard_map/ppermute | solution.py:34
  116.4 1.9 %fusion.19 = bf16[4,64,1024]{2,1,0:T(8,128)(2,1)S(1)} fusion(bf16[4,64,1024]{2,1,0:T(8,128)(2,1)} %copy-done.2, bf16[4,64,1024]{2,1,0:T(8,128)(2,1)} %collective-permute-done.5, bf16[4,64,1024]{2,1,0:T(8,128)(2,1)} %collective-permute-done.4, bf16[4,4,64,1024]{3,2,1,0:T(8,128)(2,1)} %bitcast.113, s32[]{:T(128)S(6)} %select_n.148), kind=kLoop, calls=%fused_computation.28 | loop fusion | flops 2097152 | bytes 2621444 | tf_op jit(solution)/shard_map/convert_element_type | solution.py:118
  118.3 0.7 dynamic-slice_bitcast_fusion.11
  119.0 2.7 %collective-permute-start.9 = (bf16[64,1024]{1,0:T(8,128)(2,1)S(1)}, bf16[64,1024]{1,0:T(8,128)(2,1)S(1)}, u32[]{:S(2)}, u32[]{:S(2)}) collective-permute-start(bf16[64,1024]{1,0:T(8,128)(2,1)S(1)} %get-tuple-element.42), channel_id=1, source_target_pairs={{0,48},{1,49},{2,50},{3,51},{4,52},{5,53},{6,54},{7,55},{8,56},{9,... | collective-permute-start | bytes 393224 | tf_op jit(solution)/shard_map/ppermute | solution.py:34
  121.7 0.8 collective-permute-start.8
  122.5 0.9 collective-permute-start.7
  123.4 1.7 fusion.18
  125.2 0.1 collective-permute-start.15
  125.3 2.0 %collective-permute-done.9 = bf16[64,1024]{1,0:T(8,128)(2,1)S(1)} collective-permute-done((bf16[64,1024]{1,0:T(8,128)(2,1)S(1)}, bf16[64,1024]{1,0:T(8,128)(2,1)S(1)}, u32[]{:S(2)}, u32[]{:S(2)}) %collective-permute-start.9) | collective-permute-done | bytes 131104 | tf_op jit(solution)/shard_map/ppermute | solution.py:34
  127.2 1.3 collective-permute-start.14
  128.5 1.0 collective-permute-done.8
  129.5 1.4 collective-permute-done.7
  130.9 0.5 collective-permute-done.15
  131.4 2.3 %collective-permute-done.14 = bf16[64,1024]{1,0:T(8,128)(2,1)S(1)} collective-permute-done((bf16[64,1024]{1,0:T(8,128)(2,1)S(1)}, bf16[64,1024]{1,0:T(8,128)(2,1)S(1)}, u32[]{:S(2)}, u32[]{:S(2)}) %collective-permute-start.14) | collective-permute-done | bytes 131104 | tf_op jit(solution)/shard_map/ppermute | solution.py:34
  133.7 0.8 collective-permute-done.13
  134.5 0.2 select_convert_fusion
  134.6 0.9 collective-permute-start.16
  135.5 10.7 %fusion.6 = f32[2048,1024]{1,0:T(8,128)} fusion(bf16[1024,1024]{1,0:T(8,128)(2,1)} %fusion.5, bf16[1024,4096]{1,0:T(8,128)(2,1)} %param.4, s32[]{:T(128)S(6)} %select_n.165), kind=kOutput, calls=%fused_computation.9 | convolution fusion | flops 4294967296 | bytes 14680068 | tf_op jit(solution)/shard_map/dot_general | solution.py:42
  146.2 19.3 %collective-permute-done.16 = bf16[64,1024]{1,0:T(8,128)(2,1)S(1)} collective-permute-done((bf16[64,1024]{1,0:T(8,128)(2,1)S(1)}, bf16[64,1024]{1,0:T(8,128)(2,1)S(1)}, u32[]{:S(2)}, u32[]{:S(2)}) %collective-permute-start.16) | collective-permute-done | bytes 131104 | tf_op jit(solution)/shard_map/ppermute | solution.py:34
  165.5 0.8 fusion.20
  166.3 11.8 %add_convert_fusion = bf16[2048,1024]{1,0:T(8,128)(2,1)} fusion(f32[2048,1024]{1,0:T(8,128)} %fusion.6, bf16[1024,2048]{1,0:T(8,128)(2,1)} %all-gather.2.cloned.1.call-done, bf16[1024,1024]{1,0:T(8,128)(2,1)} %collective-permute-done.17), kind=kOutput, calls=%fused_computation | convolution fusion | flops 4299161600 | bytes 18874368 | tf_op jit(solution)/shard_map/dot_general | solution.py:42
  (24 shorter events, 0.2 us)
Async XLA Ops:
  8.5 26.7 %collective-permute-start = (bf16[1024,512]{1,0:T(8,128)(2,1)S(1)}, bf16[1024,512]{1,0:T(8,128)(2,1)S(1)}, u32[]{:S(2)}, u32[]{:S(2)}) collective-permute-start(bf16[1024,512]{1,0:T(8,128)(2,1)S(1)} %constant_dynamic-slice_fusion.2), channel_id=1, source_target_pairs={{0,1},{1,0},{2,3},{3,2},{4,5},{5,4},{6,7},{7,6},{8,9},{9,8},{10,11... | collective-permute-start | bytes 3145736 | tf_op jit(solution)/shard_map/ppermute | solution.py:34
  31.6 17.8 %collective-permute-start.1 = (bf16[128,2048]{1,0:T(8,128)(2,1)}, bf16[128,2048]{1,0:T(8,128)(2,1)}, u32[]{:S(2)}, u32[]{:S(2)}) collective-permute-start(bf16[128,2048]{1,0:T(8,128)(2,1)} %dynamic_slice.73), channel_id=1, source_target_pairs={{0,1},{1,0},{2,3},{3,2},{4,5},{5,4},{6,7},{7,6},{8,9},{9,8},{10,11... | collective-permute-start | bytes 1572872 | tf_op jit(solution)/shard_map/ppermute | solution.py:34
  38.9 10.3 %all-to-all-start = ((f32[8,2,2,1024]{3,2,1,0:T(2,128)}), f32[8,2,2,1024]{3,2,1,0:T(2,128)S(1)}, u32[]{:S(2)}, u32[]{:S(2)}) async-start(f32[8,2,2,1024]{3,2,1,0:T(2,128)} %broadcast_in_dim.4), calls=%async_computation | async-start | bytes 262144 | tf_op jit(solution)/shard_map/all_to_all | solution.py:50
  49.4 26.3 %collective-permute-start.2 = (bf16[2048,1024]{1,0:T(8,128)(2,1)}, bf16[2048,1024]{1,0:T(8,128)(2,1)}, u32[]{:S(2)}, u32[]{:S(2)}) collective-permute-start(bf16[2048,1024]{1,0:T(8,128)(2,1)} %bitcast.116), channel_id=1, source_target_pairs={{0,2},{1,3},{2,0},{3,1},{4,6},{5,7},{6,4},{7,5},{8,10},{9,11},{10,... | collective-permute-start | bytes 12582920 | tf_op jit(solution)/shard_map/ppermute | solution.py:34
  50.2 12.2 %all-to-all-start.1 = ((f32[8,2,2,1024]{3,2,1,0:T(2,128)}), f32[8,2,2,1024]{3,2,1,0:T(2,128)S(1)}, u32[]{:S(2)}, u32[]{:S(2)}) async-start(f32[8,2,2,1024]{3,2,1,0:T(2,128)} %broadcast_in_dim.5), calls=%async_computation.1 | async-start | bytes 262144 | tf_op jit(solution)/shard_map/all_to_all | solution.py:50
  55.9 110.5 %all-gather.2.cloned.1.call-start = ((), (), s32[]{:S(2)}) async-start(), calls=%async_computation.2 | async-start | bytes 4718592 | tf_op jit(solution)/shard_map/all_gather | solution.py:87
  56.6 6.0 %copy-start.3 = (f32[1024]{0:T(1024)S(1)}, f32[1024]{0:T(1024)}, u32[]{:S(2)}) copy-start(f32[1024]{0:T(1024)} %param.7) | copy-start | bytes 12292
  66.9 8.8 %collective-permute-start.3 = (bf16[1024,1024]{1,0:T(8,128)(2,1)}, bf16[1024,1024]{1,0:T(8,128)(2,1)S(1)}, u32[]{:S(2)}, u32[]{:S(2)}) collective-permute-start(bf16[1024,1024]{1,0:T(8,128)(2,1)} %fusion.5), channel_id=1, source_target_pairs={{0,2},{1,3},{2,0},{3,1},{4,6},{5,7},{6,4},{7,5},{8,10},{9,11},{10,... | collective-permute-start | bytes 6291464 | tf_op jit(solution)/shard_map/ppermute | solution.py:34
  66.9 4.8 %copy-start.1 = (bf16[2,4,4,1,64,1024]{5,4,3,2,1,0:T(8,128)(2,1)S(1)}, bf16[2,4,4,1,64,1024]{5,4,3,2,1,0:T(8,128)(2,1)}, u32[]{:S(2)}) copy-start(bf16[2,4,4,1,64,1024]{5,4,3,2,1,0:T(8,128)(2,1)} %constant_dynamic-slice_fusion) | copy-start | bytes 12582916
  80.8 9.8 %copy-start = (bf16[1024,1024]{1,0:T(8,128)(2,1)}, bf16[1024,1024]{1,0:T(8,128)(2,1)S(1)}, u32[]{:S(2)}) copy-start(bf16[1024,1024]{1,0:T(8,128)(2,1)S(1)} %add_convert_fusion.2) | copy-start | bytes 6291460
  81.9 19.5 %collective-permute-start.6 = (bf16[4,64,1024]{2,1,0:T(8,128)(2,1)S(1)}, bf16[4,64,1024]{2,1,0:T(8,128)(2,1)S(1)}, u32[]{:S(2)}, u32[]{:S(2)}) collective-permute-start(bf16[4,64,1024]{2,1,0:T(8,128)(2,1)S(1)} %get-tuple-element.36), channel_id=1, source_target_pairs={{0,12},{1,13},{2,14},{3,15},{4,0},{5,1},{6,2},{7,3},{8,4},{9,5},{1... | collective-permute-start | bytes 1572872 | tf_op jit(solution)/shard_map/ppermute | solution.py:34
  83.2 30.2 %collective-permute-start.5 = (bf16[4,64,1024]{2,1,0:T(8,128)(2,1)}, bf16[4,64,1024]{2,1,0:T(8,128)(2,1)}, u32[]{:S(2)}, u32[]{:S(2)}) collective-permute-start(bf16[4,64,1024]{2,1,0:T(8,128)(2,1)} %get-tuple-element.37), channel_id=1, source_target_pairs={{0,8},{1,9},{2,10},{3,11},{4,12},{5,13},{6,14},{7,15},{8,0},{9,1},... | collective-permute-start | bytes 1572872 | tf_op jit(solution)/shard_map/ppermute | solution.py:34
  84.8 31.6 %collective-permute-start.4 = (bf16[4,64,1024]{2,1,0:T(8,128)(2,1)S(1)}, bf16[4,64,1024]{2,1,0:T(8,128)(2,1)}, u32[]{:S(2)}, u32[]{:S(2)}) collective-permute-start(bf16[4,64,1024]{2,1,0:T(8,128)(2,1)S(1)} %get-tuple-element.35), channel_id=1, source_target_pairs={{0,4},{1,5},{2,6},{3,7},{4,8},{5,9},{6,10},{7,11},{8,12},{9,13},{1... | collective-permute-start | bytes 1572872 | tf_op jit(solution)/shard_map/ppermute | solution.py:34
  92.9 28.8 %collective-permute-start.12 = (bf16[4,64,1024]{2,1,0:T(8,128)(2,1)}, bf16[4,64,1024]{2,1,0:T(8,128)(2,1)}, u32[]{:S(2)}, u32[]{:S(2)}) collective-permute-start(bf16[4,64,1024]{2,1,0:T(8,128)(2,1)} %get-tuple-element.33), channel_id=1, source_target_pairs={{0,48},{1,49},{2,50},{3,51},{4,52},{5,53},{6,54},{7,55},{8,56},{9,... | collective-permute-start | bytes 1572872 | tf_op jit(solution)/shard_map/ppermute | solution.py:34
  95.2 27.3 %collective-permute-start.11 = (bf16[4,64,1024]{2,1,0:T(8,128)(2,1)}, bf16[4,64,1024]{2,1,0:T(8,128)(2,1)}, u32[]{:S(2)}, u32[]{:S(2)}) collective-permute-start(bf16[4,64,1024]{2,1,0:T(8,128)(2,1)} %get-tuple-element.34), channel_id=1, source_target_pairs={{0,32},{1,33},{2,34},{3,35},{4,36},{5,37},{6,38},{7,39},{8,40},{9,... | collective-permute-start | bytes 1572872 | tf_op jit(solution)/shard_map/ppermute | solution.py:34
  101.4 0.8 copy-start.2
  102.2 21.3 %collective-permute-start.10 = (bf16[4,64,1024]{2,1,0:T(8,128)(2,1)S(1)}, bf16[4,64,1024]{2,1,0:T(8,128)(2,1)}, u32[]{:S(2)}, u32[]{:S(2)}) collective-permute-start(bf16[4,64,1024]{2,1,0:T(8,128)(2,1)S(1)} %get-tuple-element.32), channel_id=1, source_target_pairs={{0,16},{1,17},{2,18},{3,19},{4,20},{5,21},{6,22},{7,23},{8,24},{9,... | collective-permute-start | bytes 1572872 | tf_op jit(solution)/shard_map/ppermute | solution.py:34
  113.4 52.9 %collective-permute-start.17 = (bf16[1024,1024]{1,0:T(8,128)(2,1)}, bf16[1024,1024]{1,0:T(8,128)(2,1)}, u32[]{:S(2)}, u32[]{:S(2)}) collective-permute-start(bf16[1024,1024]{1,0:T(8,128)(2,1)} %fusion.5), channel_id=1, source_target_pairs={{0,1},{1,0},{2,3},{3,2},{4,5},{5,4},{6,7},{7,6},{8,9},{9,8},{10,11... | collective-permute-start | bytes 6291464 | tf_op jit(solution)/shard_map/ppermute | solution.py:34
  119.0 8.3 %collective-permute-start.9 = (bf16[64,1024]{1,0:T(8,128)(2,1)S(1)}, bf16[64,1024]{1,0:T(8,128)(2,1)S(1)}, u32[]{:S(2)}, u32[]{:S(2)}) collective-permute-start(bf16[64,1024]{1,0:T(8,128)(2,1)S(1)} %get-tuple-element.42), channel_id=1, source_target_pairs={{0,48},{1,49},{2,50},{3,51},{4,52},{5,53},{6,54},{7,55},{8,56},{9,... | collective-permute-start | bytes 393224 | tf_op jit(solution)/shard_map/ppermute | solution.py:34
  121.7 7.8 %collective-permute-start.8 = (bf16[64,1024]{1,0:T(8,128)(2,1)S(1)}, bf16[64,1024]{1,0:T(8,128)(2,1)S(1)}, u32[]{:S(2)}, u32[]{:S(2)}) collective-permute-start(bf16[64,1024]{1,0:T(8,128)(2,1)S(1)} %get-tuple-element.43), channel_id=1, source_target_pairs={{0,32},{1,33},{2,34},{3,35},{4,36},{5,37},{6,38},{7,39},{8,40},{9,... | collective-permute-start | bytes 393224 | tf_op jit(solution)/shard_map/ppermute | solution.py:34
  122.5 8.4 %collective-permute-start.7 = (bf16[64,1024]{1,0:T(8,128)(2,1)}, bf16[64,1024]{1,0:T(8,128)(2,1)S(1)}, u32[]{:S(2)}, u32[]{:S(2)}) collective-permute-start(bf16[64,1024]{1,0:T(8,128)(2,1)} %get-tuple-element.41), channel_id=1, source_target_pairs={{0,16},{1,17},{2,18},{3,19},{4,20},{5,21},{6,22},{7,23},{8,24},{9,... | collective-permute-start | bytes 393224 | tf_op jit(solution)/shard_map/ppermute | solution.py:34
  125.2 6.2 %collective-permute-start.15 = (bf16[64,1024]{1,0:T(8,128)(2,1)S(1)}, bf16[64,1024]{1,0:T(8,128)(2,1)S(1)}, u32[]{:S(2)}, u32[]{:S(2)}) collective-permute-start(bf16[64,1024]{1,0:T(8,128)(2,1)S(1)} %get-tuple-element.39), channel_id=1, source_target_pairs={{0,12},{1,13},{2,14},{3,15},{4,0},{5,1},{6,2},{7,3},{8,4},{9,5},{1... | collective-permute-start | bytes 393224 | tf_op jit(solution)/shard_map/ppermute | solution.py:34
  127.2 6.5 %collective-permute-start.14 = (bf16[64,1024]{1,0:T(8,128)(2,1)S(1)}, bf16[64,1024]{1,0:T(8,128)(2,1)S(1)}, u32[]{:S(2)}, u32[]{:S(2)}) collective-permute-start(bf16[64,1024]{1,0:T(8,128)(2,1)S(1)} %get-tuple-element.40), channel_id=1, source_target_pairs={{0,8},{1,9},{2,10},{3,11},{4,12},{5,13},{6,14},{7,15},{8,0},{9,1},... | collective-permute-start | bytes 393224 | tf_op jit(solution)/shard_map/ppermute | solution.py:34
  129.5 5.0 %collective-permute-start.13 = (bf16[64,1024]{1,0:T(8,128)(2,1)S(1)}, bf16[64,1024]{1,0:T(8,128)(2,1)S(1)}, u32[]{:S(2)}, u32[]{:S(2)}) collective-permute-start(bf16[64,1024]{1,0:T(8,128)(2,1)S(1)} %get-tuple-element.38), channel_id=1, source_target_pairs={{0,4},{1,5},{2,6},{3,7},{4,8},{5,9},{6,10},{7,11},{8,12},{9,13},{1... | collective-permute-start | bytes 393224 | tf_op jit(solution)/shard_map/ppermute | solution.py:34
  134.6 30.9 %collective-permute-start.16 = (bf16[64,1024]{1,0:T(8,128)(2,1)S(1)}, bf16[64,1024]{1,0:T(8,128)(2,1)S(1)}, u32[]{:S(2)}, u32[]{:S(2)}) collective-permute-start(bf16[64,1024]{1,0:T(8,128)(2,1)S(1)} %select_convert_fusion), channel_id=1, source_target_pairs={{0,64},{1,65},{2,66},{3,67},{4,68},{5,69},{6,70},{7,71},{8,72},{9,... | collective-permute-start | bytes 393224 | tf_op jit(solution)/shard_map/ppermute | solution.py:34
Sparse Core Ops, SparseCore 0:
  58.4 42.2 all-gather.1

commit v3 on v2

--- a/solution.py
+++ b/solution.py
@@ -62,6 +62,18 @@
     low, y = vocab // 4, vocab % 4
     z, core = dp // 2, dp % 2
 
+    shard = teacher_logits.astype(F32)
+    top = jnp.max(shard, axis=1)
+    total = jnp.sum(jnp.exp(shard - top[:, None]), axis=1)
+    stats = jnp.stack([top.reshape(2, 1024), total.reshape(2, 1024)], axis=1)
+    theirs = send(jnp.where(high == 0, stats[1], stats[0]), HIGH)
+    mine = jnp.where(high == 0, stats[0], stats[1])
+    teacher_top = jnp.maximum(mine[0], theirs[0])
+    teacher_total = mine[1] * jnp.exp(mine[0] - teacher_top) + theirs[1] * jnp.exp(theirs[0] - teacher_top)
+
+    piece = lax.dynamic_slice(hidden_states, (dp * 128, (1 - high) * 2048), (128, 2048))
+    piece = send(piece, HIGH)
+
     part = row_major(lax.dynamic_slice(teacher_logits, ((1 - high) * 1024, 0), (1024, 512)))
     other_part = row_major(send(part, HIGH))
     own_part = lax.dynamic_slice(teacher_logits, (high * 1024, 0), (1024, 512))
@@ -69,33 +81,27 @@
     logits = row_major(dot(hidden_states, head_weight, 1, 0))
     student_top = jnp.max(logits, axis=1)
     student_total = jnp.sum(jnp.exp(logits - student_top[:, None]), axis=1)
-    late_dp, student_total = lax.optimization_barrier((dp, student_total))
-    piece = lax.dynamic_slice(hidden_states, (late_dp * 128, (1 - high) * 2048), (128, 2048))
-    piece = send(piece, HIGH)
+    piece, student_total = lax.optimization_barrier((piece, student_total))
+    other_hidden = lax.all_gather(piece, "dp", axis=0, tiled=True)
 
-    first = jnp.where(high == 0, own_part, other_part)
-    second = jnp.where(high == 0, other_part, own_part)
-    teacher = jnp.concatenate([first, second], axis=1).astype(F32)
-    teacher_top = jnp.max(teacher, axis=1)
-    teacher_total = jnp.sum(jnp.exp(teacher - teacher_top[:, None]), axis=1)
     stats = jnp.stack(
         [jnp.stack([student_top, teacher_top]), jnp.stack([student_total, teacher_total])]
     )
     late_core, stats = lax.optimization_barrier((core, spread(stats)))
     stats = jnp.stack(merge(stats, "dp"))
-    piece, stats = lax.optimization_barrier((piece, stats))
-    other_hidden = lax.all_gather(piece, "dp", axis=0, tiled=True)
 
     rows = head_weight.reshape(2, 4, 4, 2, 64, 1024)
     theirs = pick(rows, 1 - late_core, 3).reshape(2048, 1024)
     theirs, stats = lax.optimization_barrier((theirs, stats))
     partner_rows = send(theirs, CORE).reshape(2, 1024, 1024)
-    stats = spread(stats)
-    later_core, stats, _ = lax.optimization_barrier((core, stats, theirs))
+    later_core, stats, _ = lax.optimization_barrier((core, spread(stats), theirs))
     tops, totals = merge(stats, "vocab")
     own_rows = pick(rows, later_core, 3).reshape(2, 1024, 1024)
     own_rows, tops = lax.optimization_barrier((own_rows, tops))
     student_norm, teacher_norm = tops + jnp.log(totals)
+    first = jnp.where(high == 0, own_part, other_part)
+    second = jnp.where(high == 0, other_part, own_part)
+    teacher = jnp.concatenate([first, second], axis=1).astype(F32)
 
     logit_grad = (
         token_weight[:, None]
@@ -122,7 +128,12 @@
 
     own_hidden = lax.dynamic_slice(hidden_states, (0, high * 2048), (1024, 2048))
     own_share = lax.optimization_barrier(dot(own_hidden, logit_grad, 0, 0))
-    weight_grad = (own_share + dot(other_hidden, other_grad, 0, 0)).astype(BF16)
+    weight_grad = jnp.zeros((2048, 1024), BF16)
+    for i in range(2):
+        part = slice(i * 1024, i * 1024 + 1024)
+        half = (own_share[part] + dot(other_hidden[:, part], other_grad, 0, 0)).astype(BF16)
+        weight_grad = lax.dynamic_update_slice(weight_grad, half, (i * 1024, 0))
+        weight_grad = lax.optimization_barrier(weight_grad)
     return hidden_grad, weight_grad
 
 

time: 186 us -> 194 us (1.043)
  the two profiles are of different devices: /device:TPU:32 before, /device:TPU:36 now
where the time goes in v3:
time: 194 us; the launch traced here: 193 us
  matrix products  49.5 us (26%)
  waiting for transfers between devices  49.5 us (26%)
  starting transfers between devices  39.3 us (20%)
  local copies, waits for them, and re-layouts  25.1 us (13%)
  other arithmetic  14.9 us (8%)
  between operations  14.5 us (7%)
    dot_general x8, matrix products, dot(): lax.dot_general(a, b, (((ca,), (cb,)), ((), ())), preferred_element_type=...  49.5 us
    ppermute x19, waiting for transfers between devices, send(): return lax.ppermute(value, AXES, moves)  31.5 us
    ppermute x19, starting transfers between devices, send(): return lax.ppermute(value, AXES, moves)  27.9 us
    all_to_all x2, waiting for transfers between devices, merge(): stats = lax.all_to_all(stats, axis, 0, 0, tiled=True)  18 us
    all_to_all x2, starting transfers between devices, merge(): stats = lax.all_to_all(stats, axis, 0, 0, tiled=True)  11.4 us
    dynamic_slice x2, local copies, waits for them, and re-layouts, pick(): return lax.dynamic_index_in_dim(value, index, axis, keepdims=False)  9.91 us
    unnamed x24, local copies, waits for them, and re-layouts  8.14 us
  transfers between devices with their start and end apart: 22, of which 7 were waited for; matrix products, arithmetic and copies ran while one was open for 34% of the time, Pallas kernels for 0%

profile of v3, /device:TPU:36, one launch (start us, length us, event | category | flops | bytes accessed | tf_op | source)
XLA Modules:
  0.0 192.9 jit_solution(14564833133293946866)
XLA Ops:
  7.2 2.0 %reduce_max.46 = bf16[2048]{0:T(1024)(128)(2,1)S(1)} reduce(bf16[2048,512]{1,0:T(8,128)(2,1)} %param.6, bf16[]{:T(256)} %constant.146.clone.1), dimensions={1}, to_apply=%region_1.2 | reduce | flops 1046528 | bytes 2101250 | tf_op jit(solution)/shard_map/reduce_max | solution.py:66
  9.1 2.6 %exponential_reduce_fusion.1 = f32[2048]{0:T(1024)S(1)} fusion(bf16[2048,512]{1,0:T(8,128)(2,1)} %param.6, f32[2048]{0:T(1024)S(1)} %reduce_max.52), kind=kLoop, calls=%fused_computation.10 | loop fusion | flops 3143680 | bytes 2113536 | tf_op jit(solution)/shard_map/reduce_sum | solution.py:67
  11.8 0.6 collective-permute-start
  12.4 1.1 dynamic_slice.70
  13.4 3.1 %collective-permute-start.1 = (bf16[128,2048]{1,0:T(8,128)(2,1)S(1)}, bf16[128,2048]{1,0:T(8,128)(2,1)S(1)}, u32[]{:S(2)}, u32[]{:S(2)}) collective-permute-start(bf16[128,2048]{1,0:T(8,128)(2,1)S(1)} %dynamic_slice.70), channel_id=1, source_target_pairs={{0,1},{1,0},{2,3},{3,2},{4,5},{5,4},{6,7},{7,6},{8,9},{9,8},{10,11... | collective-permute-start | bytes 1572872 | tf_op jit(solution)/shard_map/ppermute | solution.py:34
  16.5 12.8 %fusion.39 = (f32[1024]{0:T(1024)S(1)}, f32[1024,1024]{1,0:T(8,128)S(1)}) fusion(bf16[1024,4096]{1,0:T(8,128)(2,1)} %param.4, bf16[4096,1024]{1,0:T(8,128)(2,1)} %param.5), kind=kOutput, calls=%fused_computation.83 | convolution fusion | flops 8590982144 | bytes 20975616 | tf_op jit(solution)/shard_map/dot_general | solution.py:42
  29.4 2.0 %copy-done.1 = f32[1024,1024]{1,0:T(8,128)} copy-done((f32[1024,1024]{1,0:T(8,128)}, f32[1024,1024]{1,0:T(8,128)S(1)}, u32[]{:S(2)}) %copy-start.1) | copy-done | bytes 4194328
  31.4 1.0 exponential_reduce_fusion
  32.6 0.8 broadcast_in_dim.4
  33.4 5.4 %all-to-all-start = ((f32[8,2,2,1024]{3,2,1,0:T(2,128)}), f32[8,2,2,1024]{3,2,1,0:T(2,128)S(1)}, u32[]{:S(2)}, u32[]{:S(2)}) async-start(f32[8,2,2,1024]{3,2,1,0:T(2,128)} %broadcast_in_dim.4), calls=%async_computation | async-start | bytes 262144 | tf_op jit(solution)/shard_map/all_to_all | solution.py:50
  38.8 5.1 %constant_dynamic-slice_fusion.2 = bf16[2,4,4,1,64,1024]{5,4,3,2,1,0:T(8,128)(2,1)} fusion(bf16[2,4,4,2,64,1024]{5,4,3,2,1,0:T(8,128)(2,1)} %bitcast.129, s32[]{:T(128)S(6)} %select_n.160), kind=kLoop, calls=%fused_computation.75 | loop fusion | bytes 8388612 | tf_op jit(solution)/shard_map/jit(dynamic_index_in_dim)/dynamic_slice | solution.py:38
  43.9 0.1 fusion.29
  44.0 0.2 collective-permute-start.3
  44.2 1.1 constant_dynamic-slice_fusion
  45.2 0.5 collective-permute-start.2
  45.8 0.7 broadcast_in_dim.5
  46.5 6.0 %all-to-all-start.1 = ((f32[8,2,2,1024]{3,2,1,0:T(2,128)}), f32[8,2,2,1024]{3,2,1,0:T(2,128)S(1)}, u32[]{:S(2)}, u32[]{:S(2)}) async-start(f32[8,2,2,1024]{3,2,1,0:T(2,128)} %broadcast_in_dim.5), calls=%async_computation.1 | async-start | bytes 262144 | tf_op jit(solution)/shard_map/all_to_all | solution.py:50
  52.5 4.8 %constant_dynamic-slice_fusion.1 = bf16[2,4,4,1,64,1024]{5,4,3,2,1,0:T(8,128)(2,1)} fusion(bf16[2,4,4,2,64,1024]{5,4,3,2,1,0:T(8,128)(2,1)} %bitcast.130, s32[]{:T(128)S(6)} %select_n.161), kind=kLoop, calls=%fused_computation.74 | loop fusion | bytes 8388612 | tf_op jit(solution)/shard_map/jit(dynamic_index_in_dim)/dynamic_slice | solution.py:38
  57.3 18.0 %all-to-all-done.1 = f32[8,2,2,1024]{3,2,1,0:T(2,128)S(1)} async-done(((f32[8,2,2,1024]{3,2,1,0:T(2,128)}), f32[8,2,2,1024]{3,2,1,0:T(2,128)S(1)}, u32[]{:S(2)}, u32[]{:S(2)}) %all-to-all-start.1) | async-done | bytes 131104 | tf_op jit(solution)/shard_map/all_to_all | solution.py:50
  75.4 0.1 fusion.27
  75.5 0.4 broadcast_select_fusion.1
  76.0 1.6 copy-done.2
  77.6 1.7 multiply_convert_fusion
  79.3 0.3 collective-permute-start.4
  79.7 4.3 %fusion.15 = f32[1024,1024]{1,0:T(8,128)S(1)} fusion(bf16[1024,1024]{1,0:T(8,128)(2,1)S(1)} %multiply_convert_fusion, bf16[2,1024,1024]{2,1,0:T(8,128)(2,1)} %bitcast.132), kind=kOutput, calls=%fused_computation.22 | convolution fusion | flops 2147483648 | bytes 8388608 | tf_op jit(solution)/shard_map/dot_general | solution.py:42
  84.1 2.4 %fusion.13 = f32[1024,1024]{1,0:T(8,128)S(1)} fusion(bf16[1024,1024]{1,0:T(8,128)(2,1)S(1)} %multiply_convert_fusion, bf16[2,1024,1024]{2,1,0:T(8,128)(2,1)S(1)} %bitcast.133), kind=kOutput, calls=%fused_computation.20 | convolution fusion | flops 2147483648 | bytes 8388608 | tf_op jit(solution)/shard_map/dot_general | solution.py:42
  86.5 4.6 %fusion.11 = f32[1024,1024]{1,0:T(8,128)S(1)} fusion(bf16[1024,1024]{1,0:T(8,128)(2,1)} %collective-permute-done.4, bf16[2048,1024]{1,0:T(8,128)(2,1)} %collective-permute-done.3), kind=kOutput, calls=%fused_computation.18 | convolution fusion | flops 2147483648 | bytes 8388608 | tf_op jit(solution)/shard_map/dot_general | solution.py:42
  91.1 1.1 add_convert_fusion.1
  92.3 1.1 dynamic-slice_bitcast_fusion.5
  93.3 1.0 collective-permute-start.7
  94.3 1.9 collective-permute-start.6
  96.3 1.8 collective-permute-start.5
  98.0 4.6 %fusion.9 = f32[1024,1024]{1,0:T(8,128)S(1)} fusion(bf16[1024,1024]{1,0:T(8,128)(2,1)} %collective-permute-done.4, bf16[2048,1024]{1,0:T(8,128)(2,1)} %collective-permute-done.3), kind=kOutput, calls=%fused_computation.16 | convolution fusion | flops 2147483648 | bytes 8388608 | tf_op jit(solution)/shard_map/dot_general | solution.py:42
  102.6 1.1 add_convert_fusion
  103.8 1.2 dynamic-slice_bitcast_fusion.2
  104.9 0.9 collective-permute-start.13
  105.8 1.7 collective-permute-start.12
  107.5 0.8 copy-done.8
  108.3 0.3 collective-permute-start.11
  108.6 10.9 %collective-permute-done.6 = bf16[4,64,1024]{2,1,0:T(8,128)(2,1)} collective-permute-done((bf16[4,64,1024]{2,1,0:T(8,128)(2,1)}, bf16[4,64,1024]{2,1,0:T(8,128)(2,1)}, u32[]{:S(2)}, u32[]{:S(2)}) %collective-permute-start.6) | collective-permute-done | bytes 524320 | tf_op jit(solution)/shard_map/ppermute | solution.py:34
  119.5 1.5 collective-permute-start.18
  121.1 1.9 fusion.24
  123.0 0.7 dynamic-slice_bitcast_fusion.11
  123.6 0.9 collective-permute-start.10
  124.5 1.7 collective-permute-start.9
  126.2 5.4 %collective-permute-start.8 = (bf16[64,1024]{1,0:T(8,128)(2,1)}, bf16[64,1024]{1,0:T(8,128)(2,1)S(1)}, u32[]{:S(2)}, u32[]{:S(2)}) collective-permute-start(bf16[64,1024]{1,0:T(8,128)(2,1)} %get-tuple-element.35), channel_id=1, source_target_pairs={{0,16},{1,17},{2,18},{3,19},{4,20},{5,21},{6,22},{7,23},{8,24},{9,... | collective-permute-start | bytes 393224 | tf_op jit(solution)/shard_map/ppermute | solution.py:34
  131.6 1.6 collective-permute-done.11
  133.2 1.7 fusion.23
  135.0 1.3 collective-permute-start.16
  136.3 1.9 %collective-permute-start.15 = (bf16[64,1024]{1,0:T(8,128)(2,1)S(1)}, bf16[64,1024]{1,0:T(8,128)(2,1)S(1)}, u32[]{:S(2)}, u32[]{:S(2)}) collective-permute-start(bf16[64,1024]{1,0:T(8,128)(2,1)S(1)} %get-tuple-element.34), channel_id=1, source_target_pairs={{0,8},{1,9},{2,10},{3,11},{4,12},{5,13},{6,14},{7,15},{8,0},{9,1},... | collective-permute-start | bytes 393224 | tf_op jit(solution)/shard_map/ppermute | solution.py:34
  138.3 2.5 %collective-permute-start.14 = (bf16[64,1024]{1,0:T(8,128)(2,1)S(1)}, bf16[64,1024]{1,0:T(8,128)(2,1)S(1)}, u32[]{:S(2)}, u32[]{:S(2)}) collective-permute-start(bf16[64,1024]{1,0:T(8,128)(2,1)S(1)} %get-tuple-element.32), channel_id=1, source_target_pairs={{0,4},{1,5},{2,6},{3,7},{4,8},{5,9},{6,10},{7,11},{8,12},{9,13},{1... | collective-permute-start | bytes 393224 | tf_op jit(solution)/shard_map/ppermute | solution.py:34
  140.8 1.0 collective-permute-done.16
  141.8 1.6 collective-permute-done.15
  143.4 1.6 collective-permute-done.14
  145.0 0.2 select_convert_fusion
  145.1 0.3 collective-permute-start.17
  145.5 10.7 %fusion.2 = f32[2048,1024]{1,0:T(8,128)} fusion(bf16[1024,1024]{1,0:T(8,128)(2,1)} %copy-done.6, bf16[1024,4096]{1,0:T(8,128)(2,1)} %param.4, s32[]{:T(128)S(6)} %select_n.185), kind=kOutput, calls=%fused_computation.4 | convolution fusion | flops 4294967296 | bytes 14680068 | tf_op jit(solution)/shard_map/dot_general | solution.py:42
  156.1 14.8 %collective-permute-done.17 = bf16[64,1024]{1,0:T(8,128)(2,1)S(1)} collective-permute-done((bf16[64,1024]{1,0:T(8,128)(2,1)S(1)}, bf16[64,1024]{1,0:T(8,128)(2,1)S(1)}, u32[]{:S(2)}, u32[]{:S(2)}) %collective-permute-start.17) | collective-permute-done | bytes 131104 | tf_op jit(solution)/shard_map/ppermute | solution.py:34
  170.9 0.8 fusion.25
  171.8 6.0 %fusion.1 = bf16[1024,1024]{1,0:T(8,128)(2,1)S(1)} fusion(f32[2048,1024]{1,0:T(8,128)} %fusion.2, bf16[1024,1024]{1,0:T(8,128)(2,1)} %collective-permute-done.18, bf16[1024,2048]{1,0:T(8,128)(2,1)} %all-gather.2.cloned.1.call-done), kind=kOutput, calls=%fused_computation.3 | convolution fusion | flops 2149580800 | bytes 10485760 | tf_op jit(solution)/shard_map/dot_general | solution.py:42
  177.8 0.5 dynamic_update_slice.6
  178.3 1.7 copy-done.10
  180.0 4.1 %fusion.4 = bf16[2048,1024]{1,0:T(8,128)(2,1)S(1)} fusion(bf16[2048,1024]{1,0:T(8,128)(2,1)S(1)} %dynamic_update_slice.6, f32[2048,1024]{1,0:T(8,128)S(1)} %copy-done.11, bf16[1024,1024]{1,0:T(8,128)(2,1)} %collective-permute-done.18, bf16[1024,2048]{1,0:T(8,128)(2,1)S(1)} %copy-done.10), kind=kOutput, calls=%fused_computation.11 | convolution fusion | flops 2149580800 | bytes 10485760 | tf_op jit(solution)/shard_map/dot_general | solution.py:42
  184.1 2.0 %copy-done.4 = bf16[2048,1024]{1,0:T(8,128)(2,1)} copy-done((bf16[2048,1024]{1,0:T(8,128)(2,1)}, bf16[2048,1024]{1,0:T(8,128)(2,1)S(1)}, u32[]{:S(2)}) %copy-start.4) | copy-done | bytes 4194328
  (47 shorter events, 0.3 us)
Async XLA Ops:
  11.8 20.7 %collective-permute-start = (f32[2,1024]{1,0:T(2,128)S(1)}, f32[2,1024]{1,0:T(2,128)S(1)}, u32[]{:S(2)}, u32[]{:S(2)}) collective-permute-start(f32[2,1024]{1,0:T(2,128)S(1)} %get-tuple-element.39), channel_id=1, source_target_pairs={{0,1},{1,0},{2,3},{3,2},{4,5},{5,4},{6,7},{7,6},{8,9},{9,8},{10,11... | collective-permute-start | bytes 24584 | tf_op jit(solution)/shard_map/ppermute | solution.py:34
  13.4 19.1 %collective-permute-start.1 = (bf16[128,2048]{1,0:T(8,128)(2,1)S(1)}, bf16[128,2048]{1,0:T(8,128)(2,1)S(1)}, u32[]{:S(2)}, u32[]{:S(2)}) collective-permute-start(bf16[128,2048]{1,0:T(8,128)(2,1)S(1)} %dynamic_slice.70), channel_id=1, source_target_pairs={{0,1},{1,0},{2,3},{3,2},{4,5},{5,4},{6,7},{7,6},{8,9},{9,8},{10,11... | collective-permute-start | bytes 1572872 | tf_op jit(solution)/shard_map/ppermute | solution.py:34
  29.4 2.0 %copy-start.1 = (f32[1024,1024]{1,0:T(8,128)}, f32[1024,1024]{1,0:T(8,128)S(1)}, u32[]{:S(2)}) copy-start(f32[1024,1024]{1,0:T(8,128)S(1)} %get-tuple-element.43) | copy-start | bytes 12582916
  32.5 6.3 %copy-start.7 = (bf16[128,2048]{1,0:T(8,128)(2,1)}, bf16[128,2048]{1,0:T(8,128)(2,1)S(1)}, u32[]{:S(2)}) copy-start(bf16[128,2048]{1,0:T(8,128)(2,1)S(1)} %collective-permute-done.1) | copy-start | bytes 1572868
  33.4 10.5 %all-to-all-start = ((f32[8,2,2,1024]{3,2,1,0:T(2,128)}), f32[8,2,2,1024]{3,2,1,0:T(2,128)S(1)}, u32[]{:S(2)}, u32[]{:S(2)}) async-start(f32[8,2,2,1024]{3,2,1,0:T(2,128)} %broadcast_in_dim.4), calls=%async_computation | async-start | bytes 262144 | tf_op jit(solution)/shard_map/all_to_all | solution.py:50
  38.8 133.0 %all-gather.2.cloned.1.call-start = ((), (), s32[]{:S(2)}) async-start(), calls=%async_computation.2 | async-start | bytes 4718592 | tf_op jit(solution)/shard_map/all_gather | solution.py:85
  38.8 5.4 %copy-start = (bf16[2048,512]{1,0:T(8,128)(2,1)S(1)}, bf16[2048,512]{1,0:T(8,128)(2,1)}, u32[]{:S(2)}) copy-start(bf16[2048,512]{1,0:T(8,128)(2,1)} %param.6) | copy-start | bytes 6291460
  44.0 42.5 %collective-permute-start.3 = (bf16[2048,1024]{1,0:T(8,128)(2,1)}, bf16[2048,1024]{1,0:T(8,128)(2,1)}, u32[]{:S(2)}, u32[]{:S(2)}) collective-permute-start(bf16[2048,1024]{1,0:T(8,128)(2,1)} %bitcast.131), channel_id=1, source_target_pairs={{0,2},{1,3},{2,0},{3,1},{4,6},{5,7},{6,4},{7,5},{8,10},{9,11},{10,... | collective-permute-start | bytes 12582920 | tf_op jit(solution)/shard_map/ppermute | solution.py:34
  45.2 30.2 %collective-permute-start.2 = (bf16[1024,512]{1,0:T(8,128)(2,1)}, bf16[1024,512]{1,0:T(8,128)(2,1)S(1)}, u32[]{:S(2)}, u32[]{:S(2)}) collective-permute-start(bf16[1024,512]{1,0:T(8,128)(2,1)} %constant_dynamic-slice_fusion), channel_id=1, source_target_pairs={{0,1},{1,0},{2,3},{3,2},{4,5},{5,4},{6,7},{7,6},{8,9},{9,8},{10,11... | collective-permute-start | bytes 3145736 | tf_op jit(solution)/shard_map/ppermute | solution.py:34
  46.5 28.9 %all-to-all-start.1 = ((f32[8,2,2,1024]{3,2,1,0:T(2,128)}), f32[8,2,2,1024]{3,2,1,0:T(2,128)S(1)}, u32[]{:S(2)}, u32[]{:S(2)}) async-start(f32[8,2,2,1024]{3,2,1,0:T(2,128)} %broadcast_in_dim.5), calls=%async_computation.1 | async-start | bytes 262144 | tf_op jit(solution)/shard_map/all_to_all | solution.py:50
  57.3 18.6 %copy-start.9 = (f32[1024]{0:T(1024)S(1)}, f32[1024]{0:T(1024)}, u32[]{:S(2)}) copy-start(f32[1024]{0:T(1024)} %param.7) | copy-start | bytes 12292
  75.3 2.2 %copy-start.2 = (f32[1024,1024]{1,0:T(8,128)S(1)}, f32[1024,1024]{1,0:T(8,128)}, u32[]{:S(2)}) copy-start(f32[1024,1024]{1,0:T(8,128)} %copy-done.1) | copy-start | bytes 12582916
  79.3 4.8 %copy-start.6 = (bf16[1024,1024]{1,0:T(8,128)(2,1)}, bf16[1024,1024]{1,0:T(8,128)(2,1)S(1)}, u32[]{:S(2)}) copy-start(bf16[1024,1024]{1,0:T(8,128)(2,1)S(1)} %multiply_convert_fusion) | copy-start | bytes 6291460
  79.3 7.2 %collective-permute-start.4 = (bf16[1024,1024]{1,0:T(8,128)(2,1)S(1)}, bf16[1024,1024]{1,0:T(8,128)(2,1)}, u32[]{:S(2)}, u32[]{:S(2)}) collective-permute-start(bf16[1024,1024]{1,0:T(8,128)(2,1)S(1)} %multiply_convert_fusion), channel_id=1, source_target_pairs={{0,2},{1,3},{2,0},{3,1},{4,6},{5,7},{6,4},{7,5},{8,10},{9,11},{10,... | collective-permute-start | bytes 6291464 | tf_op jit(solution)/shard_map/ppermute | solution.py:34
  79.7 4.3 %copy-start.5 = (bf16[2,4,4,1,64,1024]{5,4,3,2,1,0:T(8,128)(2,1)S(1)}, bf16[2,4,4,1,64,1024]{5,4,3,2,1,0:T(8,128)(2,1)}, u32[]{:S(2)}) copy-start(bf16[2,4,4,1,64,1024]{5,4,3,2,1,0:T(8,128)(2,1)} %constant_dynamic-slice_fusion.1) | copy-start | bytes 12582916
  92.2 10.4 %copy-start.3 = (bf16[1024,1024]{1,0:T(8,128)(2,1)}, bf16[1024,1024]{1,0:T(8,128)(2,1)S(1)}, u32[]{:S(2)}) copy-start(bf16[1024,1024]{1,0:T(8,128)(2,1)S(1)} %add_convert_fusion.1) | copy-start | bytes 6291460
  93.3 14.2 %collective-permute-start.7 = (bf16[4,64,1024]{2,1,0:T(8,128)(2,1)S(1)}, bf16[4,64,1024]{2,1,0:T(8,128)(2,1)S(1)}, u32[]{:S(2)}, u32[]{:S(2)}) collective-permute-start(bf16[4,64,1024]{2,1,0:T(8,128)(2,1)S(1)} %get-tuple-element.30), channel_id=1, source_target_pairs={{0,12},{1,13},{2,14},{3,15},{4,0},{5,1},{6,2},{7,3},{8,4},{9,5},{1... | collective-permute-start | bytes 1572872 | tf_op jit(solution)/shard_map/ppermute | solution.py:34
  94.3 25.2 %collective-permute-start.6 = (bf16[4,64,1024]{2,1,0:T(8,128)(2,1)}, bf16[4,64,1024]{2,1,0:T(8,128)(2,1)}, u32[]{:S(2)}, u32[]{:S(2)}) collective-permute-start(bf16[4,64,1024]{2,1,0:T(8,128)(2,1)} %get-tuple-element.31), channel_id=1, source_target_pairs={{0,8},{1,9},{2,10},{3,11},{4,12},{5,13},{6,14},{7,15},{8,0},{9,1},... | collective-permute-start | bytes 1572872 | tf_op jit(solution)/shard_map/ppermute | solution.py:34
  96.3 24.8 %collective-permute-start.5 = (bf16[4,64,1024]{2,1,0:T(8,128)(2,1)S(1)}, bf16[4,64,1024]{2,1,0:T(8,128)(2,1)}, u32[]{:S(2)}, u32[]{:S(2)}) collective-permute-start(bf16[4,64,1024]{2,1,0:T(8,128)(2,1)S(1)} %get-tuple-element.29), channel_id=1, source_target_pairs={{0,4},{1,5},{2,6},{3,7},{4,8},{5,9},{6,10},{7,11},{8,12},{9,13},{1... | collective-permute-start | bytes 1572872 | tf_op jit(solution)/shard_map/ppermute | solution.py:34
  104.9 19.6 %collective-permute-start.13 = (bf16[4,64,1024]{2,1,0:T(8,128)(2,1)}, bf16[4,64,1024]{2,1,0:T(8,128)(2,1)}, u32[]{:S(2)}, u32[]{:S(2)}) collective-permute-start(bf16[4,64,1024]{2,1,0:T(8,128)(2,1)} %get-tuple-element.27), channel_id=1, source_target_pairs={{0,48},{1,49},{2,50},{3,51},{4,52},{5,53},{6,54},{7,55},{8,56},{9,... | collective-permute-start | bytes 1572872 | tf_op jit(solution)/shard_map/ppermute | solution.py:34
  105.8 20.4 %collective-permute-start.12 = (bf16[4,64,1024]{2,1,0:T(8,128)(2,1)}, bf16[4,64,1024]{2,1,0:T(8,128)(2,1)}, u32[]{:S(2)}, u32[]{:S(2)}) collective-permute-start(bf16[4,64,1024]{2,1,0:T(8,128)(2,1)} %get-tuple-element.28), channel_id=1, source_target_pairs={{0,32},{1,33},{2,34},{3,35},{4,36},{5,37},{6,38},{7,39},{8,40},{9,... | collective-permute-start | bytes 1572872 | tf_op jit(solution)/shard_map/ppermute | solution.py:34
  107.5 0.8 copy-start.8
  108.3 24.9 %collective-permute-start.11 = (bf16[4,64,1024]{2,1,0:T(8,128)(2,1)S(1)}, bf16[4,64,1024]{2,1,0:T(8,128)(2,1)}, u32[]{:S(2)}, u32[]{:S(2)}) collective-permute-start(bf16[4,64,1024]{2,1,0:T(8,128)(2,1)S(1)} %get-tuple-element.26), channel_id=1, source_target_pairs={{0,16},{1,17},{2,18},{3,19},{4,20},{5,21},{6,22},{7,23},{8,24},{9,... | collective-permute-start | bytes 1572872 | tf_op jit(solution)/shard_map/ppermute | solution.py:34
  119.5 52.2 %collective-permute-start.18 = (bf16[1024,1024]{1,0:T(8,128)(2,1)}, bf16[1024,1024]{1,0:T(8,128)(2,1)}, u32[]{:S(2)}, u32[]{:S(2)}) collective-permute-start(bf16[1024,1024]{1,0:T(8,128)(2,1)} %copy-done.6), channel_id=1, source_target_pairs={{0,1},{1,0},{2,3},{3,2},{4,5},{5,4},{6,7},{7,6},{8,9},{9,8},{10,11... | collective-permute-start | bytes 6291464 | tf_op jit(solution)/shard_map/ppermute | solution.py:34
  123.6 12.7 %collective-permute-start.10 = (bf16[64,1024]{1,0:T(8,128)(2,1)S(1)}, bf16[64,1024]{1,0:T(8,128)(2,1)S(1)}, u32[]{:S(2)}, u32[]{:S(2)}) collective-permute-start(bf16[64,1024]{1,0:T(8,128)(2,1)S(1)} %get-tuple-element.36), channel_id=1, source_target_pairs={{0,48},{1,49},{2,50},{3,51},{4,52},{5,53},{6,54},{7,55},{8,56},{9,... | collective-permute-start | bytes 393224 | tf_op jit(solution)/shard_map/ppermute | solution.py:34
  124.5 13.7 %collective-permute-start.9 = (bf16[64,1024]{1,0:T(8,128)(2,1)S(1)}, bf16[64,1024]{1,0:T(8,128)(2,1)S(1)}, u32[]{:S(2)}, u32[]{:S(2)}) collective-permute-start(bf16[64,1024]{1,0:T(8,128)(2,1)S(1)} %get-tuple-element.37), channel_id=1, source_target_pairs={{0,32},{1,33},{2,34},{3,35},{4,36},{5,37},{6,38},{7,39},{8,40},{9,... | collective-permute-start | bytes 393224 | tf_op jit(solution)/shard_map/ppermute | solution.py:34
  126.2 14.6 %collective-permute-start.8 = (bf16[64,1024]{1,0:T(8,128)(2,1)}, bf16[64,1024]{1,0:T(8,128)(2,1)S(1)}, u32[]{:S(2)}, u32[]{:S(2)}) collective-permute-start(bf16[64,1024]{1,0:T(8,128)(2,1)} %get-tuple-element.35), channel_id=1, source_target_pairs={{0,16},{1,17},{2,18},{3,19},{4,20},{5,21},{6,22},{7,23},{8,24},{9,... | collective-permute-start | bytes 393224 | tf_op jit(solution)/shard_map/ppermute | solution.py:34
  135.0 6.8 %collective-permute-start.16 = (bf16[64,1024]{1,0:T(8,128)(2,1)S(1)}, bf16[64,1024]{1,0:T(8,128)(2,1)S(1)}, u32[]{:S(2)}, u32[]{:S(2)}) collective-permute-start(bf16[64,1024]{1,0:T(8,128)(2,1)S(1)} %get-tuple-element.33), channel_id=1, source_target_pairs={{0,12},{1,13},{2,14},{3,15},{4,0},{5,1},{6,2},{7,3},{8,4},{9,5},{1... | collective-permute-start | bytes 393224 | tf_op jit(solution)/shard_map/ppermute | solution.py:34
  136.3 7.1 %collective-permute-start.15 = (bf16[64,1024]{1,0:T(8,128)(2,1)S(1)}, bf16[64,1024]{1,0:T(8,128)(2,1)S(1)}, u32[]{:S(2)}, u32[]{:S(2)}) collective-permute-start(bf16[64,1024]{1,0:T(8,128)(2,1)S(1)} %get-tuple-element.34), channel_id=1, source_target_pairs={{0,8},{1,9},{2,10},{3,11},{4,12},{5,13},{6,14},{7,15},{8,0},{9,1},... | collective-permute-start | bytes 393224 | tf_op jit(solution)/shard_map/ppermute | solution.py:34
  138.3 6.7 %collective-permute-start.14 = (bf16[64,1024]{1,0:T(8,128)(2,1)S(1)}, bf16[64,1024]{1,0:T(8,128)(2,1)S(1)}, u32[]{:S(2)}, u32[]{:S(2)}) collective-permute-start(bf16[64,1024]{1,0:T(8,128)(2,1)S(1)} %get-tuple-element.32), channel_id=1, source_target_pairs={{0,4},{1,5},{2,6},{3,7},{4,8},{5,9},{6,10},{7,11},{8,12},{9,13},{1... | collective-permute-start | bytes 393224 | tf_op jit(solution)/shard_map/ppermute | solution.py:34
  145.1 25.8 %collective-permute-start.17 = (bf16[64,1024]{1,0:T(8,128)(2,1)S(1)}, bf16[64,1024]{1,0:T(8,128)(2,1)S(1)}, u32[]{:S(2)}, u32[]{:S(2)}) collective-permute-start(bf16[64,1024]{1,0:T(8,128)(2,1)S(1)} %select_convert_fusion), channel_id=1, source_target_pairs={{0,64},{1,65},{2,66},{3,67},{4,68},{5,69},{6,70},{7,71},{8,72},{9,... | collective-permute-start | bytes 393224 | tf_op jit(solution)/shard_map/ppermute | solution.py:34
  171.8 6.5 %copy-start.11 = (f32[2048,1024]{1,0:T(8,128)S(1)}, f32[2048,1024]{1,0:T(8,128)}, u32[]{:S(2)}) copy-start(f32[2048,1024]{1,0:T(8,128)} %fusion.2) | copy-start | bytes 25165828
  177.8 2.2 %copy-start.10 = (bf16[1024,2048]{1,0:T(8,128)(2,1)S(1)}, bf16[1024,2048]{1,0:T(8,128)(2,1)}, u32[]{:S(2)}) copy-start(bf16[1024,2048]{1,0:T(8,128)(2,1)} %all-gather.2.cloned.1.call-done) | copy-start | bytes 12582916
  184.1 2.0 %copy-start.4 = (bf16[2048,1024]{1,0:T(8,128)(2,1)}, bf16[2048,1024]{1,0:T(8,128)(2,1)S(1)}, u32[]{:S(2)}) copy-start(bf16[2048,1024]{1,0:T(8,128)(2,1)S(1)} %fusion.4) | copy-start | bytes 12582916
Sparse Core Ops, SparseCore 0:
  45.9 33.0 all-gather.1

commit v4 on v3

--- a/solution.py
+++ b/solution.py
@@ -93,10 +93,10 @@
     rows = head_weight.reshape(2, 4, 4, 2, 64, 1024)
     theirs = pick(rows, 1 - late_core, 3).reshape(2048, 1024)
     theirs, stats = lax.optimization_barrier((theirs, stats))
-    partner_rows = send(theirs, CORE).reshape(2, 1024, 1024)
+    partner_rows = send(theirs, CORE)
     later_core, stats, _ = lax.optimization_barrier((core, spread(stats), theirs))
     tops, totals = merge(stats, "vocab")
-    own_rows = pick(rows, later_core, 3).reshape(2, 1024, 1024)
+    own_rows = pick(rows, later_core, 3).reshape(2048, 1024)
     own_rows, tops = lax.optimization_barrier((own_rows, tops))
     student_norm, teacher_norm = tops + jnp.log(totals)
     first = jnp.where(high == 0, own_part, other_part)
@@ -110,21 +110,28 @@
     partner_grad = send(logit_grad, CORE)
     other_grad = send(logit_grad, HIGH)
 
+    tokens = (slice(0, 640), slice(640, 1024))
+
     def partial(i):
-        here = lax.optimization_barrier(dot(own_rows[i], logit_grad, 1, 1))
-        here = here + dot(partner_rows[i], partner_grad, 1, 1)
-        return here.astype(BF16).reshape(4, 4, 64, 1024)
+        here = lax.optimization_barrier(dot(own_rows, logit_grad[tokens[i]], 1, 1))
+        here = here + dot(partner_rows, partner_grad[tokens[i]], 1, 1)
+        return here.astype(BF16).reshape(2, 4, 4, 64, -1)
 
     def exchange(value, axis, place, moves):
-        arrived = [send(pick(value, (place + k) % 4, axis), moves[k]) for k in (1, 2, 3)]
-        return pick(value, place, axis).astype(F32) + sum(a.astype(F32) for a in arrived)
+        slabs = [pick(value, (place + k) % 4, axis) for k in (1, 2, 3)]
+        slabs = [slab.reshape(-1, slab.shape[-1]) for slab in slabs]
+        arrived = [send(slab, moves[k]) for k, slab in zip((1, 2, 3), slabs)]
+        own = pick(value, place, axis)
+        total = own.reshape(slabs[0].shape).astype(F32) + sum(a.astype(F32) for a in arrived)
+        return total.reshape(own.shape)
 
-    a = exchange(partial(0), 1, z, Z)
-    b = exchange(partial(1), 0, y, Y)
-    a = exchange(a.astype(BF16), 0, y, Y)
-    b = exchange(b.astype(BF16), 0, z, Z)
-    arrived = send(jnp.where(low == 0, b, a).astype(BF16), LOW)
-    hidden_grad = (jnp.where(low == 0, a, b) + arrived.astype(F32)).astype(BF16).T
+    a = exchange(partial(0), 2, z, Z)
+    b = exchange(partial(1), 1, y, Y)
+    a = exchange(a.astype(BF16), 1, y, Y)
+    b = exchange(b.astype(BF16), 1, z, Z)
+    sums = jnp.concatenate([a, b], axis=2)
+    arrived = send(jnp.where(low == 0, sums[1], sums[0]).astype(BF16), LOW)
+    hidden_grad = (jnp.where(low == 0, sums[0], sums[1]) + arrived.astype(F32)).astype(BF16).T
 
     own_hidden = lax.dynamic_slice(hidden_states, (0, high * 2048), (1024, 2048))
     own_share = lax.optimization_barrier(dot(own_hidden, logit_grad, 0, 0))

time: 194 us -> 191 us (0.985)
  the two profiles are of different devices: /device:TPU:36 before, /device:TPU:1 now
where the time goes in v4:
time: 191 us; the launch traced here: 189 us
  matrix products  51.4 us (27%)
  starting transfers between devices  48.9 us (26%)
  waiting for transfers between devices  38.5 us (20%)
  local copies, waits for them, and re-layouts  23.7 us (12%)
  between operations  14.3 us (7%)
  other arithmetic  12.2 us (6%)
    dot_general x8, matrix products, dot(): lax.dot_general(a, b, (((ca,), (cb,)), ((), ())), preferred_element_type=...  51.4 us
    ppermute x19, starting transfers between devices, send(): return lax.ppermute(value, AXES, moves)  38 us
    ppermute x19, waiting for transfers between devices, send(): return lax.ppermute(value, AXES, moves)  21.1 us
    all_to_all x2, waiting for transfers between devices, merge(): stats = lax.all_to_all(stats, axis, 0, 0, tiled=True)  17.4 us
    dynamic_slice x6, local copies, waits for them, and re-layouts, pick(): return lax.dynamic_index_in_dim(value, index, axis, keepdims=False)  12.3 us
    all_to_all x2, starting transfers between devices, merge(): stats = lax.all_to_all(stats, axis, 0, 0, tiled=True)  11 us
    unnamed x18, local copies, waits for them, and re-layouts  7.29 us
  transfers between devices with their start and end apart: 22, of which 9 were waited for; matrix products, arithmetic and copies ran while one was open for 34% of the time, Pallas kernels for 0%

profile of v4, /device:TPU:1, one launch (start us, length us, event | category | flops | bytes accessed | tf_op | source)
XLA Modules:
  0.0 189.1 jit_solution(16909430553225847745)
XLA Ops:
  7.2 2.0 %reduce_max.46 = bf16[2048]{0:T(1024)(128)(2,1)S(1)} reduce(bf16[2048,512]{1,0:T(8,128)(2,1)} %param.6, bf16[]{:T(256)} %constant.148.clone.1), dimensions={1}, to_apply=%region_1.2 | reduce | flops 1046528 | bytes 2101250 | tf_op jit(solution)/shard_map/reduce_max | solution.py:66
  9.1 2.6 %exponential_reduce_fusion.1 = f32[2048]{0:T(1024)S(1)} fusion(bf16[2048,512]{1,0:T(8,128)(2,1)} %param.6, f32[2048]{0:T(1024)S(1)} %reduce_max.52), kind=kLoop, calls=%fused_computation.9 | loop fusion | flops 3143680 | bytes 2113536 | tf_op jit(solution)/shard_map/reduce_sum | solution.py:67
  11.8 3.6 %collective-permute-start = (f32[2,1024]{1,0:T(2,128)S(1)}, f32[2,1024]{1,0:T(2,128)S(1)}, u32[]{:S(2)}, u32[]{:S(2)}) collective-permute-start(f32[2,1024]{1,0:T(2,128)S(1)} %get-tuple-element.43), channel_id=1, source_target_pairs={{0,1},{1,0},{2,3},{3,2},{4,5},{5,4},{6,7},{7,6},{8,9},{9,8},{10,11... | collective-permute-start | bytes 24584 | tf_op jit(solution)/shard_map/ppermute | solution.py:34
  15.4 1.1 dynamic_slice.71
  16.5 0.1 collective-permute-start.1
  16.6 12.8 %fusion.38 = (f32[1024]{0:T(1024)S(1)}, f32[1024,1024]{1,0:T(8,128)S(1)}) fusion(bf16[1024,4096]{1,0:T(8,128)(2,1)} %param.4, bf16[4096,1024]{1,0:T(8,128)(2,1)} %param.5), kind=kOutput, calls=%fused_computation.89 | convolution fusion | flops 8590982144 | bytes 20975616 | tf_op jit(solution)/shard_map/dot_general | solution.py:42
  29.5 2.0 %copy-done.1 = f32[1024,1024]{1,0:T(8,128)} copy-done((f32[1024,1024]{1,0:T(8,128)}, f32[1024,1024]{1,0:T(8,128)S(1)}, u32[]{:S(2)}) %copy-start.1) | copy-done | bytes 4194328
  31.5 1.0 exponential_reduce_fusion
  32.6 0.8 broadcast_in_dim.4
  33.4 6.7 %all-to-all-start = ((f32[8,2,2,1024]{3,2,1,0:T(2,128)}), f32[8,2,2,1024]{3,2,1,0:T(2,128)S(1)}, u32[]{:S(2)}, u32[]{:S(2)}) async-start(f32[8,2,2,1024]{3,2,1,0:T(2,128)} %broadcast_in_dim.4), calls=%async_computation | async-start | bytes 262144 | tf_op jit(solution)/shard_map/all_to_all | solution.py:50
  40.2 5.0 %constant_dynamic-slice_fusion.18 = bf16[2,4,4,1,64,1024]{5,4,3,2,1,0:T(8,128)(2,1)} fusion(bf16[2,4,4,2,64,1024]{5,4,3,2,1,0:T(8,128)(2,1)} %bitcast.125, s32[]{:T(128)S(6)} %select_n.165), kind=kLoop, calls=%fused_computation.81 | loop fusion | bytes 8388612 | tf_op jit(solution)/shard_map/jit(dynamic_index_in_dim)/dynamic_slice | solution.py:38
  45.2 0.2 all-to-all-done
  45.4 0.1 fusion.28
  45.5 0.9 collective-permute-start.3
  46.5 1.1 constant_dynamic-slice_fusion.16
  47.5 2.7 %collective-permute-start.2 = (bf16[1024,512]{1,0:T(8,128)(2,1)}, bf16[1024,512]{1,0:T(8,128)(2,1)S(1)}, u32[]{:S(2)}, u32[]{:S(2)}) collective-permute-start(bf16[1024,512]{1,0:T(8,128)(2,1)} %constant_dynamic-slice_fusion.16), channel_id=1, source_target_pairs={{0,1},{1,0},{2,3},{3,2},{4,5},{5,4},{6,7},{7,6},{8,9},{9,8},{10,11... | collective-permute-start | bytes 3145736 | tf_op jit(solution)/shard_map/ppermute | solution.py:34
  50.3 0.7 broadcast_in_dim.5
  51.0 4.2 %all-to-all-start.1 = ((f32[8,2,2,1024]{3,2,1,0:T(2,128)}), f32[8,2,2,1024]{3,2,1,0:T(2,128)S(1)}, u32[]{:S(2)}, u32[]{:S(2)}) async-start(f32[8,2,2,1024]{3,2,1,0:T(2,128)} %broadcast_in_dim.5), calls=%async_computation.1 | async-start | bytes 262144 | tf_op jit(solution)/shard_map/all_to_all | solution.py:50
  55.2 4.9 %constant_dynamic-slice_fusion.17 = bf16[2,4,4,1,64,1024]{5,4,3,2,1,0:T(8,128)(2,1)} fusion(bf16[2,4,4,2,64,1024]{5,4,3,2,1,0:T(8,128)(2,1)} %bitcast.126, s32[]{:T(128)S(6)} %select_n.166), kind=kLoop, calls=%fused_computation.80 | loop fusion | bytes 8388612 | tf_op jit(solution)/shard_map/jit(dynamic_index_in_dim)/dynamic_slice | solution.py:38
  60.1 17.2 %all-to-all-done.1 = f32[8,2,2,1024]{3,2,1,0:T(2,128)S(1)} async-done(((f32[8,2,2,1024]{3,2,1,0:T(2,128)}), f32[8,2,2,1024]{3,2,1,0:T(2,128)S(1)}, u32[]{:S(2)}, u32[]{:S(2)}) %all-to-all-start.1) | async-done | bytes 131104 | tf_op jit(solution)/shard_map/all_to_all | solution.py:50
  77.3 0.1 fusion.26
  77.4 0.4 broadcast_select_fusion.1
  77.9 1.6 copy-done.2
  79.4 1.7 multiply_convert_fusion
  81.2 1.8 collective-permute-start.4
  82.9 4.8 %fusion.18 = f32[2048,384]{1,0:T(8,128)S(1)} fusion(bf16[2048,1024]{1,0:T(8,128)(2,1)} %bitcast.128, bf16[1024,1024]{1,0:T(8,128)(2,1)S(1)} %multiply_convert_fusion), kind=kOutput, calls=%fused_computation.24 | convolution fusion | flops 1610612736 | bytes 8126464 | tf_op jit(solution)/shard_map/dot_general | solution.py:42
  87.7 3.6 %fusion.14 = f32[2048,640]{1,0:T(8,128)S(1)} fusion(bf16[2048,1024]{1,0:T(8,128)(2,1)S(1)} %bitcast.129, bf16[1024,1024]{1,0:T(8,128)(2,1)S(1)} %multiply_convert_fusion), kind=kOutput, calls=%fused_computation.17 | convolution fusion | flops 2684354560 | bytes 10747904 | tf_op jit(solution)/shard_map/dot_general | solution.py:42
  91.3 4.8 %add_convert_fusion.1 = bf16[2048,384]{1,0:T(8,128)(2,1)S(1)} fusion(f32[2048,384]{1,0:T(8,128)S(1)} %fusion.18, bf16[2048,1024]{1,0:T(8,128)(2,1)} %collective-permute-done.3, bf16[1024,1024]{1,0:T(8,128)(2,1)} %collective-permute-done.4), kind=kOutput, calls=%fused_computation.10 | convolution fusion | flops 1612185600 | bytes 9699328 | tf_op jit(solution)/shard_map/dot_general | solution.py:42
  96.1 0.9 constant_dynamic-slice_fusion.7
  97.1 0.6 collective-permute-start.13
  97.7 1.4 collective-permute-start.12
  99.1 6.2 %add_convert_fusion = bf16[2048,640]{1,0:T(8,128)(2,1)S(1)} fusion(f32[2048,640]{1,0:T(8,128)S(1)} %fusion.14, bf16[2048,1024]{1,0:T(8,128)(2,1)} %collective-permute-done.3, bf16[1024,1024]{1,0:T(8,128)(2,1)} %collective-permute-done.4), kind=kOutput, calls=%fused_computation | convolution fusion | flops 2686976000 | bytes 13369344 | tf_op jit(solution)/shard_map/dot_general | solution.py:42
  105.4 1.4 constant_dynamic-slice_fusion.15
  106.7 1.9 collective-permute-start.7
  108.6 0.6 collective-permute-start.6
  109.2 0.6 collective-permute-start.5
  109.8 1.7 collective-permute-start.18
  111.5 7.5 %collective-permute-done.11 = bf16[512,384]{1,0:T(8,128)(2,1)} collective-permute-done((bf16[512,384]{1,0:T(8,128)(2,1)S(1)}, bf16[512,384]{1,0:T(8,128)(2,1)}, u32[]{:S(2)}, u32[]{:S(2)}) %collective-permute-start.11) | collective-permute-done | bytes 393248 | tf_op jit(solution)/shard_map/ppermute | solution.py:34
  119.0 1.4 fusion.20
  120.4 0.1 constant_dynamic-slice_fusion.3
  120.5 2.0 %collective-permute-start.16 = (bf16[128,384]{1,0:T(8,128)(2,1)S(1)}, bf16[128,384]{1,0:T(8,128)(2,1)S(1)}, u32[]{:S(2)}, u32[]{:S(2)}) collective-permute-start(bf16[128,384]{1,0:T(8,128)(2,1)S(1)} %bitcast.145), channel_id=1, source_target_pairs={{0,12},{1,13},{2,14},{3,15},{4,0},{5,1},{6,2},{7,3},{8,4},{9,5},{1... | collective-permute-start | bytes 294920 | tf_op jit(solution)/shard_map/ppermute | solution.py:34
  122.4 0.2 collective-permute-done.7
  122.6 2.2 %collective-permute-start.15 = (bf16[128,384]{1,0:T(8,128)(2,1)S(1)}, bf16[128,384]{1,0:T(8,128)(2,1)S(1)}, u32[]{:S(2)}, u32[]{:S(2)}) collective-permute-start(bf16[128,384]{1,0:T(8,128)(2,1)S(1)} %bitcast.144), channel_id=1, source_target_pairs={{0,8},{1,9},{2,10},{3,11},{4,12},{5,13},{6,14},{7,15},{8,0},{9,1},... | collective-permute-start | bytes 294920 | tf_op jit(solution)/shard_map/ppermute | solution.py:34
  124.8 1.0 collective-permute-done.6
  125.7 12.5 %collective-permute-start.14 = (bf16[128,384]{1,0:T(8,128)(2,1)S(1)}, bf16[128,384]{1,0:T(8,128)(2,1)S(1)}, u32[]{:S(2)}, u32[]{:S(2)}) collective-permute-start(bf16[128,384]{1,0:T(8,128)(2,1)S(1)} %bitcast.143), channel_id=1, source_target_pairs={{0,4},{1,5},{2,6},{3,7},{4,8},{5,9},{6,10},{7,11},{8,12},{9,13},{1... | collective-permute-start | bytes 294920 | tf_op jit(solution)/shard_map/ppermute | solution.py:34
  138.2 3.9 %collective-permute-done.5 = bf16[512,640]{1,0:T(8,128)(2,1)} collective-permute-done((bf16[512,640]{1,0:T(8,128)(2,1)}, bf16[512,640]{1,0:T(8,128)(2,1)}, u32[]{:S(2)}, u32[]{:S(2)}) %collective-permute-start.5) | collective-permute-done | bytes 655392 | tf_op jit(solution)/shard_map/ppermute | solution.py:34
  142.2 1.8 fusion.16
  144.0 0.1 constant_dynamic-slice_fusion.11
  144.1 2.7 %collective-permute-start.10 = (bf16[128,640]{1,0:T(8,128)(2,1)S(1)}, bf16[128,640]{1,0:T(8,128)(2,1)S(1)}, u32[]{:S(2)}, u32[]{:S(2)}) collective-permute-start(bf16[128,640]{1,0:T(8,128)(2,1)S(1)} %bitcast.142), channel_id=1, source_target_pairs={{0,48},{1,49},{2,50},{3,51},{4,52},{5,53},{6,54},{7,55},{8,56},{9,... | collective-permute-start | bytes 491528 | tf_op jit(solution)/shard_map/ppermute | solution.py:34
  146.8 0.4 collective-permute-start.9
  147.3 0.8 collective-permute-start.8
  148.0 0.1 convert_add_fusion.3
  148.1 1.8 collective-permute-done.10
  149.9 3.0 %collective-permute-done.9 = bf16[128,640]{1,0:T(8,128)(2,1)S(1)} collective-permute-done((bf16[128,640]{1,0:T(8,128)(2,1)S(1)}, bf16[128,640]{1,0:T(8,128)(2,1)S(1)}, u32[]{:S(2)}, u32[]{:S(2)}) %collective-permute-start.9) | collective-permute-done | bytes 163872 | tf_op jit(solution)/shard_map/ppermute | solution.py:34
  152.9 3.7 %collective-permute-done.8 = bf16[128,640]{1,0:T(8,128)(2,1)S(1)} collective-permute-done((bf16[128,640]{1,0:T(8,128)(2,1)S(1)}, bf16[128,640]{1,0:T(8,128)(2,1)S(1)}, u32[]{:S(2)}, u32[]{:S(2)}) %collective-permute-start.8) | collective-permute-done | bytes 163872 | tf_op jit(solution)/shard_map/ppermute | solution.py:34
  156.6 0.1 convert_add_fusion.2
  156.7 1.4 collective-permute-start.17
  158.1 9.1 %fusion.2 = f32[2048,1024]{1,0:T(8,128)} fusion(bf16[1024,1024]{1,0:T(8,128)(2,1)S(1)} %multiply_convert_fusion, bf16[1024,4096]{1,0:T(8,128)(2,1)} %param.4, s32[]{:T(128)S(6)} %select_n.191), kind=kOutput, calls=%fused_computation.5 | convolution fusion | flops 4294967296 | bytes 14680068 | tf_op jit(solution)/shard_map/dot_general | solution.py:42
  167.2 0.7 fusion.24
  167.9 6.0 %fusion.1 = bf16[1024,1024]{1,0:T(8,128)(2,1)S(1)} fusion(f32[2048,1024]{1,0:T(8,128)} %fusion.2, bf16[1024,1024]{1,0:T(8,128)(2,1)} %collective-permute-done.18, bf16[1024,2048]{1,0:T(8,128)(2,1)} %all-gather.2.cloned.1.call-done), kind=kOutput, calls=%fused_computation.4 | convolution fusion | flops 2149580800 | bytes 10485760 | tf_op jit(solution)/shard_map/dot_general | solution.py:42
  173.9 0.5 dynamic_update_slice.6
  174.4 1.7 copy-done.7
  176.1 4.1 %fusion.4 = bf16[2048,1024]{1,0:T(8,128)(2,1)S(1)} fusion(bf16[2048,1024]{1,0:T(8,128)(2,1)S(1)} %dynamic_update_slice.6, f32[2048,1024]{1,0:T(8,128)S(1)} %copy-done.8, bf16[1024,1024]{1,0:T(8,128)(2,1)} %collective-permute-done.18, bf16[1024,2048]{1,0:T(8,128)(2,1)S(1)} %copy-done.7), kind=kOutput, calls=%fused_computation.11 | convolution fusion | flops 2149580800 | bytes 10485760 | tf_op jit(solution)/shard_map/dot_general | solution.py:42
  180.2 2.0 %copy-done.3 = bf16[2048,1024]{1,0:T(8,128)(2,1)} copy-done((bf16[2048,1024]{1,0:T(8,128)(2,1)}, bf16[2048,1024]{1,0:T(8,128)(2,1)S(1)}, u32[]{:S(2)}) %copy-start.3) | copy-done | bytes 4194328
  (41 shorter events, 0.3 us)
Async XLA Ops:
  11.8 20.7 %collective-permute-start = (f32[2,1024]{1,0:T(2,128)S(1)}, f32[2,1024]{1,0:T(2,128)S(1)}, u32[]{:S(2)}, u32[]{:S(2)}) collective-permute-start(f32[2,1024]{1,0:T(2,128)S(1)} %get-tuple-element.43), channel_id=1, source_target_pairs={{0,1},{1,0},{2,3},{3,2},{4,5},{5,4},{6,7},{7,6},{8,9},{9,8},{10,11... | collective-permute-start | bytes 24584 | tf_op jit(solution)/shard_map/ppermute | solution.py:34
  16.5 16.1 %collective-permute-start.1 = (bf16[128,2048]{1,0:T(8,128)(2,1)S(1)}, bf16[128,2048]{1,0:T(8,128)(2,1)S(1)}, u32[]{:S(2)}, u32[]{:S(2)}) collective-permute-start(bf16[128,2048]{1,0:T(8,128)(2,1)S(1)} %dynamic_slice.71), channel_id=1, source_target_pairs={{0,1},{1,0},{2,3},{3,2},{4,5},{5,4},{6,7},{7,6},{8,9},{9,8},{10,11... | collective-permute-start | bytes 1572872 | tf_op jit(solution)/shard_map/ppermute | solution.py:34
  29.5 2.0 %copy-start.1 = (f32[1024,1024]{1,0:T(8,128)}, f32[1024,1024]{1,0:T(8,128)S(1)}, u32[]{:S(2)}) copy-start(f32[1024,1024]{1,0:T(8,128)S(1)} %get-tuple-element.47) | copy-start | bytes 12582916
  32.6 7.6 %copy-start.5 = (bf16[128,2048]{1,0:T(8,128)(2,1)}, bf16[128,2048]{1,0:T(8,128)(2,1)S(1)}, u32[]{:S(2)}) copy-start(bf16[128,2048]{1,0:T(8,128)(2,1)S(1)} %collective-permute-done.1) | copy-start | bytes 1572868
  33.4 12.0 %all-to-all-start = ((f32[8,2,2,1024]{3,2,1,0:T(2,128)}), f32[8,2,2,1024]{3,2,1,0:T(2,128)S(1)}, u32[]{:S(2)}, u32[]{:S(2)}) async-start(f32[8,2,2,1024]{3,2,1,0:T(2,128)} %broadcast_in_dim.4), calls=%async_computation | async-start | bytes 262144 | tf_op jit(solution)/shard_map/all_to_all | solution.py:50
  40.1 127.7 %all-gather.2.cloned.1.call-start = ((), (), s32[]{:S(2)}) async-start(), calls=%async_computation.2 | async-start | bytes 4718592 | tf_op jit(solution)/shard_map/all_gather | solution.py:85
  40.2 6.3 %copy-start = (bf16[2048,512]{1,0:T(8,128)(2,1)S(1)}, bf16[2048,512]{1,0:T(8,128)(2,1)}, u32[]{:S(2)}) copy-start(bf16[2048,512]{1,0:T(8,128)(2,1)} %param.6) | copy-start | bytes 6291460
  45.5 45.8 %collective-permute-start.3 = (bf16[2048,1024]{1,0:T(8,128)(2,1)}, bf16[2048,1024]{1,0:T(8,128)(2,1)}, u32[]{:S(2)}, u32[]{:S(2)}) collective-permute-start(bf16[2048,1024]{1,0:T(8,128)(2,1)} %bitcast.127), channel_id=1, source_target_pairs={{0,2},{1,3},{2,0},{3,1},{4,6},{5,7},{6,4},{7,5},{8,10},{9,11},{10,... | collective-permute-start | bytes 12582920 | tf_op jit(solution)/shard_map/ppermute | solution.py:34
  47.5 29.9 %collective-permute-start.2 = (bf16[1024,512]{1,0:T(8,128)(2,1)}, bf16[1024,512]{1,0:T(8,128)(2,1)S(1)}, u32[]{:S(2)}, u32[]{:S(2)}) collective-permute-start(bf16[1024,512]{1,0:T(8,128)(2,1)} %constant_dynamic-slice_fusion.16), channel_id=1, source_target_pairs={{0,1},{1,0},{2,3},{3,2},{4,5},{5,4},{6,7},{7,6},{8,9},{9,8},{10,11... | collective-permute-start | bytes 3145736 | tf_op jit(solution)/shard_map/ppermute | solution.py:34
  51.0 26.3 %all-to-all-start.1 = ((f32[8,2,2,1024]{3,2,1,0:T(2,128)}), f32[8,2,2,1024]{3,2,1,0:T(2,128)S(1)}, u32[]{:S(2)}, u32[]{:S(2)}) async-start(f32[8,2,2,1024]{3,2,1,0:T(2,128)} %broadcast_in_dim.5), calls=%async_computation.1 | async-start | bytes 262144 | tf_op jit(solution)/shard_map/all_to_all | solution.py:50
  60.1 17.8 %copy-start.6 = (f32[1024]{0:T(1024)S(1)}, f32[1024]{0:T(1024)}, u32[]{:S(2)}) copy-start(f32[1024]{0:T(1024)} %param.7) | copy-start | bytes 12292
  77.3 2.2 %copy-start.2 = (f32[1024,1024]{1,0:T(8,128)S(1)}, f32[1024,1024]{1,0:T(8,128)}, u32[]{:S(2)}) copy-start(f32[1024,1024]{1,0:T(8,128)} %copy-done.1) | copy-start | bytes 12582916
  81.2 10.1 %collective-permute-start.4 = (bf16[1024,1024]{1,0:T(8,128)(2,1)S(1)}, bf16[1024,1024]{1,0:T(8,128)(2,1)}, u32[]{:S(2)}, u32[]{:S(2)}) collective-permute-start(bf16[1024,1024]{1,0:T(8,128)(2,1)S(1)} %multiply_convert_fusion), channel_id=1, source_target_pairs={{0,2},{1,3},{2,0},{3,1},{4,6},{5,7},{6,4},{7,5},{8,10},{9,11},{10,... | collective-permute-start | bytes 6291464 | tf_op jit(solution)/shard_map/ppermute | solution.py:34
  82.9 4.8 %copy-start.4 = (bf16[2,4,4,1,64,1024]{5,4,3,2,1,0:T(8,128)(2,1)S(1)}, bf16[2,4,4,1,64,1024]{5,4,3,2,1,0:T(8,128)(2,1)}, u32[]{:S(2)}) copy-start(bf16[2,4,4,1,64,1024]{5,4,3,2,1,0:T(8,128)(2,1)} %constant_dynamic-slice_fusion.17) | copy-start | bytes 12582916
  97.1 12.1 %collective-permute-start.13 = (bf16[512,384]{1,0:T(8,128)(2,1)S(1)}, bf16[512,384]{1,0:T(8,128)(2,1)}, u32[]{:S(2)}, u32[]{:S(2)}) collective-permute-start(bf16[512,384]{1,0:T(8,128)(2,1)S(1)} %bitcast.139), channel_id=1, source_target_pairs={{0,48},{1,49},{2,50},{3,51},{4,52},{5,53},{6,54},{7,55},{8,56},{9,... | collective-permute-start | bytes 1179656 | tf_op jit(solution)/shard_map/ppermute | solution.py:34
  97.7 12.1 %collective-permute-start.12 = (bf16[512,384]{1,0:T(8,128)(2,1)}, bf16[512,384]{1,0:T(8,128)(2,1)}, u32[]{:S(2)}, u32[]{:S(2)}) collective-permute-start(bf16[512,384]{1,0:T(8,128)(2,1)} %bitcast.34), channel_id=1, source_target_pairs={{0,32},{1,33},{2,34},{3,35},{4,36},{5,37},{6,38},{7,39},{8,40},{9,... | collective-permute-start | bytes 1179656 | tf_op jit(solution)/shard_map/ppermute | solution.py:34
  99.1 19.9 %collective-permute-start.11 = (bf16[512,384]{1,0:T(8,128)(2,1)S(1)}, bf16[512,384]{1,0:T(8,128)(2,1)}, u32[]{:S(2)}, u32[]{:S(2)}) collective-permute-start(bf16[512,384]{1,0:T(8,128)(2,1)S(1)} %bitcast.138), channel_id=1, source_target_pairs={{0,16},{1,17},{2,18},{3,19},{4,20},{5,21},{6,22},{7,23},{8,24},{9,... | collective-permute-start | bytes 1179656 | tf_op jit(solution)/shard_map/ppermute | solution.py:34
  106.7 15.9 %collective-permute-start.7 = (bf16[512,640]{1,0:T(8,128)(2,1)}, bf16[512,640]{1,0:T(8,128)(2,1)}, u32[]{:S(2)}, u32[]{:S(2)}) collective-permute-start(bf16[512,640]{1,0:T(8,128)(2,1)} %bitcast.24), channel_id=1, source_target_pairs={{0,12},{1,13},{2,14},{3,15},{4,0},{5,1},{6,2},{7,3},{8,4},{9,5},{1... | collective-permute-start | bytes 1966088 | tf_op jit(solution)/shard_map/ppermute | solution.py:34
  108.6 17.1 %collective-permute-start.6 = (bf16[512,640]{1,0:T(8,128)(2,1)}, bf16[512,640]{1,0:T(8,128)(2,1)}, u32[]{:S(2)}, u32[]{:S(2)}) collective-permute-start(bf16[512,640]{1,0:T(8,128)(2,1)} %bitcast.23), channel_id=1, source_target_pairs={{0,8},{1,9},{2,10},{3,11},{4,12},{5,13},{6,14},{7,15},{8,0},{9,1},... | collective-permute-start | bytes 1966088 | tf_op jit(solution)/shard_map/ppermute | solution.py:34
  109.2 33.0 %collective-permute-start.5 = (bf16[512,640]{1,0:T(8,128)(2,1)}, bf16[512,640]{1,0:T(8,128)(2,1)}, u32[]{:S(2)}, u32[]{:S(2)}) collective-permute-start(bf16[512,640]{1,0:T(8,128)(2,1)} %bitcast.22), channel_id=1, source_target_pairs={{0,4},{1,5},{2,6},{3,7},{4,8},{5,9},{6,10},{7,11},{8,12},{9,13},{1... | collective-permute-start | bytes 1966088 | tf_op jit(solution)/shard_map/ppermute | solution.py:34
  109.8 58.1 %collective-permute-start.18 = (bf16[1024,1024]{1,0:T(8,128)(2,1)S(1)}, bf16[1024,1024]{1,0:T(8,128)(2,1)}, u32[]{:S(2)}, u32[]{:S(2)}) collective-permute-start(bf16[1024,1024]{1,0:T(8,128)(2,1)S(1)} %multiply_convert_fusion), channel_id=1, source_target_pairs={{0,1},{1,0},{2,3},{3,2},{4,5},{5,4},{6,7},{7,6},{8,9},{9,8},{10,11... | collective-permute-start | bytes 6291464 | tf_op jit(solution)/shard_map/ppermute | solution.py:34
  120.5 26.3 %collective-permute-start.16 = (bf16[128,384]{1,0:T(8,128)(2,1)S(1)}, bf16[128,384]{1,0:T(8,128)(2,1)S(1)}, u32[]{:S(2)}, u32[]{:S(2)}) collective-permute-start(bf16[128,384]{1,0:T(8,128)(2,1)S(1)} %bitcast.145), channel_id=1, source_target_pairs={{0,12},{1,13},{2,14},{3,15},{4,0},{5,1},{6,2},{7,3},{8,4},{9,5},{1... | collective-permute-start | bytes 294920 | tf_op jit(solution)/shard_map/ppermute | solution.py:34
  122.6 24.7 %collective-permute-start.15 = (bf16[128,384]{1,0:T(8,128)(2,1)S(1)}, bf16[128,384]{1,0:T(8,128)(2,1)S(1)}, u32[]{:S(2)}, u32[]{:S(2)}) collective-permute-start(bf16[128,384]{1,0:T(8,128)(2,1)S(1)} %bitcast.144), channel_id=1, source_target_pairs={{0,8},{1,9},{2,10},{3,11},{4,12},{5,13},{6,14},{7,15},{8,0},{9,1},... | collective-permute-start | bytes 294920 | tf_op jit(solution)/shard_map/ppermute | solution.py:34
  125.7 22.3 %collective-permute-start.14 = (bf16[128,384]{1,0:T(8,128)(2,1)S(1)}, bf16[128,384]{1,0:T(8,128)(2,1)S(1)}, u32[]{:S(2)}, u32[]{:S(2)}) collective-permute-start(bf16[128,384]{1,0:T(8,128)(2,1)S(1)} %bitcast.143), channel_id=1, source_target_pairs={{0,4},{1,5},{2,6},{3,7},{4,8},{5,9},{6,10},{7,11},{8,12},{9,13},{1... | collective-permute-start | bytes 294920 | tf_op jit(solution)/shard_map/ppermute | solution.py:34
  144.1 5.9 %collective-permute-start.10 = (bf16[128,640]{1,0:T(8,128)(2,1)S(1)}, bf16[128,640]{1,0:T(8,128)(2,1)S(1)}, u32[]{:S(2)}, u32[]{:S(2)}) collective-permute-start(bf16[128,640]{1,0:T(8,128)(2,1)S(1)} %bitcast.142), channel_id=1, source_target_pairs={{0,48},{1,49},{2,50},{3,51},{4,52},{5,53},{6,54},{7,55},{8,56},{9,... | collective-permute-start | bytes 491528 | tf_op jit(solution)/shard_map/ppermute | solution.py:34
  146.8 6.1 %collective-permute-start.9 = (bf16[128,640]{1,0:T(8,128)(2,1)S(1)}, bf16[128,640]{1,0:T(8,128)(2,1)S(1)}, u32[]{:S(2)}, u32[]{:S(2)}) collective-permute-start(bf16[128,640]{1,0:T(8,128)(2,1)S(1)} %bitcast.141), channel_id=1, source_target_pairs={{0,32},{1,33},{2,34},{3,35},{4,36},{5,37},{6,38},{7,39},{8,40},{9,... | collective-permute-start | bytes 491528 | tf_op jit(solution)/shard_map/ppermute | solution.py:34
  147.3 9.3 %collective-permute-start.8 = (bf16[128,640]{1,0:T(8,128)(2,1)S(1)}, bf16[128,640]{1,0:T(8,128)(2,1)S(1)}, u32[]{:S(2)}, u32[]{:S(2)}) collective-permute-start(bf16[128,640]{1,0:T(8,128)(2,1)S(1)} %bitcast.140), channel_id=1, source_target_pairs={{0,16},{1,17},{2,18},{3,19},{4,20},{5,21},{6,22},{7,23},{8,24},{9,... | collective-permute-start | bytes 491528 | tf_op jit(solution)/shard_map/ppermute | solution.py:34
  156.7 10.5 %collective-permute-start.17 = (bf16[64,1024]{1,0:T(8,128)(2,1)S(1)}, bf16[64,1024]{1,0:T(8,128)(2,1)S(1)}, u32[]{:S(2)}, u32[]{:S(2)}) collective-permute-start(bf16[64,1024]{1,0:T(8,128)(2,1)S(1)} %fusion.23), channel_id=1, source_target_pairs={{0,64},{1,65},{2,66},{3,67},{4,68},{5,69},{6,70},{7,71},{8,72},{9,... | collective-permute-start | bytes 393224 | tf_op jit(solution)/shard_map/ppermute | solution.py:34
  167.9 6.5 %copy-start.8 = (f32[2048,1024]{1,0:T(8,128)S(1)}, f32[2048,1024]{1,0:T(8,128)}, u32[]{:S(2)}) copy-start(f32[2048,1024]{1,0:T(8,128)} %fusion.2) | copy-start | bytes 25165828
  173.9 2.2 %copy-start.7 = (bf16[1024,2048]{1,0:T(8,128)(2,1)S(1)}, bf16[1024,2048]{1,0:T(8,128)(2,1)}, u32[]{:S(2)}) copy-start(bf16[1024,2048]{1,0:T(8,128)(2,1)} %all-gather.2.cloned.1.call-done) | copy-start | bytes 12582916
  180.2 2.0 %copy-start.3 = (bf16[2048,1024]{1,0:T(8,128)(2,1)}, bf16[2048,1024]{1,0:T(8,128)(2,1)S(1)}, u32[]{:S(2)}) copy-start(bf16[2048,1024]{1,0:T(8,128)(2,1)S(1)} %fusion.4) | copy-start | bytes 12582916
Sparse Core Ops, SparseCore 0:
  50.4 31.2 all-gather.1

commit v5 on v4

--- a/solution.py
+++ b/solution.py
@@ -1,6 +1,7 @@
 import jax
 import jax.numpy as jnp
 from jax import lax
+from jax.experimental import pallas as pl
 from jax.experimental.layout import Layout, with_layout_constraint
 from jax.sharding import PartitionSpec as P
 
@@ -53,6 +54,27 @@
     return best, jnp.sum(totals * jnp.exp(tops - best), axis=0)
 
 
+def stats_kernel(x_ref, out_ref):
+    x = x_ref[...].astype(F32)
+    top = jnp.max(x, axis=1, keepdims=True)
+    total = jnp.sum(jnp.exp(x - top), axis=1, keepdims=True)
+    lane = lax.broadcasted_iota(jnp.int32, (x.shape[0], 128), 1)
+    out_ref[...] = jnp.where(lane == 0, top, total).T[:8]
+
+
+def shard_stats(shard):
+    tokens, columns = shard.shape
+    out = pl.pallas_call(
+        stats_kernel,
+        grid=(4,),
+        in_specs=[pl.BlockSpec((tokens // 4, columns), lambda i: (i, 0))],
+        out_specs=pl.BlockSpec((8, tokens // 4), lambda i: (0, i)),
+        out_shape=jax.ShapeDtypeStruct((8, tokens), F32),
+        cost_estimate=pl.CostEstimate(flops=4 * tokens * columns, bytes_accessed=2 * tokens * columns, transcendentals=tokens * columns),
+    )(shard)
+    return out[:2]
+
+
 def row_major(value):
     return with_layout_constraint(value, Layout(major_to_minor=(0, 1)))
 
@@ -62,10 +84,8 @@
     low, y = vocab // 4, vocab % 4
     z, core = dp // 2, dp % 2
 
-    shard = teacher_logits.astype(F32)
-    top = jnp.max(shard, axis=1)
-    total = jnp.sum(jnp.exp(shard - top[:, None]), axis=1)
-    stats = jnp.stack([top.reshape(2, 1024), total.reshape(2, 1024)], axis=1)
+    stats = shard_stats(teacher_logits)
+    stats = stats.reshape(2, 2, 1024).swapaxes(0, 1)
     theirs = send(jnp.where(high == 0, stats[1], stats[0]), HIGH)
     mine = jnp.where(high == 0, stats[0], stats[1])
     teacher_top = jnp.maximum(mine[0], theirs[0])

time: 191 us -> 191 us (level)
  other arithmetic: 12.2 us -> 7.61 us
  Pallas kernels: 0 us -> 4.08 us
    pallas_call x0 -> x1, Pallas kernels: none -> 4.08 us  [shard_stats(): pl.pallas_call(stats_kernel, grid=(4,), in_specs=[pl.BlockSpec((tokens //...]
    reduce_sum x1 -> x0, other arithmetic: 2.6 us -> none  [compute(): total = jnp.sum(jnp.exp(shard - top[:, None]), axis=1)]
    reduce_max x2 -> x0, other arithmetic: 1.98 us -> none  [compute(): top = jnp.max(shard, axis=1)]
    unnamed x18 -> x19, local copies, waits for them, and re-layouts: 7.29 us -> 7.32 us
where the time goes in v5:
time: 191 us; the launch traced here: 190 us
  matrix products  51.4 us (27%)
  starting transfers between devices  48.9 us (26%)
  waiting for transfers between devices  38.5 us (20%)
  local copies, waits for them, and re-layouts  24.6 us (13%)
  between operations  14.3 us (7%)
  other arithmetic  7.61 us (4%)
  Pallas kernels  4.08 us (2%)
    dot_general x8, matrix products, dot(): lax.dot_general(a, b, (((ca,), (cb,)), ((), ())), preferred_element_type=...  51.4 us
    ppermute x19, starting transfers between devices, send(): return lax.ppermute(value, AXES, moves)  38 us
    ppermute x19, waiting for transfers between devices, send(): return lax.ppermute(value, AXES, moves)  21.1 us
    all_to_all x2, waiting for transfers between devices, merge(): stats = lax.all_to_all(stats, axis, 0, 0, tiled=True)  17.4 us
    dynamic_slice x6, local copies, waits for them, and re-layouts, pick(): return lax.dynamic_index_in_dim(value, index, axis, keepdims=False)  12.4 us
    all_to_all x2, starting transfers between devices, merge(): stats = lax.all_to_all(stats, axis, 0, 0, tiled=True)  11 us
    unnamed x19, local copies, waits for them, and re-layouts  7.32 us
    pallas_call x1, Pallas kernels, shard_stats(): pl.pallas_call(stats_kernel, grid=(4,), in_specs=[pl.BlockSpec((tokens //...  4.08 us
  transfers between devices with their start and end apart: 22, of which 9 were waited for; matrix products, arithmetic and copies ran while one was open for 34% of the time, Pallas kernels for 0%

profile of v5, /device:TPU:1, one launch (start us, length us, event | category | flops | bytes accessed | tf_op | source)
XLA Modules:
  0.0 189.5 jit_solution(10031911463567034716)
XLA Ops:
  7.2 4.1 %shard_map.59 = f32[8,2048]{1,0:T(8,128)} custom-call(bf16[2048,512]{1,0:T(8,128)(2,1)} %x_ref.1), custom_call_target="tpu_custom_call" | custom-call | flops 4194304 | bytes 2097152 | tf_op jit(solution)/shard_map/pallas_call | solution.py:67
  11.3 0.8 slice.98
  12.2 3.6 %collective-permute-start = (f32[2,1024]{1,0:T(2,128)S(1)}, f32[2,1024]{1,0:T(2,128)S(1)}, u32[]{:S(2)}, u32[]{:S(2)}) collective-permute-start(f32[2,1024]{1,0:T(2,128)S(1)} %bitcast.153), channel_id=1, source_target_pairs={{0,1},{1,0},{2,3},{3,2},{4,5},{5,4},{6,7},{7,6},{8,9},{9,8},{10,11... | collective-permute-start | bytes 24584 | tf_op jit(solution)/shard_map/ppermute | solution.py:35
  15.8 1.1 dynamic_slice.71
  16.9 0.1 collective-permute-start.1
  17.0 12.9 %fusion.37 = (f32[1024]{0:T(1024)S(1)}, f32[1024,1024]{1,0:T(8,128)S(1)}) fusion(bf16[1024,4096]{1,0:T(8,128)(2,1)} %param.4, bf16[4096,1024]{1,0:T(8,128)(2,1)} %param.5), kind=kOutput, calls=%fused_computation.85 | convolution fusion | flops 8590982144 | bytes 20975616 | tf_op jit(solution)/shard_map/dot_general | solution.py:43
  29.9 2.0 %copy-done = f32[1024,1024]{1,0:T(8,128)} copy-done((f32[1024,1024]{1,0:T(8,128)}, f32[1024,1024]{1,0:T(8,128)S(1)}, u32[]{:S(2)}) %copy-start) | copy-done | bytes 4194328
  31.9 1.0 exponential_reduce_fusion
  33.0 0.8 broadcast_in_dim.4
  33.8 6.7 %all-to-all-start = ((f32[8,2,2,1024]{3,2,1,0:T(2,128)}), f32[8,2,2,1024]{3,2,1,0:T(2,128)S(1)}, u32[]{:S(2)}, u32[]{:S(2)}) async-start(f32[8,2,2,1024]{3,2,1,0:T(2,128)} %broadcast_in_dim.4), calls=%async_computation | async-start | bytes 262144 | tf_op jit(solution)/shard_map/all_to_all | solution.py:51
  40.6 5.0 %constant_dynamic-slice_fusion.18 = bf16[2,4,4,1,64,1024]{5,4,3,2,1,0:T(8,128)(2,1)} fusion(bf16[2,4,4,2,64,1024]{5,4,3,2,1,0:T(8,128)(2,1)} %bitcast.125, s32[]{:T(128)S(6)} %select_n.165), kind=kLoop, calls=%fused_computation.77 | loop fusion | bytes 8388612 | tf_op jit(solution)/shard_map/jit(dynamic_index_in_dim)/dynamic_slice | solution.py:39
  45.6 0.2 all-to-all-done
  45.8 0.1 fusion.28
  45.9 0.9 collective-permute-start.3
  46.9 1.1 constant_dynamic-slice_fusion.16
  47.9 2.7 %collective-permute-start.2 = (bf16[1024,512]{1,0:T(8,128)(2,1)}, bf16[1024,512]{1,0:T(8,128)(2,1)S(1)}, u32[]{:S(2)}, u32[]{:S(2)}) collective-permute-start(bf16[1024,512]{1,0:T(8,128)(2,1)} %constant_dynamic-slice_fusion.16), channel_id=1, source_target_pairs={{0,1},{1,0},{2,3},{3,2},{4,5},{5,4},{6,7},{7,6},{8,9},{9,8},{10,11... | collective-permute-start | bytes 3145736 | tf_op jit(solution)/shard_map/ppermute | solution.py:35
  50.7 0.7 broadcast_in_dim.5
  51.4 4.2 %all-to-all-start.1 = ((f32[8,2,2,1024]{3,2,1,0:T(2,128)}), f32[8,2,2,1024]{3,2,1,0:T(2,128)S(1)}, u32[]{:S(2)}, u32[]{:S(2)}) async-start(f32[8,2,2,1024]{3,2,1,0:T(2,128)} %broadcast_in_dim.5), calls=%async_computation.1 | async-start | bytes 262144 | tf_op jit(solution)/shard_map/all_to_all | solution.py:51
  55.6 4.9 %constant_dynamic-slice_fusion.17 = bf16[2,4,4,1,64,1024]{5,4,3,2,1,0:T(8,128)(2,1)} fusion(bf16[2,4,4,2,64,1024]{5,4,3,2,1,0:T(8,128)(2,1)} %bitcast.126, s32[]{:T(128)S(6)} %select_n.166), kind=kLoop, calls=%fused_computation.76 | loop fusion | bytes 8388612 | tf_op jit(solution)/shard_map/jit(dynamic_index_in_dim)/dynamic_slice | solution.py:39
  60.5 17.2 %all-to-all-done.1 = f32[8,2,2,1024]{3,2,1,0:T(2,128)S(1)} async-done(((f32[8,2,2,1024]{3,2,1,0:T(2,128)}), f32[8,2,2,1024]{3,2,1,0:T(2,128)S(1)}, u32[]{:S(2)}, u32[]{:S(2)}) %all-to-all-start.1) | async-done | bytes 131104 | tf_op jit(solution)/shard_map/all_to_all | solution.py:51
  77.7 0.1 fusion.26
  77.8 0.4 broadcast_select_fusion.1
  78.3 1.6 copy-done.1
  79.9 1.7 multiply_convert_fusion
  81.6 1.8 collective-permute-start.4
  83.4 4.8 %fusion.18 = f32[2048,384]{1,0:T(8,128)S(1)} fusion(bf16[2048,1024]{1,0:T(8,128)(2,1)} %bitcast.128, bf16[1024,1024]{1,0:T(8,128)(2,1)S(1)} %multiply_convert_fusion), kind=kOutput, calls=%fused_computation.23 | convolution fusion | flops 1610612736 | bytes 8126464 | tf_op jit(solution)/shard_map/dot_general | solution.py:43
  88.1 3.6 %fusion.14 = f32[2048,640]{1,0:T(8,128)S(1)} fusion(bf16[2048,1024]{1,0:T(8,128)(2,1)S(1)} %bitcast.129, bf16[1024,1024]{1,0:T(8,128)(2,1)S(1)} %multiply_convert_fusion), kind=kOutput, calls=%fused_computation.16 | convolution fusion | flops 2684354560 | bytes 10747904 | tf_op jit(solution)/shard_map/dot_general | solution.py:43
  91.7 4.8 %add_convert_fusion.1 = bf16[2048,384]{1,0:T(8,128)(2,1)S(1)} fusion(f32[2048,384]{1,0:T(8,128)S(1)} %fusion.18, bf16[2048,1024]{1,0:T(8,128)(2,1)} %collective-permute-done.3, bf16[1024,1024]{1,0:T(8,128)(2,1)} %collective-permute-done.4), kind=kOutput, calls=%fused_computation.9 | convolution fusion | flops 1612185600 | bytes 9699328 | tf_op jit(solution)/shard_map/dot_general | solution.py:43
  96.6 0.9 constant_dynamic-slice_fusion.7
  97.5 0.6 collective-permute-start.13
  98.2 1.4 collective-permute-start.12
  99.6 6.2 %add_convert_fusion = bf16[2048,640]{1,0:T(8,128)(2,1)S(1)} fusion(f32[2048,640]{1,0:T(8,128)S(1)} %fusion.14, bf16[2048,1024]{1,0:T(8,128)(2,1)} %collective-permute-done.3, bf16[1024,1024]{1,0:T(8,128)(2,1)} %collective-permute-done.4), kind=kOutput, calls=%fused_computation | convolution fusion | flops 2686976000 | bytes 13369344 | tf_op jit(solution)/shard_map/dot_general | solution.py:43
  105.8 1.4 constant_dynamic-slice_fusion.15
  107.2 1.9 collective-permute-start.7
  109.1 0.6 collective-permute-start.6
  109.7 0.6 collective-permute-start.5
  110.2 1.7 collective-permute-start.18
  112.0 7.5 %collective-permute-done.11 = bf16[512,384]{1,0:T(8,128)(2,1)} collective-permute-done((bf16[512,384]{1,0:T(8,128)(2,1)S(1)}, bf16[512,384]{1,0:T(8,128)(2,1)}, u32[]{:S(2)}, u32[]{:S(2)}) %collective-permute-start.11) | collective-permute-done | bytes 393248 | tf_op jit(solution)/shard_map/ppermute | solution.py:35
  119.4 1.4 fusion.20
  120.9 0.1 constant_dynamic-slice_fusion.3
  120.9 2.0 %collective-permute-start.16 = (bf16[128,384]{1,0:T(8,128)(2,1)S(1)}, bf16[128,384]{1,0:T(8,128)(2,1)S(1)}, u32[]{:S(2)}, u32[]{:S(2)}) collective-permute-start(bf16[128,384]{1,0:T(8,128)(2,1)S(1)} %bitcast.145), channel_id=1, source_target_pairs={{0,12},{1,13},{2,14},{3,15},{4,0},{5,1},{6,2},{7,3},{8,4},{9,5},{1... | collective-permute-start | bytes 294920 | tf_op jit(solution)/shard_map/ppermute | solution.py:35
  122.9 0.2 collective-permute-done.7
  123.1 2.2 %collective-permute-start.15 = (bf16[128,384]{1,0:T(8,128)(2,1)S(1)}, bf16[128,384]{1,0:T(8,128)(2,1)S(1)}, u32[]{:S(2)}, u32[]{:S(2)}) collective-permute-start(bf16[128,384]{1,0:T(8,128)(2,1)S(1)} %bitcast.144), channel_id=1, source_target_pairs={{0,8},{1,9},{2,10},{3,11},{4,12},{5,13},{6,14},{7,15},{8,0},{9,1},... | collective-permute-start | bytes 294920 | tf_op jit(solution)/shard_map/ppermute | solution.py:35
  125.2 1.0 collective-permute-done.6
  126.2 12.5 %collective-permute-start.14 = (bf16[128,384]{1,0:T(8,128)(2,1)S(1)}, bf16[128,384]{1,0:T(8,128)(2,1)S(1)}, u32[]{:S(2)}, u32[]{:S(2)}) collective-permute-start(bf16[128,384]{1,0:T(8,128)(2,1)S(1)} %bitcast.143), channel_id=1, source_target_pairs={{0,4},{1,5},{2,6},{3,7},{4,8},{5,9},{6,10},{7,11},{8,12},{9,13},{1... | collective-permute-start | bytes 294920 | tf_op jit(solution)/shard_map/ppermute | solution.py:35
  138.7 3.9 %collective-permute-done.5 = bf16[512,640]{1,0:T(8,128)(2,1)} collective-permute-done((bf16[512,640]{1,0:T(8,128)(2,1)}, bf16[512,640]{1,0:T(8,128)(2,1)}, u32[]{:S(2)}, u32[]{:S(2)}) %collective-permute-start.5) | collective-permute-done | bytes 655392 | tf_op jit(solution)/shard_map/ppermute | solution.py:35
  142.6 1.8 fusion.16
  144.5 0.1 constant_dynamic-slice_fusion.11
  144.5 2.7 %collective-permute-start.10 = (bf16[128,640]{1,0:T(8,128)(2,1)S(1)}, bf16[128,640]{1,0:T(8,128)(2,1)S(1)}, u32[]{:S(2)}, u32[]{:S(2)}) collective-permute-start(bf16[128,640]{1,0:T(8,128)(2,1)S(1)} %bitcast.142), channel_id=1, source_target_pairs={{0,48},{1,49},{2,50},{3,51},{4,52},{5,53},{6,54},{7,55},{8,56},{9,... | collective-permute-start | bytes 491528 | tf_op jit(solution)/shard_map/ppermute | solution.py:35
  147.3 0.5 collective-permute-start.9
  147.7 0.8 collective-permute-start.8
  148.5 0.1 convert_add_fusion.3
  148.6 1.8 collective-permute-done.10
  150.4 3.0 %collective-permute-done.9 = bf16[128,640]{1,0:T(8,128)(2,1)S(1)} collective-permute-done((bf16[128,640]{1,0:T(8,128)(2,1)S(1)}, bf16[128,640]{1,0:T(8,128)(2,1)S(1)}, u32[]{:S(2)}, u32[]{:S(2)}) %collective-permute-start.9) | collective-permute-done | bytes 163872 | tf_op jit(solution)/shard_map/ppermute | solution.py:35
  153.4 3.7 %collective-permute-done.8 = bf16[128,640]{1,0:T(8,128)(2,1)S(1)} collective-permute-done((bf16[128,640]{1,0:T(8,128)(2,1)S(1)}, bf16[128,640]{1,0:T(8,128)(2,1)S(1)}, u32[]{:S(2)}, u32[]{:S(2)}) %collective-permute-start.8) | collective-permute-done | bytes 163872 | tf_op jit(solution)/shard_map/ppermute | solution.py:35
  157.1 0.1 convert_add_fusion.2
  157.2 1.4 collective-permute-start.17
  158.6 9.1 %fusion.2 = f32[2048,1024]{1,0:T(8,128)} fusion(bf16[1024,1024]{1,0:T(8,128)(2,1)S(1)} %multiply_convert_fusion, bf16[1024,4096]{1,0:T(8,128)(2,1)} %param.4, s32[]{:T(128)S(6)} %select_n.191), kind=kOutput, calls=%fused_computation.5 | convolution fusion | flops 4294967296 | bytes 14680068 | tf_op jit(solution)/shard_map/dot_general | solution.py:43
  167.7 0.7 fusion.24
  168.4 6.0 %fusion.1 = bf16[1024,1024]{1,0:T(8,128)(2,1)S(1)} fusion(f32[2048,1024]{1,0:T(8,128)} %fusion.2, bf16[1024,1024]{1,0:T(8,128)(2,1)} %collective-permute-done.18, bf16[1024,2048]{1,0:T(8,128)(2,1)} %all-gather.2.cloned.1.call-done), kind=kOutput, calls=%fused_computation.4 | convolution fusion | flops 2149580800 | bytes 10485760 | tf_op jit(solution)/shard_map/dot_general | solution.py:43
  174.4 0.5 dynamic_update_slice.6
  174.8 1.7 copy-done.7
  176.5 4.1 %fusion.4 = bf16[2048,1024]{1,0:T(8,128)(2,1)S(1)} fusion(bf16[2048,1024]{1,0:T(8,128)(2,1)S(1)} %dynamic_update_slice.6, f32[2048,1024]{1,0:T(8,128)S(1)} %copy-done.8, bf16[1024,1024]{1,0:T(8,128)(2,1)} %collective-permute-done.18, bf16[1024,2048]{1,0:T(8,128)(2,1)S(1)} %copy-done.7), kind=kOutput, calls=%fused_computation.10 | convolution fusion | flops 2149580800 | bytes 10485760 | tf_op jit(solution)/shard_map/dot_general | solution.py:43
  180.7 2.0 %copy-done.3 = bf16[2048,1024]{1,0:T(8,128)(2,1)} copy-done((bf16[2048,1024]{1,0:T(8,128)(2,1)}, bf16[2048,1024]{1,0:T(8,128)(2,1)S(1)}, u32[]{:S(2)}) %copy-start.3) | copy-done | bytes 4194328
  (42 shorter events, 0.3 us)
Async XLA Ops:
  12.2 20.8 %collective-permute-start = (f32[2,1024]{1,0:T(2,128)S(1)}, f32[2,1024]{1,0:T(2,128)S(1)}, u32[]{:S(2)}, u32[]{:S(2)}) collective-permute-start(f32[2,1024]{1,0:T(2,128)S(1)} %bitcast.153), channel_id=1, source_target_pairs={{0,1},{1,0},{2,3},{3,2},{4,5},{5,4},{6,7},{7,6},{8,9},{9,8},{10,11... | collective-permute-start | bytes 24584 | tf_op jit(solution)/shard_map/ppermute | solution.py:35
  16.9 16.1 %collective-permute-start.1 = (bf16[128,2048]{1,0:T(8,128)(2,1)S(1)}, bf16[128,2048]{1,0:T(8,128)(2,1)S(1)}, u32[]{:S(2)}, u32[]{:S(2)}) collective-permute-start(bf16[128,2048]{1,0:T(8,128)(2,1)S(1)} %dynamic_slice.71), channel_id=1, source_target_pairs={{0,1},{1,0},{2,3},{3,2},{4,5},{5,4},{6,7},{7,6},{8,9},{9,8},{10,11... | collective-permute-start | bytes 1572872 | tf_op jit(solution)/shard_map/ppermute | solution.py:35
  29.9 2.0 %copy-start = (f32[1024,1024]{1,0:T(8,128)}, f32[1024,1024]{1,0:T(8,128)S(1)}, u32[]{:S(2)}) copy-start(f32[1024,1024]{1,0:T(8,128)S(1)} %get-tuple-element.47) | copy-start | bytes 12582916
  33.0 7.6 %copy-start.5 = (bf16[128,2048]{1,0:T(8,128)(2,1)}, bf16[128,2048]{1,0:T(8,128)(2,1)S(1)}, u32[]{:S(2)}) copy-start(bf16[128,2048]{1,0:T(8,128)(2,1)S(1)} %collective-permute-done.1) | copy-start | bytes 1572868
  33.8 12.0 %all-to-all-start = ((f32[8,2,2,1024]{3,2,1,0:T(2,128)}), f32[8,2,2,1024]{3,2,1,0:T(2,128)S(1)}, u32[]{:S(2)}, u32[]{:S(2)}) async-start(f32[8,2,2,1024]{3,2,1,0:T(2,128)} %broadcast_in_dim.4), calls=%async_computation | async-start | bytes 262144 | tf_op jit(solution)/shard_map/all_to_all | solution.py:51
  40.6 127.8 %all-gather.2.cloned.1.call-start = ((), (), s32[]{:S(2)}) async-start(), calls=%async_computation.2 | async-start | bytes 4718592 | tf_op jit(solution)/shard_map/all_gather | solution.py:105
  40.6 6.3 %copy-start.2 = (bf16[2048,512]{1,0:T(8,128)(2,1)S(1)}, bf16[2048,512]{1,0:T(8,128)(2,1)}, u32[]{:S(2)}) copy-start(bf16[2048,512]{1,0:T(8,128)(2,1)} %x_ref.1) | copy-start | bytes 6291460
  45.9 45.8 %collective-permute-start.3 = (bf16[2048,1024]{1,0:T(8,128)(2,1)}, bf16[2048,1024]{1,0:T(8,128)(2,1)}, u32[]{:S(2)}, u32[]{:S(2)}) collective-permute-start(bf16[2048,1024]{1,0:T(8,128)(2,1)} %bitcast.127), channel_id=1, source_target_pairs={{0,2},{1,3},{2,0},{3,1},{4,6},{5,7},{6,4},{7,5},{8,10},{9,11},{10,... | collective-permute-start | bytes 12582920 | tf_op jit(solution)/shard_map/ppermute | solution.py:35
  47.9 29.9 %collective-permute-start.2 = (bf16[1024,512]{1,0:T(8,128)(2,1)}, bf16[1024,512]{1,0:T(8,128)(2,1)S(1)}, u32[]{:S(2)}, u32[]{:S(2)}) collective-permute-start(bf16[1024,512]{1,0:T(8,128)(2,1)} %constant_dynamic-slice_fusion.16), channel_id=1, source_target_pairs={{0,1},{1,0},{2,3},{3,2},{4,5},{5,4},{6,7},{7,6},{8,9},{9,8},{10,11... | collective-permute-start | bytes 3145736 | tf_op jit(solution)/shard_map/ppermute | solution.py:35
  51.4 26.3 %all-to-all-start.1 = ((f32[8,2,2,1024]{3,2,1,0:T(2,128)}), f32[8,2,2,1024]{3,2,1,0:T(2,128)S(1)}, u32[]{:S(2)}, u32[]{:S(2)}) async-start(f32[8,2,2,1024]{3,2,1,0:T(2,128)} %broadcast_in_dim.5), calls=%async_computation.1 | async-start | bytes 262144 | tf_op jit(solution)/shard_map/all_to_all | solution.py:51
  60.5 17.8 %copy-start.6 = (f32[1024]{0:T(1024)S(1)}, f32[1024]{0:T(1024)}, u32[]{:S(2)}) copy-start(f32[1024]{0:T(1024)} %param.7) | copy-start | bytes 12292
  77.7 2.2 %copy-start.1 = (f32[1024,1024]{1,0:T(8,128)S(1)}, f32[1024,1024]{1,0:T(8,128)}, u32[]{:S(2)}) copy-start(f32[1024,1024]{1,0:T(8,128)} %copy-done) | copy-start | bytes 12582916
  81.6 10.1 %collective-permute-start.4 = (bf16[1024,1024]{1,0:T(8,128)(2,1)S(1)}, bf16[1024,1024]{1,0:T(8,128)(2,1)}, u32[]{:S(2)}, u32[]{:S(2)}) collective-permute-start(bf16[1024,1024]{1,0:T(8,128)(2,1)S(1)} %multiply_convert_fusion), channel_id=1, source_target_pairs={{0,2},{1,3},{2,0},{3,1},{4,6},{5,7},{6,4},{7,5},{8,10},{9,11},{10,... | collective-permute-start | bytes 6291464 | tf_op jit(solution)/shard_map/ppermute | solution.py:35
  83.4 4.8 %copy-start.4 = (bf16[2,4,4,1,64,1024]{5,4,3,2,1,0:T(8,128)(2,1)S(1)}, bf16[2,4,4,1,64,1024]{5,4,3,2,1,0:T(8,128)(2,1)}, u32[]{:S(2)}) copy-start(bf16[2,4,4,1,64,1024]{5,4,3,2,1,0:T(8,128)(2,1)} %constant_dynamic-slice_fusion.17) | copy-start | bytes 12582916
  97.5 12.1 %collective-permute-start.13 = (bf16[512,384]{1,0:T(8,128)(2,1)S(1)}, bf16[512,384]{1,0:T(8,128)(2,1)}, u32[]{:S(2)}, u32[]{:S(2)}) collective-permute-start(bf16[512,384]{1,0:T(8,128)(2,1)S(1)} %bitcast.139), channel_id=1, source_target_pairs={{0,48},{1,49},{2,50},{3,51},{4,52},{5,53},{6,54},{7,55},{8,56},{9,... | collective-permute-start | bytes 1179656 | tf_op jit(solution)/shard_map/ppermute | solution.py:35
  98.2 12.1 %collective-permute-start.12 = (bf16[512,384]{1,0:T(8,128)(2,1)}, bf16[512,384]{1,0:T(8,128)(2,1)}, u32[]{:S(2)}, u32[]{:S(2)}) collective-permute-start(bf16[512,384]{1,0:T(8,128)(2,1)} %bitcast.32), channel_id=1, source_target_pairs={{0,32},{1,33},{2,34},{3,35},{4,36},{5,37},{6,38},{7,39},{8,40},{9,... | collective-permute-start | bytes 1179656 | tf_op jit(solution)/shard_map/ppermute | solution.py:35
  99.6 19.9 %collective-permute-start.11 = (bf16[512,384]{1,0:T(8,128)(2,1)S(1)}, bf16[512,384]{1,0:T(8,128)(2,1)}, u32[]{:S(2)}, u32[]{:S(2)}) collective-permute-start(bf16[512,384]{1,0:T(8,128)(2,1)S(1)} %bitcast.138), channel_id=1, source_target_pairs={{0,16},{1,17},{2,18},{3,19},{4,20},{5,21},{6,22},{7,23},{8,24},{9,... | collective-permute-start | bytes 1179656 | tf_op jit(solution)/shard_map/ppermute | solution.py:35
  107.2 15.9 %collective-permute-start.7 = (bf16[512,640]{1,0:T(8,128)(2,1)}, bf16[512,640]{1,0:T(8,128)(2,1)}, u32[]{:S(2)}, u32[]{:S(2)}) collective-permute-start(bf16[512,640]{1,0:T(8,128)(2,1)} %bitcast.22), channel_id=1, source_target_pairs={{0,12},{1,13},{2,14},{3,15},{4,0},{5,1},{6,2},{7,3},{8,4},{9,5},{1... | collective-permute-start | bytes 1966088 | tf_op jit(solution)/shard_map/ppermute | solution.py:35
  109.1 17.1 %collective-permute-start.6 = (bf16[512,640]{1,0:T(8,128)(2,1)}, bf16[512,640]{1,0:T(8,128)(2,1)}, u32[]{:S(2)}, u32[]{:S(2)}) collective-permute-start(bf16[512,640]{1,0:T(8,128)(2,1)} %bitcast.21), channel_id=1, source_target_pairs={{0,8},{1,9},{2,10},{3,11},{4,12},{5,13},{6,14},{7,15},{8,0},{9,1},... | collective-permute-start | bytes 1966088 | tf_op jit(solution)/shard_map/ppermute | solution.py:35
  109.7 33.0 %collective-permute-start.5 = (bf16[512,640]{1,0:T(8,128)(2,1)}, bf16[512,640]{1,0:T(8,128)(2,1)}, u32[]{:S(2)}, u32[]{:S(2)}) collective-permute-start(bf16[512,640]{1,0:T(8,128)(2,1)} %bitcast.20), channel_id=1, source_target_pairs={{0,4},{1,5},{2,6},{3,7},{4,8},{5,9},{6,10},{7,11},{8,12},{9,13},{1... | collective-permute-start | bytes 1966088 | tf_op jit(solution)/shard_map/ppermute | solution.py:35
  110.2 58.1 %collective-permute-start.18 = (bf16[1024,1024]{1,0:T(8,128)(2,1)S(1)}, bf16[1024,1024]{1,0:T(8,128)(2,1)}, u32[]{:S(2)}, u32[]{:S(2)}) collective-permute-start(bf16[1024,1024]{1,0:T(8,128)(2,1)S(1)} %multiply_convert_fusion), channel_id=1, source_target_pairs={{0,1},{1,0},{2,3},{3,2},{4,5},{5,4},{6,7},{7,6},{8,9},{9,8},{10,11... | collective-permute-start | bytes 6291464 | tf_op jit(solution)/shard_map/ppermute | solution.py:35
  120.9 26.3 %collective-permute-start.16 = (bf16[128,384]{1,0:T(8,128)(2,1)S(1)}, bf16[128,384]{1,0:T(8,128)(2,1)S(1)}, u32[]{:S(2)}, u32[]{:S(2)}) collective-permute-start(bf16[128,384]{1,0:T(8,128)(2,1)S(1)} %bitcast.145), channel_id=1, source_target_pairs={{0,12},{1,13},{2,14},{3,15},{4,0},{5,1},{6,2},{7,3},{8,4},{9,5},{1... | collective-permute-start | bytes 294920 | tf_op jit(solution)/shard_map/ppermute | solution.py:35
  123.1 24.7 %collective-permute-start.15 = (bf16[128,384]{1,0:T(8,128)(2,1)S(1)}, bf16[128,384]{1,0:T(8,128)(2,1)S(1)}, u32[]{:S(2)}, u32[]{:S(2)}) collective-permute-start(bf16[128,384]{1,0:T(8,128)(2,1)S(1)} %bitcast.144), channel_id=1, source_target_pairs={{0,8},{1,9},{2,10},{3,11},{4,12},{5,13},{6,14},{7,15},{8,0},{9,1},... | collective-permute-start | bytes 294920 | tf_op jit(solution)/shard_map/ppermute | solution.py:35
  126.2 22.3 %collective-permute-start.14 = (bf16[128,384]{1,0:T(8,128)(2,1)S(1)}, bf16[128,384]{1,0:T(8,128)(2,1)S(1)}, u32[]{:S(2)}, u32[]{:S(2)}) collective-permute-start(bf16[128,384]{1,0:T(8,128)(2,1)S(1)} %bitcast.143), channel_id=1, source_target_pairs={{0,4},{1,5},{2,6},{3,7},{4,8},{5,9},{6,10},{7,11},{8,12},{9,13},{1... | collective-permute-start | bytes 294920 | tf_op jit(solution)/shard_map/ppermute | solution.py:35
  144.5 5.8 %collective-permute-start.10 = (bf16[128,640]{1,0:T(8,128)(2,1)S(1)}, bf16[128,640]{1,0:T(8,128)(2,1)S(1)}, u32[]{:S(2)}, u32[]{:S(2)}) collective-permute-start(bf16[128,640]{1,0:T(8,128)(2,1)S(1)} %bitcast.142), channel_id=1, source_target_pairs={{0,48},{1,49},{2,50},{3,51},{4,52},{5,53},{6,54},{7,55},{8,56},{9,... | collective-permute-start | bytes 491528 | tf_op jit(solution)/shard_map/ppermute | solution.py:35
  147.3 6.1 %collective-permute-start.9 = (bf16[128,640]{1,0:T(8,128)(2,1)S(1)}, bf16[128,640]{1,0:T(8,128)(2,1)S(1)}, u32[]{:S(2)}, u32[]{:S(2)}) collective-permute-start(bf16[128,640]{1,0:T(8,128)(2,1)S(1)} %bitcast.141), channel_id=1, source_target_pairs={{0,32},{1,33},{2,34},{3,35},{4,36},{5,37},{6,38},{7,39},{8,40},{9,... | collective-permute-start | bytes 491528 | tf_op jit(solution)/shard_map/ppermute | solution.py:35
  147.7 9.3 %collective-permute-start.8 = (bf16[128,640]{1,0:T(8,128)(2,1)S(1)}, bf16[128,640]{1,0:T(8,128)(2,1)S(1)}, u32[]{:S(2)}, u32[]{:S(2)}) collective-permute-start(bf16[128,640]{1,0:T(8,128)(2,1)S(1)} %bitcast.140), channel_id=1, source_target_pairs={{0,16},{1,17},{2,18},{3,19},{4,20},{5,21},{6,22},{7,23},{8,24},{9,... | collective-permute-start | bytes 491528 | tf_op jit(solution)/shard_map/ppermute | solution.py:35
  157.2 10.5 %collective-permute-start.17 = (bf16[64,1024]{1,0:T(8,128)(2,1)S(1)}, bf16[64,1024]{1,0:T(8,128)(2,1)S(1)}, u32[]{:S(2)}, u32[]{:S(2)}) collective-permute-start(bf16[64,1024]{1,0:T(8,128)(2,1)S(1)} %fusion.23), channel_id=1, source_target_pairs={{0,64},{1,65},{2,66},{3,67},{4,68},{5,69},{6,70},{7,71},{8,72},{9,... | collective-permute-start | bytes 393224 | tf_op jit(solution)/shard_map/ppermute | solution.py:35
  168.4 6.5 %copy-start.8 = (f32[2048,1024]{1,0:T(8,128)S(1)}, f32[2048,1024]{1,0:T(8,128)}, u32[]{:S(2)}) copy-start(f32[2048,1024]{1,0:T(8,128)} %fusion.2) | copy-start | bytes 25165828
  174.4 2.2 %copy-start.7 = (bf16[1024,2048]{1,0:T(8,128)(2,1)S(1)}, bf16[1024,2048]{1,0:T(8,128)(2,1)}, u32[]{:S(2)}) copy-start(bf16[1024,2048]{1,0:T(8,128)(2,1)} %all-gather.2.cloned.1.call-done) | copy-start | bytes 12582916
  180.7 2.0 %copy-start.3 = (bf16[2048,1024]{1,0:T(8,128)(2,1)}, bf16[2048,1024]{1,0:T(8,128)(2,1)S(1)}, u32[]{:S(2)}) copy-start(bf16[2048,1024]{1,0:T(8,128)(2,1)S(1)} %fusion.4) | copy-start | bytes 12582916
Sparse Core Ops, SparseCore 0:
  50.8 31.3 all-gather.1

commit v6 on v4

--- a/solution.py
+++ b/solution.py
@@ -1,6 +1,8 @@
 import jax
 import jax.numpy as jnp
 from jax import lax
+from jax.experimental import pallas as pl
+from jax.experimental.pallas import tpu as pltpu
 from jax.experimental.layout import Layout, with_layout_constraint
 from jax.sharding import PartitionSpec as P
 
@@ -53,6 +55,54 @@
     return best, jnp.sum(totals * jnp.exp(tops - best), axis=0)
 
 
+def stats_kernel(high_ref, x_ref, theirs_ref, mine_ref, part_ref):
+    raw = x_ref[...]
+    x = raw.astype(F32)
+    top = jnp.max(x, axis=1, keepdims=True)
+    total = jnp.sum(jnp.exp(x - top), axis=1, keepdims=True)
+    lane = lax.broadcasted_iota(jnp.int32, (x.shape[0], 128), 1)
+    stats = jnp.where(lane == 0, top, total).T[:8]
+    step = pl.program_id(0)
+
+    @pl.when(step < 2)
+    def _():
+        theirs_ref[...] = stats
+        part_ref[...] = raw
+
+    @pl.when(step >= 2)
+    def _():
+        mine_ref[...] = stats
+
+
+def shard_stats(high, shard):
+    first = lambda i, high_ref: (0, jnp.minimum(i, 1))
+    last = lambda i, high_ref: (0, jnp.maximum(i - 2, 0))
+    return pl.pallas_call(
+        stats_kernel,
+        grid_spec=pltpu.PrefetchScalarGridSpec(
+            num_scalar_prefetch=1,
+            grid=(4,),
+            in_specs=[
+                pl.BlockSpec(
+                    (512, 512),
+                    lambda i, high_ref: (jnp.where(i < 2, 2 - 2 * high_ref[0] + i, 2 * high_ref[0] + i - 2), 0),
+                )
+            ],
+            out_specs=[
+                pl.BlockSpec((8, 512), first),
+                pl.BlockSpec((8, 512), last),
+                pl.BlockSpec((512, 512), lambda i, high_ref: (jnp.minimum(i, 1), 0)),
+            ],
+        ),
+        out_shape=[
+            jax.ShapeDtypeStruct((8, 1024), F32),
+            jax.ShapeDtypeStruct((8, 1024), F32),
+            jax.ShapeDtypeStruct((1024, 512), BF16),
+        ],
+        cost_estimate=pl.CostEstimate(flops=4194304, bytes_accessed=3145728, transcendentals=1048576),
+    )(high.astype(jnp.int32).reshape(1), shard)
+
+
 def row_major(value):
     return with_layout_constraint(value, Layout(major_to_minor=(0, 1)))
 
@@ -62,19 +112,14 @@
     low, y = vocab // 4, vocab % 4
     z, core = dp // 2, dp % 2
 
-    shard = teacher_logits.astype(F32)
-    top = jnp.max(shard, axis=1)
-    total = jnp.sum(jnp.exp(shard - top[:, None]), axis=1)
-    stats = jnp.stack([top.reshape(2, 1024), total.reshape(2, 1024)], axis=1)
-    theirs = send(jnp.where(high == 0, stats[1], stats[0]), HIGH)
-    mine = jnp.where(high == 0, stats[0], stats[1])
+    other_stats, mine, part = shard_stats(high, teacher_logits)
+    theirs = send(other_stats, HIGH)
     teacher_top = jnp.maximum(mine[0], theirs[0])
     teacher_total = mine[1] * jnp.exp(mine[0] - teacher_top) + theirs[1] * jnp.exp(theirs[0] - teacher_top)
 
     piece = lax.dynamic_slice(hidden_states, (dp * 128, (1 - high) * 2048), (128, 2048))
     piece = send(piece, HIGH)
 
-    part = row_major(lax.dynamic_slice(teacher_logits, ((1 - high) * 1024, 0), (1024, 512)))
     other_part = row_major(send(part, HIGH))
     own_part = lax.dynamic_slice(teacher_logits, (high * 1024, 0), (1024, 512))
 
@@ -108,7 +153,9 @@
         * (jnp.exp(logits - student_norm[:, None]) - jnp.exp(teacher - teacher_norm[:, None]))
     ).astype(BF16)
     partner_grad = send(logit_grad, CORE)
-    other_grad = send(logit_grad, HIGH)
+    other_grad = []
+    for i in range(2):
+        other_grad.append(send(logit_grad[:, i * 512 : i * 512 + 512], HIGH))
 
     tokens = (slice(0, 640), slice(640, 1024))
 
@@ -137,9 +184,8 @@
     own_share = lax.optimization_barrier(dot(own_hidden, logit_grad, 0, 0))
     weight_grad = jnp.zeros((2048, 1024), BF16)
     for i in range(2):
-        part = slice(i * 1024, i * 1024 + 1024)
-        half = (own_share[part] + dot(other_hidden[:, part], other_grad, 0, 0)).astype(BF16)
-        weight_grad = lax.dynamic_update_slice(weight_grad, half, (i * 1024, 0))
+        half = own_share[:, i * 512 : i * 512 + 512] + dot(other_hidden, other_grad[i], 0, 0)
+        weight_grad = lax.dynamic_update_slice(weight_grad, half.astype(BF16), (0, i * 512))
         weight_grad = lax.optimization_barrier(weight_grad)
     return hidden_grad, weight_grad
 

time: 191 us -> 187 us (0.979)
  waiting for transfers between devices: 38.5 us -> 51.7 us
  starting transfers between devices: 48.9 us -> 38.1 us
  other arithmetic: 12.2 us -> 5.83 us
  Pallas kernels: 0 us -> 4.51 us
  local copies, waits for them, and re-layouts: 23.7 us -> 20.9 us
  matrix products: 51.4 us -> 49.3 us
    ppermute x19 -> x20, waiting for transfers between devices: 21.1 us -> 34.4 us  [send(): return lax.ppermute(value, AXES, moves)]
    ppermute x19 -> x20, starting transfers between devices: 38 us -> 27.1 us  [send(): return lax.ppermute(value, AXES, moves)]
    pallas_call x0 -> x1, Pallas kernels: none -> 4.51 us  [shard_stats(): pl.pallas_call(stats_kernel, grid_spec=pltpu.PrefetchScalarGridSpec(num_s...]
    reduce_sum x1 -> x0, other arithmetic: 2.6 us -> none  [compute(): total = jnp.sum(jnp.exp(shard - top[:, None]), axis=1)]
    dot_general x8, matrix products: 51.4 us -> 49.3 us  [dot(): lax.dot_general(a, b, (((ca,), (cb,)), ((), ())), preferred_element_type=...]
    reduce_max x2 -> x0, other arithmetic: 1.98 us -> none  [compute(): top = jnp.max(shard, axis=1)]
    unnamed x18 -> x22, local copies, waits for them, and re-layouts: 7.29 us -> 7.2 us
  transfers between devices with their start and end apart: 22 -> 23, of which waited for: 9 -> 9; matrix products, arithmetic and copies ran while one was open for 34% -> 35% of each run, Pallas kernels for 0% -> 0%
where the time goes in v6:
time: 187 us; the launch traced here: 185 us
  waiting for transfers between devices  51.7 us (28%)
  matrix products  49.3 us (26%)
  starting transfers between devices  38.1 us (20%)
  local copies, waits for them, and re-layouts  20.9 us (11%)
  between operations  14.4 us (8%)
  other arithmetic  5.83 us (3%)
  Pallas kernels  4.51 us (2%)
    dot_general x8, matrix products, dot(): lax.dot_general(a, b, (((ca,), (cb,)), ((), ())), preferred_element_type=...  49.3 us
    ppermute x20, waiting for transfers between devices, send(): return lax.ppermute(value, AXES, moves)  34.4 us
    ppermute x20, starting transfers between devices, send(): return lax.ppermute(value, AXES, moves)  27.1 us
    all_to_all x2, waiting for transfers between devices, merge(): stats = lax.all_to_all(stats, axis, 0, 0, tiled=True)  17.3 us
    all_to_all x2, starting transfers between devices, merge(): stats = lax.all_to_all(stats, axis, 0, 0, tiled=True)  11 us
    dynamic_slice x6, local copies, waits for them, and re-layouts, pick(): return lax.dynamic_index_in_dim(value, index, axis, keepdims=False)  10.5 us
    unnamed x22, local copies, waits for them, and re-layouts  7.2 us
    pallas_call x1, Pallas kernels, shard_stats(): pl.pallas_call(stats_kernel, grid_spec=pltpu.PrefetchScalarGridSpec(num_s...  4.51 us
  transfers between devices with their start and end apart: 23, of which 9 were waited for; matrix products, arithmetic and copies ran while one was open for 35% of the time, Pallas kernels for 0%

profile of v6, /device:TPU:1, one launch (start us, length us, event | category | flops | bytes accessed | tf_op | source)
XLA Modules:
  0.0 184.7 jit_solution(9109097061857635946)
XLA Ops:
  7.2 4.5 %shard_map.59 = (f32[8,1024]{1,0:T(8,128)}, f32[8,1024]{1,0:T(8,128)}, bf16[1024,512]{1,0:T(8,128)(2,1)}) custom-call(s32[1]{0:T(128)} %bitcast.2.high_ref, bf16[2048,512]{1,0:T(8,128)(2,1)} %x_ref.1), custom_call_target="tpu_custom_call" | custom-call | flops 4194304 | bytes 3145728 | tf_op jit(solution)/shard_map/pallas_call | solution.py:80
  11.7 3.6 %collective-permute-start = (f32[8,1024]{1,0:T(8,128)}, f32[8,1024]{1,0:T(8,128)S(1)}, u32[]{:S(2)}, u32[]{:S(2)}) collective-permute-start(f32[8,1024]{1,0:T(8,128)} %get-tuple-element.16), channel_id=1, source_target_pairs={{0,1},{1,0},{2,3},{3,2},{4,5},{5,4},{6,7},{7,6},{8,9},{9,8},{10,11... | collective-permute-start | bytes 98312 | tf_op jit(solution)/shard_map/ppermute | solution.py:36
  15.2 1.1 dynamic_slice.68
  16.3 0.1 collective-permute-start.1
  16.4 12.9 %fusion.27 = (f32[1024]{0:T(1024)S(1)}, f32[1024,1024]{1,0:T(8,128)S(1)}) fusion(bf16[1024,4096]{1,0:T(8,128)(2,1)} %param.4, bf16[4096,1024]{1,0:T(8,128)(2,1)} %param.5), kind=kOutput, calls=%fused_computation.75 | convolution fusion | flops 8590982144 | bytes 20975616 | tf_op jit(solution)/shard_map/dot_general | solution.py:44
  29.3 1.9 %copy-done = f32[1024,1024]{1,0:T(8,128)} copy-done((f32[1024,1024]{1,0:T(8,128)}, f32[1024,1024]{1,0:T(8,128)S(1)}, u32[]{:S(2)}) %copy-start) | copy-done | bytes 4194328
  31.2 1.0 exponential_reduce_fusion
  32.3 0.9 fusion.24
  33.2 0.8 broadcast_in_dim.4
  34.0 6.7 %all-to-all-start = ((f32[8,2,2,1024]{3,2,1,0:T(2,128)}), f32[8,2,2,1024]{3,2,1,0:T(2,128)S(1)}, u32[]{:S(2)}, u32[]{:S(2)}) async-start(f32[8,2,2,1024]{3,2,1,0:T(2,128)} %broadcast_in_dim.4), calls=%async_computation | async-start | bytes 262144 | tf_op jit(solution)/shard_map/all_to_all | solution.py:52
  40.7 4.9 %constant_dynamic-slice_fusion.17 = bf16[2,4,4,1,64,1024]{5,4,3,2,1,0:T(8,128)(2,1)} fusion(bf16[2,4,4,2,64,1024]{5,4,3,2,1,0:T(8,128)(2,1)} %bitcast.111, s32[]{:T(128)S(6)} %select_n.142), kind=kLoop, calls=%fused_computation.69 | loop fusion | bytes 8388612 | tf_op jit(solution)/shard_map/jit(dynamic_index_in_dim)/dynamic_slice | solution.py:40
  45.6 0.4 all-to-all-done
  46.0 0.1 fusion.20
  46.1 0.9 collective-permute-start.3
  47.0 2.7 %collective-permute-start.2 = (bf16[1024,512]{1,0:T(8,128)(2,1)}, bf16[1024,512]{1,0:T(8,128)(2,1)S(1)}, u32[]{:S(2)}, u32[]{:S(2)}) collective-permute-start(bf16[1024,512]{1,0:T(8,128)(2,1)} %get-tuple-element.26), channel_id=1, source_target_pairs={{0,1},{1,0},{2,3},{3,2},{4,5},{5,4},{6,7},{7,6},{8,9},{9,8},{10,11... | collective-permute-start | bytes 3145736 | tf_op jit(solution)/shard_map/ppermute | solution.py:36
  49.8 0.7 broadcast_in_dim.5
  50.5 4.2 %all-to-all-start.1 = ((f32[8,2,2,1024]{3,2,1,0:T(2,128)}), f32[8,2,2,1024]{3,2,1,0:T(2,128)S(1)}, u32[]{:S(2)}, u32[]{:S(2)}) async-start(f32[8,2,2,1024]{3,2,1,0:T(2,128)} %broadcast_in_dim.5), calls=%async_computation.1 | async-start | bytes 262144 | tf_op jit(solution)/shard_map/all_to_all | solution.py:52
  54.7 5.1 %constant_dynamic-slice_fusion.16 = bf16[2,4,4,1,64,1024]{5,4,3,2,1,0:T(8,128)(2,1)} fusion(bf16[2,4,4,2,64,1024]{5,4,3,2,1,0:T(8,128)(2,1)} %bitcast.112, s32[]{:T(128)S(6)} %select_n.143), kind=kLoop, calls=%fused_computation.68 | loop fusion | bytes 8388612 | tf_op jit(solution)/shard_map/jit(dynamic_index_in_dim)/dynamic_slice | solution.py:40
  59.8 16.9 %all-to-all-done.1 = f32[8,2,2,1024]{3,2,1,0:T(2,128)S(1)} async-done(((f32[8,2,2,1024]{3,2,1,0:T(2,128)}), f32[8,2,2,1024]{3,2,1,0:T(2,128)S(1)}, u32[]{:S(2)}, u32[]{:S(2)}) %all-to-all-start.1) | async-done | bytes 131104 | tf_op jit(solution)/shard_map/all_to_all | solution.py:52
  76.8 0.1 fusion.18
  76.9 0.5 broadcast_select_fusion.1
  77.4 1.6 copy-done.1
  79.0 1.7 multiply_convert_fusion
  80.7 1.8 collective-permute-start.4
  82.5 4.8 %fusion.10 = f32[2048,384]{1,0:T(8,128)S(1)} fusion(bf16[2048,1024]{1,0:T(8,128)(2,1)} %bitcast.114, bf16[1024,1024]{1,0:T(8,128)(2,1)S(1)} %multiply_convert_fusion), kind=kOutput, calls=%fused_computation.19 | convolution fusion | flops 1610612736 | bytes 8126464 | tf_op jit(solution)/shard_map/dot_general | solution.py:44
  87.2 3.6 %fusion.6 = f32[2048,640]{1,0:T(8,128)S(1)} fusion(bf16[2048,1024]{1,0:T(8,128)(2,1)S(1)} %bitcast.115, bf16[1024,1024]{1,0:T(8,128)(2,1)S(1)} %multiply_convert_fusion), kind=kOutput, calls=%fused_computation.12 | convolution fusion | flops 2684354560 | bytes 10747904 | tf_op jit(solution)/shard_map/dot_general | solution.py:44
  90.9 4.8 %add_convert_fusion.1 = bf16[2048,384]{1,0:T(8,128)(2,1)S(1)} fusion(f32[2048,384]{1,0:T(8,128)S(1)} %fusion.10, bf16[2048,1024]{1,0:T(8,128)(2,1)} %collective-permute-done.3, bf16[1024,1024]{1,0:T(8,128)(2,1)} %collective-permute-done.4), kind=kOutput, calls=%fused_computation.9 | convolution fusion | flops 1612185600 | bytes 9699328 | tf_op jit(solution)/shard_map/dot_general | solution.py:44
  95.7 0.2 constant_dynamic-slice_fusion.7
  95.9 0.6 collective-permute-start.13
  96.5 1.5 collective-permute-start.12
  98.0 6.2 %add_convert_fusion = bf16[2048,640]{1,0:T(8,128)(2,1)S(1)} fusion(f32[2048,640]{1,0:T(8,128)S(1)} %fusion.6, bf16[2048,1024]{1,0:T(8,128)(2,1)} %collective-permute-done.3, bf16[1024,1024]{1,0:T(8,128)(2,1)} %collective-permute-done.4), kind=kOutput, calls=%fused_computation | convolution fusion | flops 2686976000 | bytes 13369344 | tf_op jit(solution)/shard_map/dot_general | solution.py:44
  104.2 0.3 constant_dynamic-slice_fusion.15
  104.5 1.8 collective-permute-start.7
  106.3 0.6 collective-permute-start.6
  106.9 0.6 collective-permute-start.5
  107.5 0.1 fusion.25
  107.6 0.7 collective-permute-done.12
  108.3 1.7 collective-permute-start.18
  110.0 7.6 %collective-permute-done.11 = bf16[512,384]{1,0:T(8,128)(2,1)S(1)} collective-permute-done((bf16[512,384]{1,0:T(8,128)(2,1)S(1)}, bf16[512,384]{1,0:T(8,128)(2,1)S(1)}, u32[]{:S(2)}, u32[]{:S(2)}) %collective-permute-start.11) | collective-permute-done | bytes 393248 | tf_op jit(solution)/shard_map/ppermute | solution.py:36
  117.6 1.7 collective-permute-start.19
  119.3 0.2 fusion.12
  119.5 0.1 constant_dynamic-slice_fusion.3
  119.6 0.7 collective-permute-done.7
  120.2 3.4 %collective-permute-start.16 = (bf16[128,384]{1,0:T(8,128)(2,1)S(1)}, bf16[128,384]{1,0:T(8,128)(2,1)S(1)}, u32[]{:S(2)}, u32[]{:S(2)}) collective-permute-start(bf16[128,384]{1,0:T(8,128)(2,1)S(1)} %bitcast.135), channel_id=1, source_target_pairs={{0,12},{1,13},{2,14},{3,15},{4,0},{5,1},{6,2},{7,3},{8,4},{9,5},{1... | collective-permute-start | bytes 294920 | tf_op jit(solution)/shard_map/ppermute | solution.py:36
  123.7 0.1 collective-permute-start.15
  123.8 15.9 %collective-permute-done.5 = bf16[512,640]{1,0:T(8,128)(2,1)S(1)} collective-permute-done((bf16[512,640]{1,0:T(8,128)(2,1)S(1)}, bf16[512,640]{1,0:T(8,128)(2,1)S(1)}, u32[]{:S(2)}, u32[]{:S(2)}) %collective-permute-start.5) | collective-permute-done | bytes 655392 | tf_op jit(solution)/shard_map/ppermute | solution.py:36
  139.6 0.4 fusion.8
  140.0 0.1 constant_dynamic-slice_fusion.11
  140.1 2.7 %collective-permute-start.10 = (bf16[128,640]{1,0:T(8,128)(2,1)S(1)}, bf16[128,640]{1,0:T(8,128)(2,1)S(1)}, u32[]{:S(2)}, u32[]{:S(2)}) collective-permute-start(bf16[128,640]{1,0:T(8,128)(2,1)S(1)} %bitcast.132), channel_id=1, source_target_pairs={{0,48},{1,49},{2,50},{3,51},{4,52},{5,53},{6,54},{7,55},{8,56},{9,... | collective-permute-start | bytes 491528 | tf_op jit(solution)/shard_map/ppermute | solution.py:36
  142.9 0.5 collective-permute-start.9
  143.3 3.2 %collective-permute-done.14 = bf16[128,384]{1,0:T(8,128)(2,1)S(1)} collective-permute-done((bf16[128,384]{1,0:T(8,128)(2,1)S(1)}, bf16[128,384]{1,0:T(8,128)(2,1)S(1)}, u32[]{:S(2)}, u32[]{:S(2)}) %collective-permute-start.14) | collective-permute-done | bytes 98336 | tf_op jit(solution)/shard_map/ppermute | solution.py:36
  146.5 1.4 collective-permute-start.8
  147.9 0.1 convert_add_fusion.3
  148.0 1.0 collective-permute-done.9
  149.0 5.4 %collective-permute-done.8 = bf16[128,640]{1,0:T(8,128)(2,1)S(1)} collective-permute-done((bf16[128,640]{1,0:T(8,128)(2,1)S(1)}, bf16[128,640]{1,0:T(8,128)(2,1)S(1)}, u32[]{:S(2)}, u32[]{:S(2)}) %collective-permute-start.8) | collective-permute-done | bytes 163872 | tf_op jit(solution)/shard_map/ppermute | solution.py:36
  154.4 0.1 convert_add_fusion.2
  154.5 1.4 collective-permute-start.17
  155.9 6.9 %fusion.2 = f32[2048,1024]{1,0:T(8,128)} fusion(bf16[1024,1024]{1,0:T(8,128)(2,1)S(1)} %multiply_convert_fusion, bf16[1024,4096]{1,0:T(8,128)(2,1)S(1)} %bitcast.138, s32[]{:T(128)S(6)} %select_n.167), kind=kOutput, calls=%fused_computation.5 | convolution fusion | flops 4294967296 | bytes 14680068 | tf_op jit(solution)/shard_map/dot_general | solution.py:44
  162.8 0.7 fusion.16
  163.5 6.3 %fusion.1 = bf16[2048,512]{1,0:T(8,128)(2,1)S(1)} fusion(f32[2048,1024]{1,0:T(8,128)} %fusion.2, bf16[1024,2048]{1,0:T(8,128)(2,1)} %all-gather.2.cloned.1.call-done, bf16[1024,512]{1,0:T(8,128)(2,1)} %collective-permute-done.18), kind=kOutput, calls=%fused_computation.4 | convolution fusion | flops 2149580800 | bytes 11534336 | tf_op jit(solution)/shard_map/dot_general | solution.py:44
  169.8 0.5 dynamic_update_slice.6
  170.4 1.6 copy-done.7
  172.0 3.8 %fusion.4 = bf16[2048,1024]{1,0:T(8,128)(2,1)S(1)} fusion(bf16[2048,1024]{1,0:T(8,128)(2,1)S(1)} %dynamic_update_slice.6, bf16[1024,2048]{1,0:T(8,128)(2,1)S(1)} %copy-done.7, bf16[1024,512]{1,0:T(8,128)(2,1)} %collective-permute-done.19, f32[2048,1024]{1,0:T(8,128)S(1)} %copy-done.8), kind=kOutput, calls=%fused_computation.10 | convolution fusion | flops 2149580800 | bytes 11534336 | tf_op jit(solution)/shard_map/dot_general | solution.py:44
  175.8 2.0 %copy-done.3 = bf16[2048,1024]{1,0:T(8,128)(2,1)} copy-done((bf16[2048,1024]{1,0:T(8,128)(2,1)}, bf16[2048,1024]{1,0:T(8,128)(2,1)S(1)}, u32[]{:S(2)}) %copy-start.3) | copy-done | bytes 4194328
  (45 shorter events, 0.3 us)
Async XLA Ops:
  11.7 20.6 %collective-permute-start = (f32[8,1024]{1,0:T(8,128)}, f32[8,1024]{1,0:T(8,128)S(1)}, u32[]{:S(2)}, u32[]{:S(2)}) collective-permute-start(f32[8,1024]{1,0:T(8,128)} %get-tuple-element.16), channel_id=1, source_target_pairs={{0,1},{1,0},{2,3},{3,2},{4,5},{5,4},{6,7},{7,6},{8,9},{9,8},{10,11... | collective-permute-start | bytes 98312 | tf_op jit(solution)/shard_map/ppermute | solution.py:36
  16.3 16.8 %collective-permute-start.1 = (bf16[128,2048]{1,0:T(8,128)(2,1)S(1)}, bf16[128,2048]{1,0:T(8,128)(2,1)S(1)}, u32[]{:S(2)}, u32[]{:S(2)}) collective-permute-start(bf16[128,2048]{1,0:T(8,128)(2,1)S(1)} %dynamic_slice.68), channel_id=1, source_target_pairs={{0,1},{1,0},{2,3},{3,2},{4,5},{5,4},{6,7},{7,6},{8,9},{9,8},{10,11... | collective-permute-start | bytes 1572872 | tf_op jit(solution)/shard_map/ppermute | solution.py:36
  29.3 1.9 %copy-start = (f32[1024,1024]{1,0:T(8,128)}, f32[1024,1024]{1,0:T(8,128)S(1)}, u32[]{:S(2)}) copy-start(f32[1024,1024]{1,0:T(8,128)S(1)} %get-tuple-element.53) | copy-start | bytes 12582916
  33.2 12.4 %copy-start.5 = (bf16[128,2048]{1,0:T(8,128)(2,1)}, bf16[128,2048]{1,0:T(8,128)(2,1)S(1)}, u32[]{:S(2)}) copy-start(bf16[128,2048]{1,0:T(8,128)(2,1)S(1)} %collective-permute-done.1) | copy-start | bytes 1572868
  34.0 12.0 %all-to-all-start = ((f32[8,2,2,1024]{3,2,1,0:T(2,128)}), f32[8,2,2,1024]{3,2,1,0:T(2,128)S(1)}, u32[]{:S(2)}, u32[]{:S(2)}) async-start(f32[8,2,2,1024]{3,2,1,0:T(2,128)} %broadcast_in_dim.4), calls=%async_computation | async-start | bytes 262144 | tf_op jit(solution)/shard_map/all_to_all | solution.py:52
  40.7 122.8 %all-gather.2.cloned.1.call-start = ((), (), s32[]{:S(2)}) async-start(), calls=%async_computation.2 | async-start | bytes 4718592 | tf_op jit(solution)/shard_map/all_gather | solution.py:130
  46.1 44.8 %collective-permute-start.3 = (bf16[2048,1024]{1,0:T(8,128)(2,1)}, bf16[2048,1024]{1,0:T(8,128)(2,1)}, u32[]{:S(2)}, u32[]{:S(2)}) collective-permute-start(bf16[2048,1024]{1,0:T(8,128)(2,1)} %bitcast.113), channel_id=1, source_target_pairs={{0,2},{1,3},{2,0},{3,1},{4,6},{5,7},{6,4},{7,5},{8,10},{9,11},{10,... | collective-permute-start | bytes 12582920 | tf_op jit(solution)/shard_map/ppermute | solution.py:36
  47.0 29.8 %collective-permute-start.2 = (bf16[1024,512]{1,0:T(8,128)(2,1)}, bf16[1024,512]{1,0:T(8,128)(2,1)S(1)}, u32[]{:S(2)}, u32[]{:S(2)}) collective-permute-start(bf16[1024,512]{1,0:T(8,128)(2,1)} %get-tuple-element.26), channel_id=1, source_target_pairs={{0,1},{1,0},{2,3},{3,2},{4,5},{5,4},{6,7},{7,6},{8,9},{9,8},{10,11... | collective-permute-start | bytes 3145736 | tf_op jit(solution)/shard_map/ppermute | solution.py:36
  50.5 26.2 %all-to-all-start.1 = ((f32[8,2,2,1024]{3,2,1,0:T(2,128)}), f32[8,2,2,1024]{3,2,1,0:T(2,128)S(1)}, u32[]{:S(2)}, u32[]{:S(2)}) async-start(f32[8,2,2,1024]{3,2,1,0:T(2,128)} %broadcast_in_dim.5), calls=%async_computation.1 | async-start | bytes 262144 | tf_op jit(solution)/shard_map/all_to_all | solution.py:52
  54.7 22.2 %copy-start.2 = (bf16[2048,512]{1,0:T(8,128)(2,1)S(1)}, bf16[2048,512]{1,0:T(8,128)(2,1)}, u32[]{:S(2)}) copy-start(bf16[2048,512]{1,0:T(8,128)(2,1)} %x_ref.1) | copy-start | bytes 6291460
  59.8 17.6 %copy-start.6 = (f32[1024]{0:T(1024)S(1)}, f32[1024]{0:T(1024)}, u32[]{:S(2)}) copy-start(f32[1024]{0:T(1024)} %param.7) | copy-start | bytes 12292
  76.7 2.2 %copy-start.1 = (f32[1024,1024]{1,0:T(8,128)S(1)}, f32[1024,1024]{1,0:T(8,128)}, u32[]{:S(2)}) copy-start(f32[1024,1024]{1,0:T(8,128)} %copy-done) | copy-start | bytes 12582916
  80.7 10.2 %collective-permute-start.4 = (bf16[1024,1024]{1,0:T(8,128)(2,1)S(1)}, bf16[1024,1024]{1,0:T(8,128)(2,1)}, u32[]{:S(2)}, u32[]{:S(2)}) collective-permute-start(bf16[1024,1024]{1,0:T(8,128)(2,1)S(1)} %multiply_convert_fusion), channel_id=1, source_target_pairs={{0,2},{1,3},{2,0},{3,1},{4,6},{5,7},{6,4},{7,5},{8,10},{9,11},{10,... | collective-permute-start | bytes 6291464 | tf_op jit(solution)/shard_map/ppermute | solution.py:36
  82.5 4.8 %copy-start.4 = (bf16[2,4,4,1,64,1024]{5,4,3,2,1,0:T(8,128)(2,1)S(1)}, bf16[2,4,4,1,64,1024]{5,4,3,2,1,0:T(8,128)(2,1)}, u32[]{:S(2)}) copy-start(bf16[2,4,4,1,64,1024]{5,4,3,2,1,0:T(8,128)(2,1)} %constant_dynamic-slice_fusion.16) | copy-start | bytes 12582916
  95.9 11.0 %collective-permute-start.13 = (bf16[512,384]{1,0:T(8,128)(2,1)S(1)}, bf16[512,384]{1,0:T(8,128)(2,1)S(1)}, u32[]{:S(2)}, u32[]{:S(2)}) collective-permute-start(bf16[512,384]{1,0:T(8,128)(2,1)S(1)} %bitcast.129), channel_id=1, source_target_pairs={{0,48},{1,49},{2,50},{3,51},{4,52},{5,53},{6,54},{7,55},{8,56},{9,... | collective-permute-start | bytes 1179656 | tf_op jit(solution)/shard_map/ppermute | solution.py:36
  96.5 11.8 %collective-permute-start.12 = (bf16[512,384]{1,0:T(8,128)(2,1)S(1)}, bf16[512,384]{1,0:T(8,128)(2,1)S(1)}, u32[]{:S(2)}, u32[]{:S(2)}) collective-permute-start(bf16[512,384]{1,0:T(8,128)(2,1)S(1)} %bitcast.128), channel_id=1, source_target_pairs={{0,32},{1,33},{2,34},{3,35},{4,36},{5,37},{6,38},{7,39},{8,40},{9,... | collective-permute-start | bytes 1179656 | tf_op jit(solution)/shard_map/ppermute | solution.py:36
  98.0 19.6 %collective-permute-start.11 = (bf16[512,384]{1,0:T(8,128)(2,1)S(1)}, bf16[512,384]{1,0:T(8,128)(2,1)S(1)}, u32[]{:S(2)}, u32[]{:S(2)}) collective-permute-start(bf16[512,384]{1,0:T(8,128)(2,1)S(1)} %bitcast.127), channel_id=1, source_target_pairs={{0,16},{1,17},{2,18},{3,19},{4,20},{5,21},{6,22},{7,23},{8,24},{9,... | collective-permute-start | bytes 1179656 | tf_op jit(solution)/shard_map/ppermute | solution.py:36
  104.2 51.7 %slice-start = ((s8[8388608]{0:T(1024)(128)(4,1)}), s8[4194304]{0:T(1024)(128)(4,1)S(1)}, s32[]{:S(2)}) async-start(s8[8388608]{0:T(1024)(128)(4,1)} %bitcast.137), calls=%async_computation.3 | async-start | bytes 8388608
  104.5 15.7 %collective-permute-start.7 = (bf16[512,640]{1,0:T(8,128)(2,1)S(1)}, bf16[512,640]{1,0:T(8,128)(2,1)S(1)}, u32[]{:S(2)}, u32[]{:S(2)}) collective-permute-start(bf16[512,640]{1,0:T(8,128)(2,1)S(1)} %bitcast.126), channel_id=1, source_target_pairs={{0,12},{1,13},{2,14},{3,15},{4,0},{5,1},{6,2},{7,3},{8,4},{9,5},{1... | collective-permute-start | bytes 1966088 | tf_op jit(solution)/shard_map/ppermute | solution.py:36
  106.3 17.4 %collective-permute-start.6 = (bf16[512,640]{1,0:T(8,128)(2,1)S(1)}, bf16[512,640]{1,0:T(8,128)(2,1)S(1)}, u32[]{:S(2)}, u32[]{:S(2)}) collective-permute-start(bf16[512,640]{1,0:T(8,128)(2,1)S(1)} %bitcast.125), channel_id=1, source_target_pairs={{0,8},{1,9},{2,10},{3,11},{4,12},{5,13},{6,14},{7,15},{8,0},{9,1},... | collective-permute-start | bytes 1966088 | tf_op jit(solution)/shard_map/ppermute | solution.py:36
  106.9 32.8 %collective-permute-start.5 = (bf16[512,640]{1,0:T(8,128)(2,1)S(1)}, bf16[512,640]{1,0:T(8,128)(2,1)S(1)}, u32[]{:S(2)}, u32[]{:S(2)}) collective-permute-start(bf16[512,640]{1,0:T(8,128)(2,1)S(1)} %bitcast.124), channel_id=1, source_target_pairs={{0,4},{1,5},{2,6},{3,7},{4,8},{5,9},{6,10},{7,11},{8,12},{9,13},{1... | collective-permute-start | bytes 1966088 | tf_op jit(solution)/shard_map/ppermute | solution.py:36
  108.3 55.2 %collective-permute-start.18 = (bf16[1024,512]{1,0:T(8,128)(2,1)S(1)}, bf16[1024,512]{1,0:T(8,128)(2,1)}, u32[]{:S(2)}, u32[]{:S(2)}) collective-permute-start(bf16[1024,512]{1,0:T(8,128)(2,1)S(1)} %get-tuple-element.37), channel_id=1, source_target_pairs={{0,1},{1,0},{2,3},{3,2},{4,5},{5,4},{6,7},{7,6},{8,9},{9,8},{10,11... | collective-permute-start | bytes 3145736 | tf_op jit(solution)/shard_map/ppermute | solution.py:36
  117.6 52.7 %collective-permute-start.19 = (bf16[1024,512]{1,0:T(8,128)(2,1)S(1)}, bf16[1024,512]{1,0:T(8,128)(2,1)}, u32[]{:S(2)}, u32[]{:S(2)}) collective-permute-start(bf16[1024,512]{1,0:T(8,128)(2,1)S(1)} %get-tuple-element.36), channel_id=1, source_target_pairs={{0,1},{1,0},{2,3},{3,2},{4,5},{5,4},{6,7},{7,6},{8,9},{9,8},{10,11... | collective-permute-start | bytes 3145736 | tf_op jit(solution)/shard_map/ppermute | solution.py:36
  119.3 36.6 %slice-start.1 = ((s8[8388608]{0:T(1024)(128)(4,1)}), s8[4194304]{0:T(1024)(128)(4,1)S(1)}, s32[]{:S(2)}) async-start(s8[8388608]{0:T(1024)(128)(4,1)} %bitcast.137), calls=%async_computation.4 | async-start | bytes 8388608
  120.2 19.9 %collective-permute-start.16 = (bf16[128,384]{1,0:T(8,128)(2,1)S(1)}, bf16[128,384]{1,0:T(8,128)(2,1)S(1)}, u32[]{:S(2)}, u32[]{:S(2)}) collective-permute-start(bf16[128,384]{1,0:T(8,128)(2,1)S(1)} %bitcast.135), channel_id=1, source_target_pairs={{0,12},{1,13},{2,14},{3,15},{4,0},{5,1},{6,2},{7,3},{8,4},{9,5},{1... | collective-permute-start | bytes 294920 | tf_op jit(solution)/shard_map/ppermute | solution.py:36
  123.7 19.2 %collective-permute-start.15 = (bf16[128,384]{1,0:T(8,128)(2,1)S(1)}, bf16[128,384]{1,0:T(8,128)(2,1)S(1)}, u32[]{:S(2)}, u32[]{:S(2)}) collective-permute-start(bf16[128,384]{1,0:T(8,128)(2,1)S(1)} %bitcast.134), channel_id=1, source_target_pairs={{0,8},{1,9},{2,10},{3,11},{4,12},{5,13},{6,14},{7,15},{8,0},{9,1},... | collective-permute-start | bytes 294920 | tf_op jit(solution)/shard_map/ppermute | solution.py:36
  139.6 6.9 %collective-permute-start.14 = (bf16[128,384]{1,0:T(8,128)(2,1)S(1)}, bf16[128,384]{1,0:T(8,128)(2,1)S(1)}, u32[]{:S(2)}, u32[]{:S(2)}) collective-permute-start(bf16[128,384]{1,0:T(8,128)(2,1)S(1)} %bitcast.133), channel_id=1, source_target_pairs={{0,4},{1,5},{2,6},{3,7},{4,8},{5,9},{6,10},{7,11},{8,12},{9,13},{1... | collective-permute-start | bytes 294920 | tf_op jit(solution)/shard_map/ppermute | solution.py:36
  140.1 7.8 %collective-permute-start.10 = (bf16[128,640]{1,0:T(8,128)(2,1)S(1)}, bf16[128,640]{1,0:T(8,128)(2,1)S(1)}, u32[]{:S(2)}, u32[]{:S(2)}) collective-permute-start(bf16[128,640]{1,0:T(8,128)(2,1)S(1)} %bitcast.132), channel_id=1, source_target_pairs={{0,48},{1,49},{2,50},{3,51},{4,52},{5,53},{6,54},{7,55},{8,56},{9,... | collective-permute-start | bytes 491528 | tf_op jit(solution)/shard_map/ppermute | solution.py:36
  142.9 6.1 %collective-permute-start.9 = (bf16[128,640]{1,0:T(8,128)(2,1)S(1)}, bf16[128,640]{1,0:T(8,128)(2,1)S(1)}, u32[]{:S(2)}, u32[]{:S(2)}) collective-permute-start(bf16[128,640]{1,0:T(8,128)(2,1)S(1)} %bitcast.131), channel_id=1, source_target_pairs={{0,32},{1,33},{2,34},{3,35},{4,36},{5,37},{6,38},{7,39},{8,40},{9,... | collective-permute-start | bytes 491528 | tf_op jit(solution)/shard_map/ppermute | solution.py:36
  146.5 7.9 %collective-permute-start.8 = (bf16[128,640]{1,0:T(8,128)(2,1)S(1)}, bf16[128,640]{1,0:T(8,128)(2,1)S(1)}, u32[]{:S(2)}, u32[]{:S(2)}) collective-permute-start(bf16[128,640]{1,0:T(8,128)(2,1)S(1)} %bitcast.130), channel_id=1, source_target_pairs={{0,16},{1,17},{2,18},{3,19},{4,20},{5,21},{6,22},{7,23},{8,24},{9,... | collective-permute-start | bytes 491528 | tf_op jit(solution)/shard_map/ppermute | solution.py:36
  154.5 8.3 %collective-permute-start.17 = (bf16[64,1024]{1,0:T(8,128)(2,1)S(1)}, bf16[64,1024]{1,0:T(8,128)(2,1)S(1)}, u32[]{:S(2)}, u32[]{:S(2)}) collective-permute-start(bf16[64,1024]{1,0:T(8,128)(2,1)S(1)} %fusion.15), channel_id=1, source_target_pairs={{0,64},{1,65},{2,66},{3,67},{4,68},{5,69},{6,70},{7,71},{8,72},{9,... | collective-permute-start | bytes 393224 | tf_op jit(solution)/shard_map/ppermute | solution.py:36
  163.5 6.8 %copy-start.8 = (f32[2048,1024]{1,0:T(8,128)S(1)}, f32[2048,1024]{1,0:T(8,128)}, u32[]{:S(2)}) copy-start(f32[2048,1024]{1,0:T(8,128)} %fusion.2) | copy-start | bytes 25165828
  169.8 2.2 %copy-start.7 = (bf16[1024,2048]{1,0:T(8,128)(2,1)S(1)}, bf16[1024,2048]{1,0:T(8,128)(2,1)}, u32[]{:S(2)}) copy-start(bf16[1024,2048]{1,0:T(8,128)(2,1)} %all-gather.2.cloned.1.call-done) | copy-start | bytes 12582916
  175.8 2.0 %copy-start.3 = (bf16[2048,1024]{1,0:T(8,128)(2,1)}, bf16[2048,1024]{1,0:T(8,128)(2,1)S(1)}, u32[]{:S(2)}) copy-start(bf16[2048,1024]{1,0:T(8,128)(2,1)S(1)} %fusion.4) | copy-start | bytes 12582916
Sparse Core Ops, SparseCore 0:
  49.9 31.1 all-gather.1

commit v7 on v6

--- a/solution.py
+++ b/solution.py
@@ -153,9 +153,7 @@
         * (jnp.exp(logits - student_norm[:, None]) - jnp.exp(teacher - teacher_norm[:, None]))
     ).astype(BF16)
     partner_grad = send(logit_grad, CORE)
-    other_grad = []
-    for i in range(2):
-        other_grad.append(send(logit_grad[:, i * 512 : i * 512 + 512], HIGH))
+    other_grad = send(logit_grad, HIGH)
 
     tokens = (slice(0, 640), slice(640, 1024))
 
@@ -184,8 +182,9 @@
     own_share = lax.optimization_barrier(dot(own_hidden, logit_grad, 0, 0))
     weight_grad = jnp.zeros((2048, 1024), BF16)
     for i in range(2):
-        half = own_share[:, i * 512 : i * 512 + 512] + dot(other_hidden, other_grad[i], 0, 0)
-        weight_grad = lax.dynamic_update_slice(weight_grad, half.astype(BF16), (0, i * 512))
+        part = slice(i * 1024, i * 1024 + 1024)
+        half = (own_share[part] + dot(other_hidden[:, part], other_grad, 0, 0)).astype(BF16)
+        weight_grad = lax.dynamic_update_slice(weight_grad, half, (i * 1024, 0))
         weight_grad = lax.optimization_barrier(weight_grad)
     return hidden_grad, weight_grad
 

time: 187 us -> 190 us (1.016)
  waiting for transfers between devices: 51.7 us -> 38.8 us
  starting transfers between devices: 38.1 us -> 48.4 us
  other arithmetic: 5.83 us -> 8.43 us
  matrix products: 49.3 us -> 51.4 us
    ppermute x20 -> x19, waiting for transfers between devices: 34.4 us -> 21.5 us  [send(): return lax.ppermute(value, AXES, moves)]
    ppermute x20 -> x19, starting transfers between devices: 27.1 us -> 37.4 us  [send(): return lax.ppermute(value, AXES, moves)]
    dot_general x8, matrix products: 49.3 us -> 51.4 us  [dot(): lax.dot_general(a, b, (((ca,), (cb,)), ((), ())), preferred_element_type=...]
    unnamed x22 -> x18, local copies, waits for them, and re-layouts: 7.2 us -> 7.31 us
  transfers between devices with their start and end apart: 23 -> 22, of which waited for: 9 -> 10; matrix products, arithmetic and copies ran while one was open for 35% -> 34% of each run, Pallas kernels for 0% -> 0%
where the time goes in v7:
time: 190 us; the launch traced here: 189 us
  matrix products  51.4 us (27%)
  starting transfers between devices  48.4 us (25%)
  waiting for transfers between devices  38.8 us (20%)
  local copies, waits for them, and re-layouts  22.7 us (12%)
  between operations  14.3 us (8%)
  other arithmetic  8.43 us (4%)
  Pallas kernels  4.52 us (2%)
    dot_general x8, matrix products, dot(): lax.dot_general(a, b, (((ca,), (cb,)), ((), ())), preferred_element_type=...  51.4 us
    ppermute x19, starting transfers between devices, send(): return lax.ppermute(value, AXES, moves)  37.4 us
    ppermute x19, waiting for transfers between devices, send(): return lax.ppermute(value, AXES, moves)  21.5 us
    all_to_all x2, waiting for transfers between devices, merge(): stats = lax.all_to_all(stats, axis, 0, 0, tiled=True)  17.3 us
    dynamic_slice x6, local copies, waits for them, and re-layouts, pick(): return lax.dynamic_index_in_dim(value, index, axis, keepdims=False)  12.4 us
    all_to_all x2, starting transfers between devices, merge(): stats = lax.all_to_all(stats, axis, 0, 0, tiled=True)  11 us
    unnamed x18, local copies, waits for them, and re-layouts  7.31 us
    pallas_call x1, Pallas kernels, shard_stats(): pl.pallas_call(stats_kernel, grid_spec=pltpu.PrefetchScalarGridSpec(num_s...  4.52 us
  transfers between devices with their start and end apart: 22, of which 10 were waited for; matrix products, arithmetic and copies ran while one was open for 34% of the time, Pallas kernels for 0%

profile of v7, /device:TPU:1, one launch (start us, length us, event | category | flops | bytes accessed | tf_op | source)
XLA Modules:
  0.0 188.7 jit_solution(6218302846178362233)
XLA Ops:
  7.2 4.5 %shard_map.59 = (f32[8,1024]{1,0:T(8,128)}, f32[8,1024]{1,0:T(8,128)}, bf16[1024,512]{1,0:T(8,128)(2,1)}) custom-call(s32[1]{0:T(128)} %bitcast.2.high_ref, bf16[2048,512]{1,0:T(8,128)(2,1)} %x_ref.1), custom_call_target="tpu_custom_call" | custom-call | flops 4194304 | bytes 3145728 | tf_op jit(solution)/shard_map/pallas_call | solution.py:80
  11.7 3.6 %collective-permute-start = (f32[8,1024]{1,0:T(8,128)}, f32[8,1024]{1,0:T(8,128)S(1)}, u32[]{:S(2)}, u32[]{:S(2)}) collective-permute-start(f32[8,1024]{1,0:T(8,128)} %get-tuple-element.16), channel_id=1, source_target_pairs={{0,1},{1,0},{2,3},{3,2},{4,5},{5,4},{6,7},{7,6},{8,9},{9,8},{10,11... | collective-permute-start | bytes 98312 | tf_op jit(solution)/shard_map/ppermute | solution.py:36
  15.3 1.1 dynamic_slice.68
  16.3 0.1 collective-permute-start.1
  16.4 12.9 %fusion.34 = (f32[1024]{0:T(1024)S(1)}, f32[1024,1024]{1,0:T(8,128)S(1)}) fusion(bf16[1024,4096]{1,0:T(8,128)(2,1)} %param.4, bf16[4096,1024]{1,0:T(8,128)(2,1)} %param.5), kind=kOutput, calls=%fused_computation.78 | convolution fusion | flops 8590982144 | bytes 20975616 | tf_op jit(solution)/shard_map/dot_general | solution.py:44
  29.3 2.0 %copy-done = f32[1024,1024]{1,0:T(8,128)} copy-done((f32[1024,1024]{1,0:T(8,128)}, f32[1024,1024]{1,0:T(8,128)S(1)}, u32[]{:S(2)}) %copy-start) | copy-done | bytes 4194328
  31.3 1.0 exponential_reduce_fusion
  32.4 0.9 fusion.32
  33.3 0.8 broadcast_in_dim.4
  34.1 6.8 %all-to-all-start = ((f32[8,2,2,1024]{3,2,1,0:T(2,128)}), f32[8,2,2,1024]{3,2,1,0:T(2,128)S(1)}, u32[]{:S(2)}, u32[]{:S(2)}) async-start(f32[8,2,2,1024]{3,2,1,0:T(2,128)} %broadcast_in_dim.4), calls=%async_computation | async-start | bytes 262144 | tf_op jit(solution)/shard_map/all_to_all | solution.py:52
  40.8 4.9 %constant_dynamic-slice_fusion.17 = bf16[2,4,4,1,64,1024]{5,4,3,2,1,0:T(8,128)(2,1)} fusion(bf16[2,4,4,2,64,1024]{5,4,3,2,1,0:T(8,128)(2,1)} %bitcast.109, s32[]{:T(128)S(6)} %select_n.142), kind=kLoop, calls=%fused_computation.73 | loop fusion | bytes 8388612 | tf_op jit(solution)/shard_map/jit(dynamic_index_in_dim)/dynamic_slice | solution.py:40
  45.7 0.4 all-to-all-done
  46.1 0.1 fusion.28
  46.2 0.9 collective-permute-start.3
  47.1 2.7 %collective-permute-start.2 = (bf16[1024,512]{1,0:T(8,128)(2,1)}, bf16[1024,512]{1,0:T(8,128)(2,1)S(1)}, u32[]{:S(2)}, u32[]{:S(2)}) collective-permute-start(bf16[1024,512]{1,0:T(8,128)(2,1)} %get-tuple-element.26), channel_id=1, source_target_pairs={{0,1},{1,0},{2,3},{3,2},{4,5},{5,4},{6,7},{7,6},{8,9},{9,8},{10,11... | collective-permute-start | bytes 3145736 | tf_op jit(solution)/shard_map/ppermute | solution.py:36
  49.9 0.7 broadcast_in_dim.5
  50.6 4.2 %all-to-all-start.1 = ((f32[8,2,2,1024]{3,2,1,0:T(2,128)}), f32[8,2,2,1024]{3,2,1,0:T(2,128)S(1)}, u32[]{:S(2)}, u32[]{:S(2)}) async-start(f32[8,2,2,1024]{3,2,1,0:T(2,128)} %broadcast_in_dim.5), calls=%async_computation.1 | async-start | bytes 262144 | tf_op jit(solution)/shard_map/all_to_all | solution.py:52
  54.8 5.1 %constant_dynamic-slice_fusion.16 = bf16[2,4,4,1,64,1024]{5,4,3,2,1,0:T(8,128)(2,1)} fusion(bf16[2,4,4,2,64,1024]{5,4,3,2,1,0:T(8,128)(2,1)} %bitcast.110, s32[]{:T(128)S(6)} %select_n.143), kind=kLoop, calls=%fused_computation.72 | loop fusion | bytes 8388612 | tf_op jit(solution)/shard_map/jit(dynamic_index_in_dim)/dynamic_slice | solution.py:40
  59.9 16.9 %all-to-all-done.1 = f32[8,2,2,1024]{3,2,1,0:T(2,128)S(1)} async-done(((f32[8,2,2,1024]{3,2,1,0:T(2,128)}), f32[8,2,2,1024]{3,2,1,0:T(2,128)S(1)}, u32[]{:S(2)}, u32[]{:S(2)}) %all-to-all-start.1) | async-done | bytes 131104 | tf_op jit(solution)/shard_map/all_to_all | solution.py:52
  76.9 0.1 fusion.26
  77.0 0.5 broadcast_select_fusion.1
  77.4 1.6 copy-done.1
  79.0 1.7 multiply_convert_fusion
  80.8 1.8 collective-permute-start.4
  82.6 4.8 %fusion.18 = f32[2048,384]{1,0:T(8,128)S(1)} fusion(bf16[2048,1024]{1,0:T(8,128)(2,1)} %bitcast.112, bf16[1024,1024]{1,0:T(8,128)(2,1)S(1)} %multiply_convert_fusion), kind=kOutput, calls=%fused_computation.23 | convolution fusion | flops 1610612736 | bytes 8126464 | tf_op jit(solution)/shard_map/dot_general | solution.py:44
  87.3 3.6 %fusion.14 = f32[2048,640]{1,0:T(8,128)S(1)} fusion(bf16[2048,1024]{1,0:T(8,128)(2,1)S(1)} %bitcast.113, bf16[1024,1024]{1,0:T(8,128)(2,1)S(1)} %multiply_convert_fusion), kind=kOutput, calls=%fused_computation.16 | convolution fusion | flops 2684354560 | bytes 10747904 | tf_op jit(solution)/shard_map/dot_general | solution.py:44
  90.9 4.8 %add_convert_fusion.1 = bf16[2048,384]{1,0:T(8,128)(2,1)S(1)} fusion(f32[2048,384]{1,0:T(8,128)S(1)} %fusion.18, bf16[2048,1024]{1,0:T(8,128)(2,1)} %collective-permute-done.3, bf16[1024,1024]{1,0:T(8,128)(2,1)} %collective-permute-done.4), kind=kOutput, calls=%fused_computation.9 | convolution fusion | flops 1612185600 | bytes 9699328 | tf_op jit(solution)/shard_map/dot_general | solution.py:44
  95.8 0.9 constant_dynamic-slice_fusion.7
  96.7 0.6 collective-permute-start.13
  97.3 1.4 collective-permute-start.12
  98.7 6.2 %add_convert_fusion = bf16[2048,640]{1,0:T(8,128)(2,1)S(1)} fusion(f32[2048,640]{1,0:T(8,128)S(1)} %fusion.14, bf16[2048,1024]{1,0:T(8,128)(2,1)} %collective-permute-done.3, bf16[1024,1024]{1,0:T(8,128)(2,1)} %collective-permute-done.4), kind=kOutput, calls=%fused_computation | convolution fusion | flops 2686976000 | bytes 13369344 | tf_op jit(solution)/shard_map/dot_general | solution.py:44
  105.0 1.4 constant_dynamic-slice_fusion.15
  106.4 1.7 collective-permute-start.7
  108.1 0.6 collective-permute-start.6
  108.7 0.6 collective-permute-start.5
  109.2 0.1 collective-permute-done.12
  109.4 1.7 collective-permute-start.18
  111.1 7.5 %collective-permute-done.11 = bf16[512,384]{1,0:T(8,128)(2,1)} collective-permute-done((bf16[512,384]{1,0:T(8,128)(2,1)S(1)}, bf16[512,384]{1,0:T(8,128)(2,1)}, u32[]{:S(2)}, u32[]{:S(2)}) %collective-permute-start.11) | collective-permute-done | bytes 393248 | tf_op jit(solution)/shard_map/ppermute | solution.py:36
  118.6 1.4 fusion.20
  120.0 0.1 constant_dynamic-slice_fusion.3
  120.1 1.8 collective-permute-start.16
  121.9 0.3 collective-permute-done.7
  122.2 2.0 %collective-permute-start.15 = (bf16[128,384]{1,0:T(8,128)(2,1)S(1)}, bf16[128,384]{1,0:T(8,128)(2,1)S(1)}, u32[]{:S(2)}, u32[]{:S(2)}) collective-permute-start(bf16[128,384]{1,0:T(8,128)(2,1)S(1)} %bitcast.128), channel_id=1, source_target_pairs={{0,8},{1,9},{2,10},{3,11},{4,12},{5,13},{6,14},{7,15},{8,0},{9,1},... | collective-permute-start | bytes 294920 | tf_op jit(solution)/shard_map/ppermute | solution.py:36
  124.2 1.0 collective-permute-done.6
  125.2 12.5 %collective-permute-start.14 = (bf16[128,384]{1,0:T(8,128)(2,1)S(1)}, bf16[128,384]{1,0:T(8,128)(2,1)S(1)}, u32[]{:S(2)}, u32[]{:S(2)}) collective-permute-start(bf16[128,384]{1,0:T(8,128)(2,1)S(1)} %bitcast.127), channel_id=1, source_target_pairs={{0,4},{1,5},{2,6},{3,7},{4,8},{5,9},{6,10},{7,11},{8,12},{9,13},{1... | collective-permute-start | bytes 294920 | tf_op jit(solution)/shard_map/ppermute | solution.py:36
  137.7 3.9 %collective-permute-done.5 = bf16[512,640]{1,0:T(8,128)(2,1)} collective-permute-done((bf16[512,640]{1,0:T(8,128)(2,1)}, bf16[512,640]{1,0:T(8,128)(2,1)}, u32[]{:S(2)}, u32[]{:S(2)}) %collective-permute-start.5) | collective-permute-done | bytes 655392 | tf_op jit(solution)/shard_map/ppermute | solution.py:36
  141.7 1.8 fusion.16
  143.5 0.1 constant_dynamic-slice_fusion.11
  143.6 2.7 %collective-permute-start.10 = (bf16[128,640]{1,0:T(8,128)(2,1)S(1)}, bf16[128,640]{1,0:T(8,128)(2,1)S(1)}, u32[]{:S(2)}, u32[]{:S(2)}) collective-permute-start(bf16[128,640]{1,0:T(8,128)(2,1)S(1)} %bitcast.126), channel_id=1, source_target_pairs={{0,48},{1,49},{2,50},{3,51},{4,52},{5,53},{6,54},{7,55},{8,56},{9,... | collective-permute-start | bytes 491528 | tf_op jit(solution)/shard_map/ppermute | solution.py:36
  146.3 0.4 collective-permute-start.9
  146.8 0.8 collective-permute-start.8
  147.5 0.1 convert_add_fusion.3
  147.6 1.7 collective-permute-done.10
  149.3 3.1 %collective-permute-done.9 = bf16[128,640]{1,0:T(8,128)(2,1)S(1)} collective-permute-done((bf16[128,640]{1,0:T(8,128)(2,1)S(1)}, bf16[128,640]{1,0:T(8,128)(2,1)S(1)}, u32[]{:S(2)}, u32[]{:S(2)}) %collective-permute-start.9) | collective-permute-done | bytes 163872 | tf_op jit(solution)/shard_map/ppermute | solution.py:36
  152.4 3.8 %collective-permute-done.8 = bf16[128,640]{1,0:T(8,128)(2,1)S(1)} collective-permute-done((bf16[128,640]{1,0:T(8,128)(2,1)S(1)}, bf16[128,640]{1,0:T(8,128)(2,1)S(1)}, u32[]{:S(2)}, u32[]{:S(2)}) %collective-permute-start.8) | collective-permute-done | bytes 163872 | tf_op jit(solution)/shard_map/ppermute | solution.py:36
  156.2 0.1 convert_add_fusion.2
  156.3 1.4 collective-permute-start.17
  157.7 9.1 %fusion.2 = f32[2048,1024]{1,0:T(8,128)} fusion(bf16[1024,1024]{1,0:T(8,128)(2,1)S(1)} %multiply_convert_fusion, bf16[1024,4096]{1,0:T(8,128)(2,1)} %param.4, s32[]{:T(128)S(6)} %select_n.167), kind=kOutput, calls=%fused_computation.5 | convolution fusion | flops 4294967296 | bytes 14680068 | tf_op jit(solution)/shard_map/dot_general | solution.py:44
  166.8 0.7 fusion.24
  167.5 6.0 %fusion.1 = bf16[1024,1024]{1,0:T(8,128)(2,1)S(1)} fusion(f32[2048,1024]{1,0:T(8,128)} %fusion.2, bf16[1024,1024]{1,0:T(8,128)(2,1)} %collective-permute-done.18, bf16[1024,2048]{1,0:T(8,128)(2,1)} %all-gather.2.cloned.1.call-done), kind=kOutput, calls=%fused_computation.4 | convolution fusion | flops 2149580800 | bytes 10485760 | tf_op jit(solution)/shard_map/dot_general | solution.py:44
  173.5 0.5 dynamic_update_slice.6
  174.0 1.7 copy-done.7
  175.7 4.1 %fusion.4 = bf16[2048,1024]{1,0:T(8,128)(2,1)S(1)} fusion(bf16[2048,1024]{1,0:T(8,128)(2,1)S(1)} %dynamic_update_slice.6, f32[2048,1024]{1,0:T(8,128)S(1)} %copy-done.8, bf16[1024,1024]{1,0:T(8,128)(2,1)} %collective-permute-done.18, bf16[1024,2048]{1,0:T(8,128)(2,1)S(1)} %copy-done.7), kind=kOutput, calls=%fused_computation.10 | convolution fusion | flops 2149580800 | bytes 10485760 | tf_op jit(solution)/shard_map/dot_general | solution.py:44
  179.8 2.0 %copy-done.3 = bf16[2048,1024]{1,0:T(8,128)(2,1)} copy-done((bf16[2048,1024]{1,0:T(8,128)(2,1)}, bf16[2048,1024]{1,0:T(8,128)(2,1)S(1)}, u32[]{:S(2)}) %copy-start.3) | copy-done | bytes 4194328
  (37 shorter events, 0.2 us)
Async XLA Ops:
  11.7 20.7 %collective-permute-start = (f32[8,1024]{1,0:T(8,128)}, f32[8,1024]{1,0:T(8,128)S(1)}, u32[]{:S(2)}, u32[]{:S(2)}) collective-permute-start(f32[8,1024]{1,0:T(8,128)} %get-tuple-element.16), channel_id=1, source_target_pairs={{0,1},{1,0},{2,3},{3,2},{4,5},{5,4},{6,7},{7,6},{8,9},{9,8},{10,11... | collective-permute-start | bytes 98312 | tf_op jit(solution)/shard_map/ppermute | solution.py:36
  16.3 16.9 %collective-permute-start.1 = (bf16[128,2048]{1,0:T(8,128)(2,1)S(1)}, bf16[128,2048]{1,0:T(8,128)(2,1)S(1)}, u32[]{:S(2)}, u32[]{:S(2)}) collective-permute-start(bf16[128,2048]{1,0:T(8,128)(2,1)S(1)} %dynamic_slice.68), channel_id=1, source_target_pairs={{0,1},{1,0},{2,3},{3,2},{4,5},{5,4},{6,7},{7,6},{8,9},{9,8},{10,11... | collective-permute-start | bytes 1572872 | tf_op jit(solution)/shard_map/ppermute | solution.py:36
  29.3 2.0 %copy-start = (f32[1024,1024]{1,0:T(8,128)}, f32[1024,1024]{1,0:T(8,128)S(1)}, u32[]{:S(2)}) copy-start(f32[1024,1024]{1,0:T(8,128)S(1)} %get-tuple-element.51) | copy-start | bytes 12582916
  33.2 12.4 %copy-start.5 = (bf16[128,2048]{1,0:T(8,128)(2,1)}, bf16[128,2048]{1,0:T(8,128)(2,1)S(1)}, u32[]{:S(2)}) copy-start(bf16[128,2048]{1,0:T(8,128)(2,1)S(1)} %collective-permute-done.1) | copy-start | bytes 1572868
  34.1 12.0 %all-to-all-start = ((f32[8,2,2,1024]{3,2,1,0:T(2,128)}), f32[8,2,2,1024]{3,2,1,0:T(2,128)S(1)}, u32[]{:S(2)}, u32[]{:S(2)}) async-start(f32[8,2,2,1024]{3,2,1,0:T(2,128)} %broadcast_in_dim.4), calls=%async_computation | async-start | bytes 262144 | tf_op jit(solution)/shard_map/all_to_all | solution.py:52
  40.8 126.7 %all-gather.2.cloned.1.call-start = ((), (), s32[]{:S(2)}) async-start(), calls=%async_computation.2 | async-start | bytes 4718592 | tf_op jit(solution)/shard_map/all_gather | solution.py:130
  46.2 44.7 %collective-permute-start.3 = (bf16[2048,1024]{1,0:T(8,128)(2,1)}, bf16[2048,1024]{1,0:T(8,128)(2,1)}, u32[]{:S(2)}, u32[]{:S(2)}) collective-permute-start(bf16[2048,1024]{1,0:T(8,128)(2,1)} %bitcast.111), channel_id=1, source_target_pairs={{0,2},{1,3},{2,0},{3,1},{4,6},{5,7},{6,4},{7,5},{8,10},{9,11},{10,... | collective-permute-start | bytes 12582920 | tf_op jit(solution)/shard_map/ppermute | solution.py:36
  47.1 29.8 %collective-permute-start.2 = (bf16[1024,512]{1,0:T(8,128)(2,1)}, bf16[1024,512]{1,0:T(8,128)(2,1)S(1)}, u32[]{:S(2)}, u32[]{:S(2)}) collective-permute-start(bf16[1024,512]{1,0:T(8,128)(2,1)} %get-tuple-element.26), channel_id=1, source_target_pairs={{0,1},{1,0},{2,3},{3,2},{4,5},{5,4},{6,7},{7,6},{8,9},{9,8},{10,11... | collective-permute-start | bytes 3145736 | tf_op jit(solution)/shard_map/ppermute | solution.py:36
  50.6 26.2 %all-to-all-start.1 = ((f32[8,2,2,1024]{3,2,1,0:T(2,128)}), f32[8,2,2,1024]{3,2,1,0:T(2,128)S(1)}, u32[]{:S(2)}, u32[]{:S(2)}) async-start(f32[8,2,2,1024]{3,2,1,0:T(2,128)} %broadcast_in_dim.5), calls=%async_computation.1 | async-start | bytes 262144 | tf_op jit(solution)/shard_map/all_to_all | solution.py:52
  54.8 22.2 %copy-start.2 = (bf16[2048,512]{1,0:T(8,128)(2,1)S(1)}, bf16[2048,512]{1,0:T(8,128)(2,1)}, u32[]{:S(2)}) copy-start(bf16[2048,512]{1,0:T(8,128)(2,1)} %x_ref.1) | copy-start | bytes 6291460
  59.9 17.6 %copy-start.6 = (f32[1024]{0:T(1024)S(1)}, f32[1024]{0:T(1024)}, u32[]{:S(2)}) copy-start(f32[1024]{0:T(1024)} %param.7) | copy-start | bytes 12292
  76.8 2.2 %copy-start.1 = (f32[1024,1024]{1,0:T(8,128)S(1)}, f32[1024,1024]{1,0:T(8,128)}, u32[]{:S(2)}) copy-start(f32[1024,1024]{1,0:T(8,128)} %copy-done) | copy-start | bytes 12582916
  80.8 10.2 %collective-permute-start.4 = (bf16[1024,1024]{1,0:T(8,128)(2,1)S(1)}, bf16[1024,1024]{1,0:T(8,128)(2,1)}, u32[]{:S(2)}, u32[]{:S(2)}) collective-permute-start(bf16[1024,1024]{1,0:T(8,128)(2,1)S(1)} %multiply_convert_fusion), channel_id=1, source_target_pairs={{0,2},{1,3},{2,0},{3,1},{4,6},{5,7},{6,4},{7,5},{8,10},{9,11},{10,... | collective-permute-start | bytes 6291464 | tf_op jit(solution)/shard_map/ppermute | solution.py:36
  82.6 4.8 %copy-start.4 = (bf16[2,4,4,1,64,1024]{5,4,3,2,1,0:T(8,128)(2,1)S(1)}, bf16[2,4,4,1,64,1024]{5,4,3,2,1,0:T(8,128)(2,1)}, u32[]{:S(2)}) copy-start(bf16[2,4,4,1,64,1024]{5,4,3,2,1,0:T(8,128)(2,1)} %constant_dynamic-slice_fusion.16) | copy-start | bytes 12582916
  96.7 11.9 %collective-permute-start.13 = (bf16[512,384]{1,0:T(8,128)(2,1)S(1)}, bf16[512,384]{1,0:T(8,128)(2,1)}, u32[]{:S(2)}, u32[]{:S(2)}) collective-permute-start(bf16[512,384]{1,0:T(8,128)(2,1)S(1)} %bitcast.123), channel_id=1, source_target_pairs={{0,48},{1,49},{2,50},{3,51},{4,52},{5,53},{6,54},{7,55},{8,56},{9,... | collective-permute-start | bytes 1179656 | tf_op jit(solution)/shard_map/ppermute | solution.py:36
  97.3 12.1 %collective-permute-start.12 = (bf16[512,384]{1,0:T(8,128)(2,1)}, bf16[512,384]{1,0:T(8,128)(2,1)}, u32[]{:S(2)}, u32[]{:S(2)}) collective-permute-start(bf16[512,384]{1,0:T(8,128)(2,1)} %bitcast.30), channel_id=1, source_target_pairs={{0,32},{1,33},{2,34},{3,35},{4,36},{5,37},{6,38},{7,39},{8,40},{9,... | collective-permute-start | bytes 1179656 | tf_op jit(solution)/shard_map/ppermute | solution.py:36
  98.7 19.8 %collective-permute-start.11 = (bf16[512,384]{1,0:T(8,128)(2,1)S(1)}, bf16[512,384]{1,0:T(8,128)(2,1)}, u32[]{:S(2)}, u32[]{:S(2)}) collective-permute-start(bf16[512,384]{1,0:T(8,128)(2,1)S(1)} %bitcast.122), channel_id=1, source_target_pairs={{0,16},{1,17},{2,18},{3,19},{4,20},{5,21},{6,22},{7,23},{8,24},{9,... | collective-permute-start | bytes 1179656 | tf_op jit(solution)/shard_map/ppermute | solution.py:36
  106.4 15.9 %collective-permute-start.7 = (bf16[512,640]{1,0:T(8,128)(2,1)}, bf16[512,640]{1,0:T(8,128)(2,1)}, u32[]{:S(2)}, u32[]{:S(2)}) collective-permute-start(bf16[512,640]{1,0:T(8,128)(2,1)} %bitcast.20), channel_id=1, source_target_pairs={{0,12},{1,13},{2,14},{3,15},{4,0},{5,1},{6,2},{7,3},{8,4},{9,5},{1... | collective-permute-start | bytes 1966088 | tf_op jit(solution)/shard_map/ppermute | solution.py:36
  108.1 17.1 %collective-permute-start.6 = (bf16[512,640]{1,0:T(8,128)(2,1)}, bf16[512,640]{1,0:T(8,128)(2,1)}, u32[]{:S(2)}, u32[]{:S(2)}) collective-permute-start(bf16[512,640]{1,0:T(8,128)(2,1)} %bitcast.19), channel_id=1, source_target_pairs={{0,8},{1,9},{2,10},{3,11},{4,12},{5,13},{6,14},{7,15},{8,0},{9,1},... | collective-permute-start | bytes 1966088 | tf_op jit(solution)/shard_map/ppermute | solution.py:36
  108.7 33.0 %collective-permute-start.5 = (bf16[512,640]{1,0:T(8,128)(2,1)}, bf16[512,640]{1,0:T(8,128)(2,1)}, u32[]{:S(2)}, u32[]{:S(2)}) collective-permute-start(bf16[512,640]{1,0:T(8,128)(2,1)} %bitcast.18), channel_id=1, source_target_pairs={{0,4},{1,5},{2,6},{3,7},{4,8},{5,9},{6,10},{7,11},{8,12},{9,13},{1... | collective-permute-start | bytes 1966088 | tf_op jit(solution)/shard_map/ppermute | solution.py:36
  109.4 58.1 %collective-permute-start.18 = (bf16[1024,1024]{1,0:T(8,128)(2,1)S(1)}, bf16[1024,1024]{1,0:T(8,128)(2,1)}, u32[]{:S(2)}, u32[]{:S(2)}) collective-permute-start(bf16[1024,1024]{1,0:T(8,128)(2,1)S(1)} %multiply_convert_fusion), channel_id=1, source_target_pairs={{0,1},{1,0},{2,3},{3,2},{4,5},{5,4},{6,7},{7,6},{8,9},{9,8},{10,11... | collective-permute-start | bytes 6291464 | tf_op jit(solution)/shard_map/ppermute | solution.py:36
  120.1 26.2 %collective-permute-start.16 = (bf16[128,384]{1,0:T(8,128)(2,1)S(1)}, bf16[128,384]{1,0:T(8,128)(2,1)S(1)}, u32[]{:S(2)}, u32[]{:S(2)}) collective-permute-start(bf16[128,384]{1,0:T(8,128)(2,1)S(1)} %bitcast.129), channel_id=1, source_target_pairs={{0,12},{1,13},{2,14},{3,15},{4,0},{5,1},{6,2},{7,3},{8,4},{9,5},{1... | collective-permute-start | bytes 294920 | tf_op jit(solution)/shard_map/ppermute | solution.py:36
  122.2 24.5 %collective-permute-start.15 = (bf16[128,384]{1,0:T(8,128)(2,1)S(1)}, bf16[128,384]{1,0:T(8,128)(2,1)S(1)}, u32[]{:S(2)}, u32[]{:S(2)}) collective-permute-start(bf16[128,384]{1,0:T(8,128)(2,1)S(1)} %bitcast.128), channel_id=1, source_target_pairs={{0,8},{1,9},{2,10},{3,11},{4,12},{5,13},{6,14},{7,15},{8,0},{9,1},... | collective-permute-start | bytes 294920 | tf_op jit(solution)/shard_map/ppermute | solution.py:36
  125.2 22.3 %collective-permute-start.14 = (bf16[128,384]{1,0:T(8,128)(2,1)S(1)}, bf16[128,384]{1,0:T(8,128)(2,1)S(1)}, u32[]{:S(2)}, u32[]{:S(2)}) collective-permute-start(bf16[128,384]{1,0:T(8,128)(2,1)S(1)} %bitcast.127), channel_id=1, source_target_pairs={{0,4},{1,5},{2,6},{3,7},{4,8},{5,9},{6,10},{7,11},{8,12},{9,13},{1... | collective-permute-start | bytes 294920 | tf_op jit(solution)/shard_map/ppermute | solution.py:36
  143.6 5.7 %collective-permute-start.10 = (bf16[128,640]{1,0:T(8,128)(2,1)S(1)}, bf16[128,640]{1,0:T(8,128)(2,1)S(1)}, u32[]{:S(2)}, u32[]{:S(2)}) collective-permute-start(bf16[128,640]{1,0:T(8,128)(2,1)S(1)} %bitcast.126), channel_id=1, source_target_pairs={{0,48},{1,49},{2,50},{3,51},{4,52},{5,53},{6,54},{7,55},{8,56},{9,... | collective-permute-start | bytes 491528 | tf_op jit(solution)/shard_map/ppermute | solution.py:36
  146.3 6.1 %collective-permute-start.9 = (bf16[128,640]{1,0:T(8,128)(2,1)S(1)}, bf16[128,640]{1,0:T(8,128)(2,1)S(1)}, u32[]{:S(2)}, u32[]{:S(2)}) collective-permute-start(bf16[128,640]{1,0:T(8,128)(2,1)S(1)} %bitcast.125), channel_id=1, source_target_pairs={{0,32},{1,33},{2,34},{3,35},{4,36},{5,37},{6,38},{7,39},{8,40},{9,... | collective-permute-start | bytes 491528 | tf_op jit(solution)/shard_map/ppermute | solution.py:36
  146.8 9.5 %collective-permute-start.8 = (bf16[128,640]{1,0:T(8,128)(2,1)S(1)}, bf16[128,640]{1,0:T(8,128)(2,1)S(1)}, u32[]{:S(2)}, u32[]{:S(2)}) collective-permute-start(bf16[128,640]{1,0:T(8,128)(2,1)S(1)} %bitcast.124), channel_id=1, source_target_pairs={{0,16},{1,17},{2,18},{3,19},{4,20},{5,21},{6,22},{7,23},{8,24},{9,... | collective-permute-start | bytes 491528 | tf_op jit(solution)/shard_map/ppermute | solution.py:36
  156.3 10.5 %collective-permute-start.17 = (bf16[64,1024]{1,0:T(8,128)(2,1)S(1)}, bf16[64,1024]{1,0:T(8,128)(2,1)S(1)}, u32[]{:S(2)}, u32[]{:S(2)}) collective-permute-start(bf16[64,1024]{1,0:T(8,128)(2,1)S(1)} %fusion.23), channel_id=1, source_target_pairs={{0,64},{1,65},{2,66},{3,67},{4,68},{5,69},{6,70},{7,71},{8,72},{9,... | collective-permute-start | bytes 393224 | tf_op jit(solution)/shard_map/ppermute | solution.py:36
  167.5 6.5 %copy-start.8 = (f32[2048,1024]{1,0:T(8,128)S(1)}, f32[2048,1024]{1,0:T(8,128)}, u32[]{:S(2)}) copy-start(f32[2048,1024]{1,0:T(8,128)} %fusion.2) | copy-start | bytes 25165828
  173.5 2.2 %copy-start.7 = (bf16[1024,2048]{1,0:T(8,128)(2,1)S(1)}, bf16[1024,2048]{1,0:T(8,128)(2,1)}, u32[]{:S(2)}) copy-start(bf16[1024,2048]{1,0:T(8,128)(2,1)} %all-gather.2.cloned.1.call-done) | copy-start | bytes 12582916
  179.8 2.0 %copy-start.3 = (bf16[2048,1024]{1,0:T(8,128)(2,1)}, bf16[2048,1024]{1,0:T(8,128)(2,1)S(1)}, u32[]{:S(2)}) copy-start(bf16[2048,1024]{1,0:T(8,128)(2,1)S(1)} %fusion.4) | copy-start | bytes 12582916
Sparse Core Ops, SparseCore 0:
  50.0 31.1 all-gather.1

commit v8 on v7

--- a/solution.py
+++ b/solution.py
@@ -66,7 +66,13 @@
 
     @pl.when(step < 2)
     def _():
-        theirs_ref[...] = stats
+        high_part = stats.astype(BF16)
+        rest = stats - high_part.astype(F32)
+        middle = rest.astype(BF16)
+        low_part = rest - middle.astype(F32)
+        row = lax.broadcasted_iota(jnp.int32, stats.shape, 0)
+        split = jnp.where(row == 2, middle.astype(F32), jnp.where(row == 3, low_part, high_part.astype(F32)))
+        theirs_ref[...] = split.astype(BF16)
         part_ref[...] = raw
 
     @pl.when(step >= 2)
@@ -95,7 +101,7 @@
             ],
         ),
         out_shape=[
-            jax.ShapeDtypeStruct((8, 1024), F32),
+            jax.ShapeDtypeStruct((8, 1024), BF16),
             jax.ShapeDtypeStruct((8, 1024), F32),
             jax.ShapeDtypeStruct((1024, 512), BF16),
         ],
@@ -113,12 +119,14 @@
     z, core = dp // 2, dp % 2
 
     other_stats, mine, part = shard_stats(high, teacher_logits)
-    theirs = send(other_stats, HIGH)
+
+    piece = lax.dynamic_slice(hidden_states, (dp * 128, (1 - high) * 2048), (128, 2048))
+    piece = send(jnp.concatenate([piece, other_stats.reshape(4, 2048)[:4]], axis=0), HIGH)
+    theirs = piece[128:].reshape(8, 1024)[:4].astype(F32)
+    theirs = (theirs[0], theirs[1] + theirs[2] + theirs[3])
+    piece = piece[:128]
     teacher_top = jnp.maximum(mine[0], theirs[0])
     teacher_total = mine[1] * jnp.exp(mine[0] - teacher_top) + theirs[1] * jnp.exp(theirs[0] - teacher_top)
-
-    piece = lax.dynamic_slice(hidden_states, (dp * 128, (1 - high) * 2048), (128, 2048))
-    piece = send(piece, HIGH)
 
     other_part = row_major(send(part, HIGH))
     own_part = lax.dynamic_slice(teacher_logits, (high * 1024, 0), (1024, 512))

time: 190 us -> 191 us (level)
  starting transfers between devices: 48.4 us -> 46.1 us
  matrix products: 51.4 us -> 53.6 us
  other arithmetic: 8.43 us -> 10.5 us
    ppermute x19 -> x18, starting transfers between devices: 37.4 us -> 34.7 us  [send(): return lax.ppermute(value, AXES, moves)]
    dot_general x8, matrix products: 51.4 us -> 53.6 us  [dot(): lax.dot_general(a, b, (((ca,), (cb,)), ((), ())), preferred_element_type=...]
    reduce_sum x1, other arithmetic: 1.04 us -> 3.08 us  [compute(): student_total = jnp.sum(jnp.exp(logits - student_top[:, None]), axis=1)]
    unnamed x18 -> x14, local copies, waits for them, and re-layouts: 7.31 us -> 5.29 us
    ppermute x19 -> x18, waiting for transfers between devices: 21.5 us -> 20.8 us  [send(): return lax.ppermute(value, AXES, moves)]
  transfers between devices with their start and end apart: 22 -> 21, of which waited for: 10 -> 10; matrix products, arithmetic and copies ran while one was open for 34% -> 35% of each run, Pallas kernels for 0% -> 0%
where the time goes in v8:
time: 191 us; the launch traced here: 189 us
  matrix products  53.6 us (28%)
  starting transfers between devices  46.1 us (24%)
  waiting for transfers between devices  38.2 us (20%)
  local copies, waits for them, and re-layouts  22.2 us (12%)
  between operations  14.3 us (7%)
  other arithmetic  10.5 us (5%)
  Pallas kernels  4.54 us (2%)
    dot_general x8, matrix products, dot(): lax.dot_general(a, b, (((ca,), (cb,)), ((), ())), preferred_element_type=...  53.6 us
    ppermute x18, starting transfers between devices, send(): return lax.ppermute(value, AXES, moves)  34.7 us
    ppermute x18, waiting for transfers between devices, send(): return lax.ppermute(value, AXES, moves)  20.8 us
    all_to_all x2, waiting for transfers between devices, merge(): stats = lax.all_to_all(stats, axis, 0, 0, tiled=True)  17.3 us
    dynamic_slice x6, local copies, waits for them, and re-layouts, pick(): return lax.dynamic_index_in_dim(value, index, axis, keepdims=False)  12.3 us
    all_to_all x2, starting transfers between devices, merge(): stats = lax.all_to_all(stats, axis, 0, 0, tiled=True)  11.4 us
    unnamed x14, local copies, waits for them, and re-layouts  5.29 us
    pallas_call x1, Pallas kernels, shard_stats(): pl.pallas_call(stats_kernel, grid_spec=pltpu.PrefetchScalarGridSpec(num_s...  4.54 us
  transfers between devices with their start and end apart: 21, of which 10 were waited for; matrix products, arithmetic and copies ran while one was open for 35% of the time, Pallas kernels for 0%

profile of v8, /device:TPU:1, one launch (start us, length us, event | category | flops | bytes accessed | tf_op | source)
XLA Modules:
  0.0 189.5 jit_solution(14612303344683320033)
XLA Ops:
  7.2 4.5 %shard_map.59 = (bf16[8,1024]{1,0:T(8,128)(2,1)}, f32[8,1024]{1,0:T(8,128)}, bf16[1024,512]{1,0:T(8,128)(2,1)}) custom-call(s32[1]{0:T(128)} %bitcast.2.high_ref, bf16[2048,512]{1,0:T(8,128)(2,1)} %x_ref.1), custom_call_target="tpu_custom_call" | custom-call | flops 4194304 | bytes 3145728 | tf_op jit(solution)/shard_map/pallas_call | solution.py:86
  11.7 0.7 reshape.120
  12.5 1.1 dynamic_slice.68
  13.6 3.6 %collective-permute-start = (bf16[132,2048]{1,0:T(8,128)(2,1)S(1)}, bf16[132,2048]{1,0:T(8,128)(2,1)S(1)}, u32[]{:S(2)}, u32[]{:S(2)}) collective-permute-start(bf16[132,2048]{1,0:T(8,128)(2,1)S(1)} %pad_maximum_fusion), channel_id=1, source_target_pairs={{0,1},{1,0},{2,3},{3,2},{4,5},{5,4},{6,7},{7,6},{8,9},{9,8},{10,11... | collective-permute-start | bytes 1622024 | tf_op jit(solution)/shard_map/ppermute | solution.py:36
  17.2 15.1 %fusion.35 = (f32[1024]{0:T(1024)S(1)}, f32[1024,1024]{1,0:T(8,128)}) fusion(bf16[1024,4096]{1,0:T(8,128)(2,1)} %param.4, bf16[4096,1024]{1,0:T(8,128)(2,1)} %param.5), kind=kOutput, calls=%fused_computation.82 | convolution fusion | flops 8590982144 | bytes 20975616 | tf_op jit(solution)/shard_map/dot_general | solution.py:44
  32.3 3.1 %exponential_reduce_fusion = f32[1024]{0:T(1024)S(1)} fusion(f32[1024,1024]{1,0:T(8,128)} %get-tuple-element.51, f32[1024]{0:T(1024)S(1)} %get-tuple-element.50), kind=kLoop, calls=%fused_computation.8 | loop fusion | flops 2096128 | bytes 4202496 | tf_op jit(solution)/shard_map/reduce_sum | solution.py:136
  35.5 0.8 slice.96
  36.3 0.9 fusion.33
  37.2 0.7 broadcast_in_dim.4
  37.9 6.3 %all-to-all-start = ((f32[8,2,2,1024]{3,2,1,0:T(2,128)}), f32[8,2,2,1024]{3,2,1,0:T(2,128)S(1)}, u32[]{:S(2)}, u32[]{:S(2)}) async-start(f32[8,2,2,1024]{3,2,1,0:T(2,128)} %broadcast_in_dim.4), calls=%async_computation | async-start | bytes 262144 | tf_op jit(solution)/shard_map/all_to_all | solution.py:52
  44.2 4.8 %constant_dynamic-slice_fusion.17 = bf16[2,4,4,1,64,1024]{5,4,3,2,1,0:T(8,128)(2,1)} fusion(bf16[2,4,4,2,64,1024]{5,4,3,2,1,0:T(8,128)(2,1)} %bitcast.109, s32[]{:T(128)S(6)} %select_n.142), kind=kLoop, calls=%fused_computation.75 | loop fusion | bytes 8388612 | tf_op jit(solution)/shard_map/jit(dynamic_index_in_dim)/dynamic_slice | solution.py:40
  49.0 0.4 all-to-all-done
  49.4 0.1 fusion.28
  49.5 0.9 collective-permute-start.2
  50.5 0.2 collective-permute-start.1
  50.7 0.7 broadcast_in_dim.5
  51.4 5.1 %all-to-all-start.1 = ((f32[8,2,2,1024]{3,2,1,0:T(2,128)}), f32[8,2,2,1024]{3,2,1,0:T(2,128)S(1)}, u32[]{:S(2)}, u32[]{:S(2)}) async-start(f32[8,2,2,1024]{3,2,1,0:T(2,128)} %broadcast_in_dim.5), calls=%async_computation.1 | async-start | bytes 262144 | tf_op jit(solution)/shard_map/all_to_all | solution.py:52
  56.5 5.1 %constant_dynamic-slice_fusion.16 = bf16[2,4,4,1,64,1024]{5,4,3,2,1,0:T(8,128)(2,1)} fusion(bf16[2,4,4,2,64,1024]{5,4,3,2,1,0:T(8,128)(2,1)} %bitcast.110, s32[]{:T(128)S(6)} %select_n.143), kind=kLoop, calls=%fused_computation.74 | loop fusion | bytes 8388612 | tf_op jit(solution)/shard_map/jit(dynamic_index_in_dim)/dynamic_slice | solution.py:40
  61.6 16.9 %all-to-all-done.1 = f32[8,2,2,1024]{3,2,1,0:T(2,128)S(1)} async-done(((f32[8,2,2,1024]{3,2,1,0:T(2,128)}), f32[8,2,2,1024]{3,2,1,0:T(2,128)S(1)}, u32[]{:S(2)}, u32[]{:S(2)}) %all-to-all-start.1) | async-done | bytes 131104 | tf_op jit(solution)/shard_map/all_to_all | solution.py:52
  78.6 0.1 fusion.26
  78.7 0.5 broadcast_select_fusion.1
  79.2 1.6 copy-done
  80.8 1.7 multiply_convert_fusion
  82.5 1.8 collective-permute-start.3
  84.3 4.8 %fusion.18 = f32[2048,384]{1,0:T(8,128)S(1)} fusion(bf16[2048,1024]{1,0:T(8,128)(2,1)} %bitcast.112, bf16[1024,1024]{1,0:T(8,128)(2,1)S(1)} %multiply_convert_fusion), kind=kOutput, calls=%fused_computation.23 | convolution fusion | flops 1610612736 | bytes 8126464 | tf_op jit(solution)/shard_map/dot_general | solution.py:44
  89.1 3.6 %fusion.14 = f32[2048,640]{1,0:T(8,128)S(1)} fusion(bf16[2048,1024]{1,0:T(8,128)(2,1)S(1)} %bitcast.113, bf16[1024,1024]{1,0:T(8,128)(2,1)S(1)} %multiply_convert_fusion), kind=kOutput, calls=%fused_computation.16 | convolution fusion | flops 2684354560 | bytes 10747904 | tf_op jit(solution)/shard_map/dot_general | solution.py:44
  92.7 4.8 %add_convert_fusion.1 = bf16[2048,384]{1,0:T(8,128)(2,1)S(1)} fusion(f32[2048,384]{1,0:T(8,128)S(1)} %fusion.18, bf16[2048,1024]{1,0:T(8,128)(2,1)} %collective-permute-done.2, bf16[1024,1024]{1,0:T(8,128)(2,1)} %collective-permute-done.3), kind=kOutput, calls=%fused_computation.9 | convolution fusion | flops 1612185600 | bytes 9699328 | tf_op jit(solution)/shard_map/dot_general | solution.py:44
  97.5 0.9 constant_dynamic-slice_fusion.7
  98.5 0.6 collective-permute-start.12
  99.1 1.4 collective-permute-start.11
  100.5 6.2 %add_convert_fusion = bf16[2048,640]{1,0:T(8,128)(2,1)S(1)} fusion(f32[2048,640]{1,0:T(8,128)S(1)} %fusion.14, bf16[2048,1024]{1,0:T(8,128)(2,1)} %collective-permute-done.2, bf16[1024,1024]{1,0:T(8,128)(2,1)} %collective-permute-done.3), kind=kOutput, calls=%fused_computation | convolution fusion | flops 2686976000 | bytes 13369344 | tf_op jit(solution)/shard_map/dot_general | solution.py:44
  106.7 1.4 constant_dynamic-slice_fusion.15
  108.1 1.7 collective-permute-start.6
  109.8 0.6 collective-permute-start.5
  110.4 0.6 collective-permute-start.4
  111.0 0.2 collective-permute-done.11
  111.1 2.5 %collective-permute-start.17 = (bf16[1024,1024]{1,0:T(8,128)(2,1)S(1)}, bf16[1024,1024]{1,0:T(8,128)(2,1)}, u32[]{:S(2)}, u32[]{:S(2)}) collective-permute-start(bf16[1024,1024]{1,0:T(8,128)(2,1)S(1)} %multiply_convert_fusion), channel_id=1, source_target_pairs={{0,1},{1,0},{2,3},{3,2},{4,5},{5,4},{6,7},{7,6},{8,9},{9,8},{10,11... | collective-permute-start | bytes 6291464 | tf_op jit(solution)/shard_map/ppermute | solution.py:36
  113.6 6.8 %collective-permute-done.10 = bf16[512,384]{1,0:T(8,128)(2,1)} collective-permute-done((bf16[512,384]{1,0:T(8,128)(2,1)S(1)}, bf16[512,384]{1,0:T(8,128)(2,1)}, u32[]{:S(2)}, u32[]{:S(2)}) %collective-permute-start.10) | collective-permute-done | bytes 393248 | tf_op jit(solution)/shard_map/ppermute | solution.py:36
  120.4 1.4 fusion.20
  121.8 0.1 constant_dynamic-slice_fusion.3
  121.9 1.8 collective-permute-start.15
  123.6 0.3 collective-permute-done.6
  123.9 2.0 %collective-permute-start.14 = (bf16[128,384]{1,0:T(8,128)(2,1)S(1)}, bf16[128,384]{1,0:T(8,128)(2,1)S(1)}, u32[]{:S(2)}, u32[]{:S(2)}) collective-permute-start(bf16[128,384]{1,0:T(8,128)(2,1)S(1)} %bitcast.128), channel_id=1, source_target_pairs={{0,8},{1,9},{2,10},{3,11},{4,12},{5,13},{6,14},{7,15},{8,0},{9,1},... | collective-permute-start | bytes 294920 | tf_op jit(solution)/shard_map/ppermute | solution.py:36
  126.0 1.0 collective-permute-done.5
  126.9 12.5 %collective-permute-start.13 = (bf16[128,384]{1,0:T(8,128)(2,1)S(1)}, bf16[128,384]{1,0:T(8,128)(2,1)S(1)}, u32[]{:S(2)}, u32[]{:S(2)}) collective-permute-start(bf16[128,384]{1,0:T(8,128)(2,1)S(1)} %bitcast.127), channel_id=1, source_target_pairs={{0,4},{1,5},{2,6},{3,7},{4,8},{5,9},{6,10},{7,11},{8,12},{9,13},{1... | collective-permute-start | bytes 294920 | tf_op jit(solution)/shard_map/ppermute | solution.py:36
  139.4 3.9 %collective-permute-done.4 = bf16[512,640]{1,0:T(8,128)(2,1)} collective-permute-done((bf16[512,640]{1,0:T(8,128)(2,1)}, bf16[512,640]{1,0:T(8,128)(2,1)}, u32[]{:S(2)}, u32[]{:S(2)}) %collective-permute-start.4) | collective-permute-done | bytes 655392 | tf_op jit(solution)/shard_map/ppermute | solution.py:36
  143.4 1.8 fusion.16
  145.2 0.1 constant_dynamic-slice_fusion.11
  145.3 2.7 %collective-permute-start.9 = (bf16[128,640]{1,0:T(8,128)(2,1)S(1)}, bf16[128,640]{1,0:T(8,128)(2,1)S(1)}, u32[]{:S(2)}, u32[]{:S(2)}) collective-permute-start(bf16[128,640]{1,0:T(8,128)(2,1)S(1)} %bitcast.126), channel_id=1, source_target_pairs={{0,48},{1,49},{2,50},{3,51},{4,52},{5,53},{6,54},{7,55},{8,56},{9,... | collective-permute-start | bytes 491528 | tf_op jit(solution)/shard_map/ppermute | solution.py:36
  148.0 0.4 collective-permute-start.8
  148.4 0.8 collective-permute-start.7
  149.2 0.1 convert_add_fusion.3
  149.3 1.7 collective-permute-done.9
  151.0 3.1 %collective-permute-done.8 = bf16[128,640]{1,0:T(8,128)(2,1)S(1)} collective-permute-done((bf16[128,640]{1,0:T(8,128)(2,1)S(1)}, bf16[128,640]{1,0:T(8,128)(2,1)S(1)}, u32[]{:S(2)}, u32[]{:S(2)}) %collective-permute-start.8) | collective-permute-done | bytes 163872 | tf_op jit(solution)/shard_map/ppermute | solution.py:36
  154.1 3.8 %collective-permute-done.7 = bf16[128,640]{1,0:T(8,128)(2,1)S(1)} collective-permute-done((bf16[128,640]{1,0:T(8,128)(2,1)S(1)}, bf16[128,640]{1,0:T(8,128)(2,1)S(1)}, u32[]{:S(2)}, u32[]{:S(2)}) %collective-permute-start.7) | collective-permute-done | bytes 163872 | tf_op jit(solution)/shard_map/ppermute | solution.py:36
  157.9 0.1 convert_add_fusion.2
  158.1 0.5 collective-permute-start.16
  158.6 9.0 %fusion.2 = f32[2048,1024]{1,0:T(8,128)} fusion(bf16[1024,1024]{1,0:T(8,128)(2,1)S(1)} %multiply_convert_fusion, bf16[1024,4096]{1,0:T(8,128)(2,1)} %param.4, s32[]{:T(128)S(6)} %select_n.167), kind=kOutput, calls=%fused_computation.5 | convolution fusion | flops 4294967296 | bytes 14680068 | tf_op jit(solution)/shard_map/dot_general | solution.py:44
  167.6 0.7 fusion.24
  168.3 6.0 %fusion.1 = bf16[1024,1024]{1,0:T(8,128)(2,1)S(1)} fusion(f32[2048,1024]{1,0:T(8,128)} %fusion.2, bf16[1024,1024]{1,0:T(8,128)(2,1)} %collective-permute-done.17, bf16[1024,2048]{1,0:T(8,128)(2,1)} %all-gather.2.cloned.1.call-done), kind=kOutput, calls=%fused_computation.4 | convolution fusion | flops 2149580800 | bytes 10485760 | tf_op jit(solution)/shard_map/dot_general | solution.py:44
  174.3 0.5 dynamic_update_slice.6
  174.8 1.7 copy-done.5
  176.5 4.1 %fusion.4 = bf16[2048,1024]{1,0:T(8,128)(2,1)S(1)} fusion(bf16[2048,1024]{1,0:T(8,128)(2,1)S(1)} %dynamic_update_slice.6, f32[2048,1024]{1,0:T(8,128)S(1)} %copy-done.6, bf16[1024,1024]{1,0:T(8,128)(2,1)} %collective-permute-done.17, bf16[1024,2048]{1,0:T(8,128)(2,1)S(1)} %copy-done.5), kind=kOutput, calls=%fused_computation.10 | convolution fusion | flops 2149580800 | bytes 10485760 | tf_op jit(solution)/shard_map/dot_general | solution.py:44
  180.6 2.0 %copy-done.2 = bf16[2048,1024]{1,0:T(8,128)(2,1)} copy-done((bf16[2048,1024]{1,0:T(8,128)(2,1)}, bf16[2048,1024]{1,0:T(8,128)(2,1)S(1)}, u32[]{:S(2)}) %copy-start.2) | copy-done | bytes 4194328
  (36 shorter events, 0.3 us)
Async XLA Ops:
  13.6 21.8 %collective-permute-start = (bf16[132,2048]{1,0:T(8,128)(2,1)S(1)}, bf16[132,2048]{1,0:T(8,128)(2,1)S(1)}, u32[]{:S(2)}, u32[]{:S(2)}) collective-permute-start(bf16[132,2048]{1,0:T(8,128)(2,1)S(1)} %pad_maximum_fusion), channel_id=1, source_target_pairs={{0,1},{1,0},{2,3},{3,2},{4,5},{5,4},{6,7},{7,6},{8,9},{9,8},{10,11... | collective-permute-start | bytes 1622024 | tf_op jit(solution)/shard_map/ppermute | solution.py:36
  37.9 11.5 %all-to-all-start = ((f32[8,2,2,1024]{3,2,1,0:T(2,128)}), f32[8,2,2,1024]{3,2,1,0:T(2,128)S(1)}, u32[]{:S(2)}, u32[]{:S(2)}) async-start(f32[8,2,2,1024]{3,2,1,0:T(2,128)} %broadcast_in_dim.4), calls=%async_computation | async-start | bytes 262144 | tf_op jit(solution)/shard_map/all_to_all | solution.py:52
  44.2 124.1 %all-gather.2.cloned.1.call-start = ((), (), s32[]{:S(2)}) async-start(), calls=%async_computation.2 | async-start | bytes 4718592 | tf_op jit(solution)/shard_map/all_gather | solution.py:138
  49.5 43.1 %collective-permute-start.2 = (bf16[2048,1024]{1,0:T(8,128)(2,1)}, bf16[2048,1024]{1,0:T(8,128)(2,1)}, u32[]{:S(2)}, u32[]{:S(2)}) collective-permute-start(bf16[2048,1024]{1,0:T(8,128)(2,1)} %bitcast.111), channel_id=1, source_target_pairs={{0,2},{1,3},{2,0},{3,1},{4,6},{5,7},{6,4},{7,5},{8,10},{9,11},{10,... | collective-permute-start | bytes 12582920 | tf_op jit(solution)/shard_map/ppermute | solution.py:36
  50.5 28.2 %collective-permute-start.1 = (bf16[1024,512]{1,0:T(8,128)(2,1)}, bf16[1024,512]{1,0:T(8,128)(2,1)S(1)}, u32[]{:S(2)}, u32[]{:S(2)}) collective-permute-start(bf16[1024,512]{1,0:T(8,128)(2,1)} %get-tuple-element.26), channel_id=1, source_target_pairs={{0,1},{1,0},{2,3},{3,2},{4,5},{5,4},{6,7},{7,6},{8,9},{9,8},{10,11... | collective-permute-start | bytes 3145736 | tf_op jit(solution)/shard_map/ppermute | solution.py:36
  51.4 27.1 %all-to-all-start.1 = ((f32[8,2,2,1024]{3,2,1,0:T(2,128)}), f32[8,2,2,1024]{3,2,1,0:T(2,128)S(1)}, u32[]{:S(2)}, u32[]{:S(2)}) async-start(f32[8,2,2,1024]{3,2,1,0:T(2,128)} %broadcast_in_dim.5), calls=%async_computation.1 | async-start | bytes 262144 | tf_op jit(solution)/shard_map/all_to_all | solution.py:52
  56.5 22.2 %copy-start.1 = (bf16[2048,512]{1,0:T(8,128)(2,1)S(1)}, bf16[2048,512]{1,0:T(8,128)(2,1)}, u32[]{:S(2)}) copy-start(bf16[2048,512]{1,0:T(8,128)(2,1)} %x_ref.1) | copy-start | bytes 6291460
  61.6 17.6 %copy-start.4 = (f32[1024]{0:T(1024)S(1)}, f32[1024]{0:T(1024)}, u32[]{:S(2)}) copy-start(f32[1024]{0:T(1024)} %param.7) | copy-start | bytes 12292
  78.5 2.2 %copy-start = (f32[1024,1024]{1,0:T(8,128)S(1)}, f32[1024,1024]{1,0:T(8,128)}, u32[]{:S(2)}) copy-start(f32[1024,1024]{1,0:T(8,128)} %get-tuple-element.51) | copy-start | bytes 12582916
  82.5 10.2 %collective-permute-start.3 = (bf16[1024,1024]{1,0:T(8,128)(2,1)S(1)}, bf16[1024,1024]{1,0:T(8,128)(2,1)}, u32[]{:S(2)}, u32[]{:S(2)}) collective-permute-start(bf16[1024,1024]{1,0:T(8,128)(2,1)S(1)} %multiply_convert_fusion), channel_id=1, source_target_pairs={{0,2},{1,3},{2,0},{3,1},{4,6},{5,7},{6,4},{7,5},{8,10},{9,11},{10,... | collective-permute-start | bytes 6291464 | tf_op jit(solution)/shard_map/ppermute | solution.py:36
  84.3 4.8 %copy-start.3 = (bf16[2,4,4,1,64,1024]{5,4,3,2,1,0:T(8,128)(2,1)S(1)}, bf16[2,4,4,1,64,1024]{5,4,3,2,1,0:T(8,128)(2,1)}, u32[]{:S(2)}) copy-start(bf16[2,4,4,1,64,1024]{5,4,3,2,1,0:T(8,128)(2,1)} %constant_dynamic-slice_fusion.16) | copy-start | bytes 12582916
  98.5 11.9 %collective-permute-start.12 = (bf16[512,384]{1,0:T(8,128)(2,1)S(1)}, bf16[512,384]{1,0:T(8,128)(2,1)}, u32[]{:S(2)}, u32[]{:S(2)}) collective-permute-start(bf16[512,384]{1,0:T(8,128)(2,1)S(1)} %bitcast.123), channel_id=1, source_target_pairs={{0,48},{1,49},{2,50},{3,51},{4,52},{5,53},{6,54},{7,55},{8,56},{9,... | collective-permute-start | bytes 1179656 | tf_op jit(solution)/shard_map/ppermute | solution.py:36
  99.1 12.0 %collective-permute-start.11 = (bf16[512,384]{1,0:T(8,128)(2,1)}, bf16[512,384]{1,0:T(8,128)(2,1)}, u32[]{:S(2)}, u32[]{:S(2)}) collective-permute-start(bf16[512,384]{1,0:T(8,128)(2,1)} %bitcast.30), channel_id=1, source_target_pairs={{0,32},{1,33},{2,34},{3,35},{4,36},{5,37},{6,38},{7,39},{8,40},{9,... | collective-permute-start | bytes 1179656 | tf_op jit(solution)/shard_map/ppermute | solution.py:36
  100.5 19.9 %collective-permute-start.10 = (bf16[512,384]{1,0:T(8,128)(2,1)S(1)}, bf16[512,384]{1,0:T(8,128)(2,1)}, u32[]{:S(2)}, u32[]{:S(2)}) collective-permute-start(bf16[512,384]{1,0:T(8,128)(2,1)S(1)} %bitcast.122), channel_id=1, source_target_pairs={{0,16},{1,17},{2,18},{3,19},{4,20},{5,21},{6,22},{7,23},{8,24},{9,... | collective-permute-start | bytes 1179656 | tf_op jit(solution)/shard_map/ppermute | solution.py:36
  108.1 15.9 %collective-permute-start.6 = (bf16[512,640]{1,0:T(8,128)(2,1)}, bf16[512,640]{1,0:T(8,128)(2,1)}, u32[]{:S(2)}, u32[]{:S(2)}) collective-permute-start(bf16[512,640]{1,0:T(8,128)(2,1)} %bitcast.20), channel_id=1, source_target_pairs={{0,12},{1,13},{2,14},{3,15},{4,0},{5,1},{6,2},{7,3},{8,4},{9,5},{1... | collective-permute-start | bytes 1966088 | tf_op jit(solution)/shard_map/ppermute | solution.py:36
  109.8 17.1 %collective-permute-start.5 = (bf16[512,640]{1,0:T(8,128)(2,1)}, bf16[512,640]{1,0:T(8,128)(2,1)}, u32[]{:S(2)}, u32[]{:S(2)}) collective-permute-start(bf16[512,640]{1,0:T(8,128)(2,1)} %bitcast.19), channel_id=1, source_target_pairs={{0,8},{1,9},{2,10},{3,11},{4,12},{5,13},{6,14},{7,15},{8,0},{9,1},... | collective-permute-start | bytes 1966088 | tf_op jit(solution)/shard_map/ppermute | solution.py:36
  110.4 33.0 %collective-permute-start.4 = (bf16[512,640]{1,0:T(8,128)(2,1)}, bf16[512,640]{1,0:T(8,128)(2,1)}, u32[]{:S(2)}, u32[]{:S(2)}) collective-permute-start(bf16[512,640]{1,0:T(8,128)(2,1)} %bitcast.18), channel_id=1, source_target_pairs={{0,4},{1,5},{2,6},{3,7},{4,8},{5,9},{6,10},{7,11},{8,12},{9,13},{1... | collective-permute-start | bytes 1966088 | tf_op jit(solution)/shard_map/ppermute | solution.py:36
  111.1 57.2 %collective-permute-start.17 = (bf16[1024,1024]{1,0:T(8,128)(2,1)S(1)}, bf16[1024,1024]{1,0:T(8,128)(2,1)}, u32[]{:S(2)}, u32[]{:S(2)}) collective-permute-start(bf16[1024,1024]{1,0:T(8,128)(2,1)S(1)} %multiply_convert_fusion), channel_id=1, source_target_pairs={{0,1},{1,0},{2,3},{3,2},{4,5},{5,4},{6,7},{7,6},{8,9},{9,8},{10,11... | collective-permute-start | bytes 6291464 | tf_op jit(solution)/shard_map/ppermute | solution.py:36
  121.9 26.1 %collective-permute-start.15 = (bf16[128,384]{1,0:T(8,128)(2,1)S(1)}, bf16[128,384]{1,0:T(8,128)(2,1)S(1)}, u32[]{:S(2)}, u32[]{:S(2)}) collective-permute-start(bf16[128,384]{1,0:T(8,128)(2,1)S(1)} %bitcast.129), channel_id=1, source_target_pairs={{0,12},{1,13},{2,14},{3,15},{4,0},{5,1},{6,2},{7,3},{8,4},{9,5},{1... | collective-permute-start | bytes 294920 | tf_op jit(solution)/shard_map/ppermute | solution.py:36
  123.9 24.5 %collective-permute-start.14 = (bf16[128,384]{1,0:T(8,128)(2,1)S(1)}, bf16[128,384]{1,0:T(8,128)(2,1)S(1)}, u32[]{:S(2)}, u32[]{:S(2)}) collective-permute-start(bf16[128,384]{1,0:T(8,128)(2,1)S(1)} %bitcast.128), channel_id=1, source_target_pairs={{0,8},{1,9},{2,10},{3,11},{4,12},{5,13},{6,14},{7,15},{8,0},{9,1},... | collective-permute-start | bytes 294920 | tf_op jit(solution)/shard_map/ppermute | solution.py:36
  126.9 22.3 %collective-permute-start.13 = (bf16[128,384]{1,0:T(8,128)(2,1)S(1)}, bf16[128,384]{1,0:T(8,128)(2,1)S(1)}, u32[]{:S(2)}, u32[]{:S(2)}) collective-permute-start(bf16[128,384]{1,0:T(8,128)(2,1)S(1)} %bitcast.127), channel_id=1, source_target_pairs={{0,4},{1,5},{2,6},{3,7},{4,8},{5,9},{6,10},{7,11},{8,12},{9,13},{1... | collective-permute-start | bytes 294920 | tf_op jit(solution)/shard_map/ppermute | solution.py:36
  145.3 5.7 %collective-permute-start.9 = (bf16[128,640]{1,0:T(8,128)(2,1)S(1)}, bf16[128,640]{1,0:T(8,128)(2,1)S(1)}, u32[]{:S(2)}, u32[]{:S(2)}) collective-permute-start(bf16[128,640]{1,0:T(8,128)(2,1)S(1)} %bitcast.126), channel_id=1, source_target_pairs={{0,48},{1,49},{2,50},{3,51},{4,52},{5,53},{6,54},{7,55},{8,56},{9,... | collective-permute-start | bytes 491528 | tf_op jit(solution)/shard_map/ppermute | solution.py:36
  148.0 6.1 %collective-permute-start.8 = (bf16[128,640]{1,0:T(8,128)(2,1)S(1)}, bf16[128,640]{1,0:T(8,128)(2,1)S(1)}, u32[]{:S(2)}, u32[]{:S(2)}) collective-permute-start(bf16[128,640]{1,0:T(8,128)(2,1)S(1)} %bitcast.125), channel_id=1, source_target_pairs={{0,32},{1,33},{2,34},{3,35},{4,36},{5,37},{6,38},{7,39},{8,40},{9,... | collective-permute-start | bytes 491528 | tf_op jit(solution)/shard_map/ppermute | solution.py:36
  148.4 9.5 %collective-permute-start.7 = (bf16[128,640]{1,0:T(8,128)(2,1)S(1)}, bf16[128,640]{1,0:T(8,128)(2,1)S(1)}, u32[]{:S(2)}, u32[]{:S(2)}) collective-permute-start(bf16[128,640]{1,0:T(8,128)(2,1)S(1)} %bitcast.124), channel_id=1, source_target_pairs={{0,16},{1,17},{2,18},{3,19},{4,20},{5,21},{6,22},{7,23},{8,24},{9,... | collective-permute-start | bytes 491528 | tf_op jit(solution)/shard_map/ppermute | solution.py:36
  158.1 9.6 %collective-permute-start.16 = (bf16[64,1024]{1,0:T(8,128)(2,1)S(1)}, bf16[64,1024]{1,0:T(8,128)(2,1)S(1)}, u32[]{:S(2)}, u32[]{:S(2)}) collective-permute-start(bf16[64,1024]{1,0:T(8,128)(2,1)S(1)} %fusion.23), channel_id=1, source_target_pairs={{0,64},{1,65},{2,66},{3,67},{4,68},{5,69},{6,70},{7,71},{8,72},{9,... | collective-permute-start | bytes 393224 | tf_op jit(solution)/shard_map/ppermute | solution.py:36
  168.3 6.5 %copy-start.6 = (f32[2048,1024]{1,0:T(8,128)S(1)}, f32[2048,1024]{1,0:T(8,128)}, u32[]{:S(2)}) copy-start(f32[2048,1024]{1,0:T(8,128)} %fusion.2) | copy-start | bytes 25165828
  174.3 2.2 %copy-start.5 = (bf16[1024,2048]{1,0:T(8,128)(2,1)S(1)}, bf16[1024,2048]{1,0:T(8,128)(2,1)}, u32[]{:S(2)}) copy-start(bf16[1024,2048]{1,0:T(8,128)(2,1)} %all-gather.2.cloned.1.call-done) | copy-start | bytes 12582916
  180.6 2.0 %copy-start.2 = (bf16[2048,1024]{1,0:T(8,128)(2,1)}, bf16[2048,1024]{1,0:T(8,128)(2,1)S(1)}, u32[]{:S(2)}) copy-start(bf16[2048,1024]{1,0:T(8,128)(2,1)S(1)} %fusion.4) | copy-start | bytes 12582916
Sparse Core Ops, SparseCore 0:
  50.8 33.0 all-gather.1
